TPU v7x, 32 devices: a whole 2x2x4 slice. The times are simulated.
32 devices in a mesh: wrk: 8 (over z, y), firm: 4 (over x, core).
Axes of the slice: x: 2, y: 2, z: 4, core: 2. Of those that a mesh axis runs over, the one named last changes fastest.
Arguments:
- feat_wrk: float32 [4096, 64], P('wrk'), may hold values from -9 to 9
- feat_firm: float32 [64, 16384], P(None, 'firm'), may hold values from -12 to 12
- surplus: float32 [64, 64], replicated, may hold values from -0.125 to 1.125
- row_start: float32 [4096], P('wrk'), may hold values from -5 to 5
- col_start: float32 [16384], P('firm'), may hold values from -5 to 5
- row_mass: float32 [4096], P('wrk'), may hold values from -1.5 to 1.5
- col_mass: float32 [16384], P('firm'), may hold values from -1.5 to 1.5
- row_cot: float32 [4096], P('wrk'), may hold values from -5 to 5
- col_cot: float32 [16384], P('firm'), may hold values from -5 to 5
Outputs:
- grad_surplus: float32 [64, 64], replicated
- grad_row: float32 [4096], P('wrk')
- grad_col: float32 [16384], P('firm')
All inputs are finite; a program needn't handle non-finite values.
Results may differ from a plain program's by a relative error of at most 0.0003.
Values sent between devices are 32-bit elements; how exact they have to be, the bound alone decides.
No kernel may reach another device: no remote copies, remote signals or barrier semaphores. Data moves between devices by JAX's collectives and lax.ppermute only.
A program may use at most 64 MiB of HBM per device.

v0:
```python
import math

import jax
import jax.numpy as jnp
from jax import lax
from jax.sharding import PartitionSpec as P

ITERS = 3


HIGHEST = lax.Precision.HIGHEST


def joined(part, axis, combine):
    gathered = jax.tree.map(lambda a: lax.all_gather(a, axis), part)

    def take(source):
        return jax.tree.map(lambda a: lax.dynamic_index_in_dim(a, source, 0, False), gathered)

    return lax.fori_loop(
        1, lax.axis_size(axis), lambda source, state: combine(state, take(source)), take(0)
    )


def pair_combine(first, second):
    larger = jnp.maximum(first[0], second[0])
    return (larger, first[1] * jnp.exp(first[0] - larger) + second[1] * jnp.exp(second[0] - larger))


def block_layout(firm_cols):
    col_count = firm_cols.shape[1]
    block_width = math.gcd(col_count, 512)
    return (block_width, jnp.arange(col_count // block_width, dtype=jnp.int32))


def row_local(mixed, firm_cols, col_shift):
    block_width, block_ids = block_layout(firm_cols)
    row_count = mixed.shape[0]

    def block_step(carry, block_index):
        run_max, run_total = carry
        first_col = block_index * block_width
        tile_cols = lax.dynamic_slice_in_dim(firm_cols, first_col, block_width, 1)
        shift_part = lax.dynamic_slice_in_dim(col_shift, first_col, block_width, 0)
        scores = jnp.dot(mixed, tile_cols, precision=HIGHEST) - shift_part[None, :]
        new_max = jnp.maximum(run_max, jnp.max(scores, axis=1))
        run_total = run_total * jnp.exp(run_max - new_max) + jnp.sum(
            jnp.exp(scores - new_max[:, None]), axis=1
        )
        return ((new_max, run_total), None)

    start_state = (
        jnp.full((row_count,), -jnp.inf, jnp.float32),
        jnp.zeros((row_count,), jnp.float32),
    )
    (run_max, run_total), unused = lax.scan(block_step, start_state, block_ids)
    return (run_max, run_total)


def col_local(mixed, firm_cols, row_shift):
    block_width, block_ids = block_layout(firm_cols)

    def block_step(carry, block_index):
        first_col = block_index * block_width
        tile_cols = lax.dynamic_slice_in_dim(firm_cols, first_col, block_width, 1)
        scores = jnp.dot(mixed, tile_cols, precision=HIGHEST) - row_shift[:, None]
        largest = jnp.max(scores, axis=0)
        return (carry, (largest, jnp.sum(jnp.exp(scores - largest[None, :]), axis=0)))

    unused, (block_max, block_total) = lax.scan(block_step, 0, block_ids)
    return (block_max.reshape(-1), block_total.reshape(-1))


def row_reduce(run_max, run_total):
    largest, summed = joined((run_max, run_total), "firm", pair_combine)
    return largest + jnp.log(summed)


def col_reduce(run_max, run_total):
    largest, summed = joined((run_max, run_total), "wrk", pair_combine)
    return largest + jnp.log(summed)


def col_weights(mixed, firm_cols, row_pot, col_log, col_weight):
    block_width, block_ids = block_layout(firm_cols)
    row_count = mixed.shape[0]

    def block_step(carry, block_index):
        grad_part, row_total = carry
        first_col = block_index * block_width
        tile_cols = lax.dynamic_slice_in_dim(firm_cols, first_col, block_width, 1)
        log_part = lax.dynamic_slice_in_dim(col_log, first_col, block_width, 0)
        weight_part = lax.dynamic_slice_in_dim(col_weight, first_col, block_width, 0)
        scores = jnp.dot(mixed, tile_cols, precision=HIGHEST) - row_pot[:, None]
        weights = jnp.exp(scores - log_part[None, :]) * weight_part[None, :]
        grad_part = grad_part + lax.dot_general(
            weights, tile_cols, (((1,), (1,)), ((), ())), precision=HIGHEST
        )
        return ((grad_part, row_total + jnp.sum(weights, axis=1)), None)

    start_state = (
        jnp.zeros((row_count, mixed.shape[1]), jnp.float32),
        jnp.zeros((row_count,), jnp.float32),
    )
    (grad_part, row_total), unused = lax.scan(block_step, start_state, block_ids)
    return (grad_part, row_total)


def row_weights(mixed, firm_cols, col_pot, row_log, row_weight):
    block_width, block_ids = block_layout(firm_cols)

    def block_step(grad_part, block_index):
        first_col = block_index * block_width
        tile_cols = lax.dynamic_slice_in_dim(firm_cols, first_col, block_width, 1)
        shift_part = lax.dynamic_slice_in_dim(col_pot, first_col, block_width, 0)
        scores = jnp.dot(mixed, tile_cols, precision=HIGHEST) - shift_part[None, :]
        weights = jnp.exp(scores - row_log[:, None]) * row_weight[:, None]
        grad_part = grad_part + lax.dot_general(
            weights, tile_cols, (((1,), (1,)), ((), ())), precision=HIGHEST
        )
        return (grad_part, jnp.sum(weights, axis=0))

    grad_part, col_blocks = lax.scan(block_step, jnp.zeros(mixed.shape, jnp.float32), block_ids)
    return (grad_part, col_blocks.reshape(-1))


def body(feat_wrk, feat_firm, surplus, row_start, col_start, row_mass, col_mass, row_cot, col_cot):
    mixed = jnp.dot(feat_wrk, surplus, precision=HIGHEST)
    row_pots = [row_start]
    col_pots = [col_start]
    row_logs = []
    col_logs = []
    for iteration in range(ITERS):
        run_max, run_total = row_local(mixed, feat_firm, col_pots[-1])
        row_log = row_reduce(run_max, run_total)
        row_pots.append(0.5 * row_pots[-1] + 0.5 * (row_log - row_mass))
        run_max, run_total = col_local(mixed, feat_firm, row_pots[-1])
        col_log = col_reduce(run_max, run_total)
        col_pots.append(0.5 * col_pots[-1] + 0.5 * (col_log - col_mass))
        row_logs.append(row_log)
        col_logs.append(col_log)
    row_bar = row_cot
    col_bar = col_cot
    grad_mixed = jnp.zeros(mixed.shape, jnp.float32)
    for iteration in reversed(range(ITERS)):
        first_part, row_total = col_weights(
            mixed, feat_firm, row_pots[iteration + 1], col_logs[iteration], 0.5 * col_bar
        )
        row_bar = row_bar - lax.psum(row_total, "firm")
        col_bar = 0.5 * col_bar
        second_part, col_total = row_weights(
            mixed, feat_firm, col_pots[iteration], row_logs[iteration], 0.5 * row_bar
        )
        col_bar = col_bar - lax.psum(col_total, "wrk")
        row_bar = 0.5 * row_bar
        grad_mixed = grad_mixed + first_part + second_part
    local_term = jnp.dot(feat_wrk.T, grad_mixed, precision=HIGHEST)
    grad_surplus = lax.psum(local_term, ("wrk", "firm"))
    return (grad_surplus, row_bar, col_bar)


def solution(mesh):
    return jax.shard_map(
        body,
        mesh=mesh,
        in_specs=(
            P("wrk", None),
            P(None, "firm"),
            P(),
            P("wrk"),
            P("firm"),
            P("wrk"),
            P("firm"),
            P("wrk"),
            P("firm"),
        ),
        out_specs=(P(), P("wrk"), P("firm")),
        check_vma=False,
    )
```

profile of v0, /device:TPU:0, one launch (start us, length us, event | category | flops | bytes accessed | tf_op | source)
XLA Modules:
  0.0 702.1 jit_solution(9204164012576274984)
XLA Ops:
  1.5 1.4 fusion.74
  2.9 28.4 %while.264 = (s32[]{:T(128)}, f32[512]{0:T(512)S(1)}, f32[512]{0:T(512)S(1)}, s32[8]{0:T(128)S(1)}, f32[64,4096]{1,0:T(8,128)}, /*index=5*/f32[512,64]{1,0:T(8,1...) while((s32[]{:T(128)}, f32[512]{0:T(512)S(1)}, ...), condition=%wide.region_3.4_spmd.clone, body=%wide.region_0.3_spmd.clone.sunk | while | flops 202377728 | bytes 2392250 | solution.py:56
  4.3 2.0 fusion.142
  7.8 2.0 fusion.142
  11.4 2.0 fusion.142
  14.9 2.0 fusion.142
  18.5 2.0 fusion.142
  22.0 2.0 fusion.142
  25.6 2.0 fusion.142
  29.1 2.0 fusion.142
  31.3 6.2 all-gather.7
  37.5 5.5 all-gather.6
  45.1 28.0 %while.256 = (s32[]{:T(128)}, f32[8,512]{1,0:T(8,128)S(1)}, f32[8,512]{1,0:T(8,128)S(1)}, s32[8]{0:T(128)S(1)}, f32[64,4096]{1,0:T(8,128)}, /*index=5*/f32[512,6...) while((s32[]{:T(128)}, f32[8,512]{1,0:T(8,128)S(1)}, ...), condition=%wide.region_9.10_spmd, body=%wide.region_6.9_spmd.sunk | while | flops 202374144 | bytes 2375859 | solution.py:70
  46.4 1.9 fusion.136
  49.9 1.9 fusion.136
  53.4 1.9 fusion.136
  56.9 1.9 fusion.136
  60.4 1.9 fusion.136
  63.9 1.9 fusion.136
  67.4 1.9 fusion.136
  70.9 1.9 fusion.136
  73.1 31.2 %all-gather.9 = f32[8,1,4096]{2,1,0:T(1,128)S(1)} all-gather(f32[1,1,4096]{2,1,0:T(1,128)S(1)} %reshape.96), channel_id=1, replica_groups=mesh['wrk'=8,'firm'=4] {'wrk'}, dimensions={0}, use_global_device_ids=true | all-gather | bytes 147456 | tf_op jit(solution)/shard_map/all_gather | solution.py:15
  104.5 30.5 %all-gather.8 = f32[8,1,4096]{2,1,0:T(1,128)S(1)} all-gather(f32[1,1,4096]{2,1,0:T(1,128)S(1)} %reshape.94), channel_id=1, replica_groups=mesh['wrk'=8,'firm'=4] {'wrk'}, dimensions={0}, use_global_device_ids=true | all-gather | bytes 147456 | tf_op jit(solution)/shard_map/all_gather | solution.py:15
  135.9 21.2 %while.265 = (s32[]{:T(128)}, f32[512]{0:T(512)S(1)}, f32[512]{0:T(512)S(1)}, s32[8]{0:T(128)S(1)}, f32[64,4096]{1,0:T(8,128)S(1)}, /*index=5*/f32[512,64]{1,0:T...) while((s32[]{:T(128)}, f32[512]{0:T(512)S(1)}, ...), condition=%wide.region_15.16_spmd.clone, body=%wide.region_12.15_spmd.clone.sunk | while | flops 202377728 | bytes 2523322 | solution.py:56
  157.1 5.2 all-gather.11
  162.3 5.2 all-gather.10
  168.9 20.7 %while.259 = (s32[]{:T(128)}, f32[8,512]{1,0:T(8,128)S(1)}, f32[8,512]{1,0:T(8,128)S(1)}, s32[8]{0:T(128)S(1)}, f32[64,4096]{1,0:T(8,128)S(1)}, /*index=5*/f32[5...) while((s32[]{:T(128)}, f32[8,512]{1,0:T(8,128)S(1)}, ...), condition=%wide.region_21.22_spmd, body=%wide.region_18.21_spmd.sunk | while | flops 202374144 | bytes 2506931 | solution.py:70
  189.7 30.6 %all-gather.13 = f32[8,1,4096]{2,1,0:T(1,128)S(1)} all-gather(f32[1,1,4096]{2,1,0:T(1,128)S(1)} %reshape.104), channel_id=1, replica_groups=mesh['wrk'=8,'firm'=4] {'wrk'}, dimensions={0}, use_global_device_ids=true | all-gather | bytes 147456 | tf_op jit(solution)/shard_map/all_gather | solution.py:15
  220.4 30.5 %all-gather.12 = f32[8,1,4096]{2,1,0:T(1,128)S(1)} all-gather(f32[1,1,4096]{2,1,0:T(1,128)S(1)} %reshape.102), channel_id=1, replica_groups=mesh['wrk'=8,'firm'=4] {'wrk'}, dimensions={0}, use_global_device_ids=true | all-gather | bytes 147456 | tf_op jit(solution)/shard_map/all_gather | solution.py:15
  252.9 21.2 %while.266 = (s32[]{:T(128)}, f32[512]{0:T(512)S(1)}, f32[512]{0:T(512)S(1)}, s32[8]{0:T(128)S(1)}, f32[64,4096]{1,0:T(8,128)S(1)}, /*index=5*/f32[512,64]{1,0:T...) while((s32[]{:T(128)}, f32[512]{0:T(512)S(1)}, ...), condition=%wide.region_27.28_spmd.clone, body=%wide.region_24.27_spmd.clone.sunk | while | flops 202377728 | bytes 2523322 | solution.py:56
  274.0 5.2 all-gather.15
  279.2 5.2 all-gather.14
  285.9 20.7 %while.262 = (s32[]{:T(128)}, f32[8,512]{1,0:T(8,128)S(1)}, f32[8,512]{1,0:T(8,128)S(1)}, s32[8]{0:T(128)S(1)}, f32[64,4096]{1,0:T(8,128)S(1)}, /*index=5*/f32[5...) while((s32[]{:T(128)}, f32[8,512]{1,0:T(8,128)S(1)}, ...), condition=%wide.region_33.34_spmd, body=%wide.region_30.33_spmd.sunk | while | flops 202374144 | bytes 2506931 | solution.py:70
  306.7 30.5 %all-gather.17 = f32[8,1,4096]{2,1,0:T(1,128)S(1)} all-gather(f32[1,1,4096]{2,1,0:T(1,128)S(1)} %reshape.112), channel_id=1, replica_groups=mesh['wrk'=8,'firm'=4] {'wrk'}, dimensions={0}, use_global_device_ids=true | all-gather | bytes 147456 | tf_op jit(solution)/shard_map/all_gather | solution.py:15
  337.3 30.7 %all-gather.16 = f32[8,1,4096]{2,1,0:T(1,128)S(1)} all-gather(f32[1,1,4096]{2,1,0:T(1,128)S(1)} %reshape.110), channel_id=1, replica_groups=mesh['wrk'=8,'firm'=4] {'wrk'}, dimensions={0}, use_global_device_ids=true | all-gather | bytes 147456 | tf_op jit(solution)/shard_map/all_gather | solution.py:15
  370.1 27.8 %while.267 = (s32[]{:T(128)}, f32[512,64]{0,1:T(8,128)S(1)}, f32[512]{0:T(512)S(1)}, s32[8]{0:T(128)S(1)}, f32[64,4096]{1,0:T(8,128)S(1)}, /*index=5*/f32[512,64...) while((s32[]{:T(128)}, f32[512,64]{0,1:T(8,128)S(1)}, ...), condition=%wide.region_38.39_spmd.clone, body=%wide.region_36.38_spmd.clone.sunk | while | flops 403767808 | bytes 2906322 | solution.py:105
  397.9 5.7 psum.49
  403.6 29.6 %while.268 = (s32[]{:T(128)}, f32[512,64]{0,1:T(8,128)S(1)}, f32[8,512]{1,0:T(8,128)S(1)}, s32[8]{0:T(128)S(1)}, f32[64,4096]{1,0:T(8,128)S(1)}, /*index=5*/f32[...) while((s32[]{:T(128)}, f32[512,64]{0,1:T(8,128)S(1)}, ...), condition=%wide.region_42.43_spmd.clone, body=%wide.region_40.42_spmd.clone.sunk | while | flops 403766784 | bytes 2900177 | solution.py:123
  433.3 37.0 %psum.50 = f32[4096]{0:T(1024)S(1)} all-reduce(f32[4096]{0:T(1024)S(1)} %bitcast.266), channel_id=1, replica_groups=mesh['wrk'=8,'firm'=4] {'wrk'}, use_global_device_ids=true, to_apply=%region_43.44 | all-reduce | flops 4096 | bytes 32768 | tf_op jit(solution)/shard_map/psum | solution.py:154
  470.3 27.8 %while.269 = (s32[]{:T(128)}, f32[512,64]{0,1:T(8,128)S(1)}, f32[512]{0:T(512)S(1)}, s32[8]{0:T(128)S(1)}, f32[64,4096]{1,0:T(8,128)S(1)}, /*index=5*/f32[512,64...) while((s32[]{:T(128)}, f32[512,64]{0,1:T(8,128)S(1)}, ...), condition=%wide.region_46.47_spmd.clone, body=%wide.region_44.46_spmd.clone.sunk | while | flops 403767808 | bytes 2906322 | solution.py:105
  498.1 5.7 psum.51
  503.8 29.7 %while.270 = (s32[]{:T(128)}, f32[512,64]{0,1:T(8,128)S(1)}, f32[8,512]{1,0:T(8,128)S(1)}, s32[8]{0:T(128)S(1)}, f32[64,4096]{1,0:T(8,128)S(1)}, /*index=5*/f32[...) while((s32[]{:T(128)}, f32[512,64]{0,1:T(8,128)S(1)}, ...), condition=%wide.region_50.51_spmd.clone, body=%wide.region_48.50_spmd.clone.sunk | while | flops 403766784 | bytes 2900177 | solution.py:123
  533.5 33.0 %psum.52 = f32[4096]{0:T(1024)S(1)} all-reduce(f32[4096]{0:T(1024)S(1)} %bitcast.267), channel_id=1, replica_groups=mesh['wrk'=8,'firm'=4] {'wrk'}, use_global_device_ids=true, to_apply=%region_51.52 | all-reduce | flops 4096 | bytes 32768 | tf_op jit(solution)/shard_map/psum | solution.py:154
  566.5 27.8 %while.271 = (s32[]{:T(128)}, f32[512,64]{0,1:T(8,128)S(1)}, f32[512]{0:T(512)S(1)}, s32[8]{0:T(128)S(1)}, f32[64,4096]{1,0:T(8,128)S(1)}, /*index=5*/f32[512,64...) while((s32[]{:T(128)}, f32[512,64]{0,1:T(8,128)S(1)}, ...), condition=%wide.region_54.55_spmd.clone, body=%wide.region_52.54_spmd.clone.sunk | while | flops 403767808 | bytes 2906322 | solution.py:105
  594.3 5.9 psum.53
  600.2 29.7 %while.272 = (s32[]{:T(128)}, f32[512,64]{0,1:T(8,128)S(1)}, f32[8,512]{1,0:T(8,128)S(1)}, s32[8]{0:T(128)S(1)}, f32[64,4096]{1,0:T(8,128)S(1)}, /*index=5*/f32[...) while((s32[]{:T(128)}, f32[512,64]{0,1:T(8,128)S(1)}, ...), condition=%wide.region_58.59_spmd.clone, body=%wide.region_56.58_spmd.clone.sunk | while | flops 403766784 | bytes 2900177 | solution.py:123
  630.5 33.0 %psum.55 = f32[4096]{0:T(1024)S(1)} all-reduce(f32[4096]{0:T(1024)S(1)} %bitcast.268), channel_id=1, replica_groups=mesh['wrk'=8,'firm'=4] {'wrk'}, use_global_device_ids=true, to_apply=%region_60.61 | all-reduce | flops 4096 | bytes 32768 | tf_op jit(solution)/shard_map/psum | solution.py:154
  664.4 37.0 %psum.54 = f32[64,64]{0,1:T(8,128)S(1)} all-reduce(f32[64,64]{0,1:T(8,128)S(1)} %convolution_bitcast_fusion), channel_id=1, replica_groups=mesh['wrk'=8,'firm'=4] {'wrk','firm'}, use_global_device_ids=true, to_apply=%region_59.60 | all-reduce | flops 4096 | bytes 32768 | tf_op jit(solution)/shard_map/psum | solution.py:158
  (718 shorter events, 229.8 us)
Async XLA Ops:
  0.6 0.9 copy-start
  0.6 2.3 copy-start.4
  43.0 0.6 copy-start.6
  43.6 0.7 slice-start.3
  44.3 0.7 copy-start.12
  44.4 0.7 copy-start.11
  73.1 62.7 %copy-start.1 = (f32[64,4096]{1,0:T(8,128)S(1)}, f32[64,4096]{1,0:T(8,128)}, u32[]{:S(2)}) copy-start(f32[64,4096]{1,0:T(8,128)} %get-tuple-element.3573) | copy-start | bytes 3145732
  135.1 0.7 copy-start.10
  167.4 0.6 copy-start.5
  168.0 0.7 slice-start.2
  250.9 0.6 copy-start.2
  251.6 0.7 slice-start
  284.4 0.6 copy-start.7
  285.0 0.7 slice-start.4
  368.0 0.6 copy-start.3
  368.7 0.7 slice-start.1
  369.4 0.7 copy-start.9
  397.9 5.7 copy-start.13
  630.0 0.6 copy-start.8
where the time goes:
time: 705 us; the launch traced here: 702 us
  blocking collectives  374 us (53%)
  matrix products  170 us (24%)
  local copies, waits for them, and re-layouts  78.9 us (11%)
  loops' own time  67.1 us (10%)
  other arithmetic  11.6 us (2%)
    all_gather x12, blocking collectives, joined(): gathered = jax.tree.map(lambda a: lax.all_gather(a, axis), part)  216 us
    psum x3, blocking collectives, body(): col_bar = col_bar - lax.psum(col_total, 'wrk')  103 us
    dot_general x48, matrix products, block_step(): scores = jnp.dot(mixed, tile_cols, precision=HIGHEST) - shift_part[None, :]  60.1 us
    dynamic_slice x96, local copies, waits for them, and re-layouts, row_local(): (run_max, run_total), unused = lax.scan(block_step, start_state, block_ids)  56.3 us
    dot_general x48, matrix products, block_step(): lax.dot_general(weights, tile_cols, (((1,), (1,)), ((), ())), precision=H...  47.3 us
    psum x1, blocking collectives, body(): grad_surplus = lax.psum(local_term, ('wrk', 'firm'))  37 us
    dot_general x24, matrix products, block_step(): scores = jnp.dot(mixed, tile_cols, precision=HIGHEST) - row_shift[:, None]  31.3 us
    dot_general x24, matrix products, block_step(): scores = jnp.dot(mixed, tile_cols, precision=HIGHEST) - row_pot[:, None]  29.4 us

commit v1 on v0

v1 whole, which is shorter than its diff:
```python
import math

import jax
import jax.numpy as jnp
from jax import lax
from jax.experimental import pallas as pl
from jax.experimental.pallas import tpu as pltpu
from jax.sharding import PartitionSpec as P

ITERS = 3
LOG2E = 1.0 / math.log(2.0)
HIGHEST = lax.Precision.HIGHEST
LANES = 128
GROUP = 8
WHOLE = pl.BlockSpec(memory_space=pltpu.VMEM)
VMEM_LIMIT = 24 * 1024 * 1024


def tree(values, combine):
    values = list(values)
    while len(values) > 1:
        paired = [combine(values[i], values[i + 1]) for i in range(0, len(values) - 1, 2)]
        if len(values) % 2:
            paired.append(values[-1])
        values = paired
    return values[0]


def shape_of(*dims):
    return jax.ShapeDtypeStruct(dims, jnp.float32)


def call(kernel, name, outs, args, scratch=(), aliases=None):
    return pl.pallas_call(
        kernel,
        name=name,
        out_shape=outs,
        in_specs=[WHOLE] * len(args),
        out_specs=jax.tree.map(lambda _: WHOLE, outs),
        scratch_shapes=scratch,
        input_output_aliases=aliases or {},
        compiler_params=pltpu.CompilerParams(vmem_limit_bytes=VMEM_LIMIT),
    )(*args)


def lane(k):
    return pl.ds(k * LANES, LANES)


def lse_parts(parts):
    largest = tree(parts, jnp.maximum)
    return largest + jnp.log2(tree([jnp.exp2(p - largest) for p in parts], jnp.add))


def spread_rows(value, ref):
    for block in range(value.shape[0]):
        wide = jnp.broadcast_to(value[block : block + 1, :], (LANES, LANES))
        ref[pl.ds(block * LANES, LANES), :] = wide.T


def row_lse(s_ref, shift_ref, max_ref, sum_ref, out_ref):
    rows, cols = s_ref.shape
    tiles = cols // LANES

    def group_step(g, carry):
        r = pl.ds(g * GROUP, GROUP)
        terms = [s_ref[r, lane(k)] - shift_ref[k : k + 1, :] for k in range(tiles)]
        largest = tree(terms, jnp.maximum)
        max_ref[r, :] = largest
        sum_ref[r, :] = tree([jnp.exp2(t - largest) for t in terms], jnp.add)
        return carry

    lax.fori_loop(0, rows // GROUP, group_step, 0)
    for block in range(rows // LANES):
        b = pl.ds(block * LANES, LANES)
        maxes = max_ref[b, :].T
        sums = sum_ref[b, :].T
        largest = jnp.max(maxes, axis=0, keepdims=True)
        total = jnp.sum(sums * jnp.exp2(maxes - largest), axis=0, keepdims=True)
        out_ref[block : block + 1, :] = largest + jnp.log2(total)


def col_blocking(cols):
    tiles = cols // LANES
    width = math.gcd(tiles, 8)
    return width, tiles // width


def send_all(col_ref, out_ref):
    value = col_ref[...]
    for peer in range(out_ref.shape[0]):
        out_ref[peer] = value


def col_lse(s_ref, shift_ref, col_ref):
    rows, cols = s_ref.shape
    width, chunks = col_blocking(cols)
    per_step = math.gcd(rows // GROUP, 8)
    steps = rows // (GROUP * per_step)

    def chunk_step(c, carry):
        def terms_of(step, q):
            r = pl.ds(step * (GROUP * per_step) + q * GROUP, GROUP)
            shift = shift_ref[r, :]
            return [
                s_ref[r, pl.ds(c * (width * LANES) + k * LANES, LANES)] - shift
                for k in range(width)
            ]

        def max_step(step, maxes):
            for q in range(per_step):
                terms = terms_of(step, q)
                maxes = tuple(jnp.maximum(m, t) for m, t in zip(maxes, terms))
            return maxes

        low = jnp.full((GROUP, LANES), -jnp.inf, jnp.float32)
        maxes = lax.fori_loop(0, steps, max_step, (low,) * width)

        def sum_step(step, sums):
            for q in range(per_step):
                terms = terms_of(step, q)
                sums = tuple(s + jnp.exp2(t - m) for s, t, m in zip(sums, terms, maxes))
            return sums

        zero = jnp.zeros((GROUP, LANES), jnp.float32)
        sums = lax.fori_loop(0, steps, sum_step, (zero,) * width)
        for k in range(width):
            largest = jnp.max(maxes[k], axis=0, keepdims=True)
            total = jnp.sum(sums[k] * jnp.exp2(maxes[k] - largest), axis=0, keepdims=True)
            col_ref[pl.ds(c * width + k, 1), :] = largest + jnp.log2(total)
        return carry

    lax.fori_loop(0, chunks, chunk_step, 0)


def first_row_kernel(fw_ref, ff_ref, sp_ref, start_ref, s_ref, out_ref, cp_ref, rhs_ref, max_ref, sum_ref):
    rank, cols = ff_ref.shape
    mixed = lax.dot_general(
        sp_ref[...], fw_ref[...], (((0,), (1,)), ((), ())), precision=HIGHEST,
        preferred_element_type=jnp.float32,
    ) * LOG2E

    def split(value):
        first = value.astype(jnp.bfloat16)
        rest = value - first.astype(jnp.float32)
        second = rest.astype(jnp.bfloat16)
        third = (rest - second.astype(jnp.float32)).astype(jnp.bfloat16)
        return first, second, third

    m1, m2, m3 = split(mixed)
    lhs = jnp.concatenate([m1, m2, m1, m2, m3, m1], axis=0)
    width = math.gcd(cols, 512)

    def dot_step(c, carry):
        chunk = pl.ds(c * width, width)
        f1, f2, f3 = split(ff_ref[:, chunk])
        rhs = jnp.concatenate([f1, f1, f2, f2, f1, f3], axis=0)
        s_ref[:, chunk] = lax.dot_general(
            lhs, rhs, (((0,), (0,)), ((), ())), preferred_element_type=jnp.float32
        )
        return carry

    lax.fori_loop(0, cols // width, dot_step, 0)
    cp_ref[...] = start_ref[...] * LOG2E
    row_lse(s_ref, cp_ref, max_ref, sum_ref, out_ref)


def damped(old, log, mass):
    return 0.5 * old + 0.5 * (log - mass * LOG2E)


def col_kernel_of(parts, first):
    def kernel(*refs):
        s_ref, part_refs = refs[0], refs[1 : 1 + parts]
        old_ref, mass_ref, out_ref, log_ref, pot_ref, wide_ref, col_ref = refs[1 + parts :]
        log = lse_parts([p[...] for p in part_refs])
        old = old_ref[...] * LOG2E if first else old_ref[...]
        pot = damped(old, log, mass_ref[...])
        log_ref[...] = log
        pot_ref[...] = pot
        spread_rows(pot, wide_ref)
        col_lse(s_ref, wide_ref, col_ref)
        send_all(col_ref, out_ref)

    return kernel


def row_kernel_of(first):
    def kernel(s_ref, got_ref, old_ref, mass_ref, out_ref, log_ref, pot_ref, max_ref, sum_ref):
        log = lse_parts([got_ref[p] for p in range(got_ref.shape[0])])
        old = old_ref[...] * LOG2E if first else old_ref[...]
        log_ref[...] = log
        pot_ref[...] = damped(old, log, mass_ref[...])
        row_lse(s_ref, pot_ref, max_ref, sum_ref, out_ref)

    return kernel


def col_adjoint_pass(s_ref, wide_ref, log_ref, weight_ref, total_ref, acc_in, acc_out, out_ref):
    rows, cols = s_ref.shape
    tiles = cols // LANES
    per_step = math.gcd(rows // GROUP, 4)

    def group_step(g, carry):
        rs = [pl.ds(g * (GROUP * per_step) + q * GROUP, GROUP) for q in range(per_step)]
        shifts = [wide_ref[r, :] for r in rs]
        totals = [None] * per_step
        for k in range(tiles):
            log = log_ref[k : k + 1, :]
            weight = weight_ref[k : k + 1, :]
            for q in range(per_step):
                value = jnp.exp2(s_ref[rs[q], lane(k)] - shifts[q] - log) * weight
                totals[q] = value if totals[q] is None else totals[q] + value
                kept = value if acc_in is None else acc_in[rs[q], lane(k)] + value
                acc_out[rs[q], lane(k)] = kept
        for q in range(per_step):
            total_ref[rs[q], :] = totals[q]
        return carry

    lax.fori_loop(0, rows // (GROUP * per_step), group_step, 0)
    for block in range(rows // LANES):
        part = total_ref[pl.ds(block * LANES, LANES), :].T
        out_ref[block : block + 1, :] = jnp.sum(part, axis=0, keepdims=True)


def last_col_adjoint_kernel(s_ref, got_ref, cot_ref, pot_ref, acc_ref, out_ref, half_ref, wide_ref, total_ref, log_ref):
    log_ref[...] = lse_parts([got_ref[p] for p in range(got_ref.shape[0])])
    half_ref[...] = 0.5 * cot_ref[...]
    spread_rows(pot_ref[...], wide_ref)
    col_adjoint_pass(s_ref, wide_ref, log_ref, half_ref, total_ref, None, acc_ref, out_ref)


def col_adjoint_kernel(s_ref, acc_in, got_ref, half_in, pot_ref, log_ref, acc_ref, out_ref, half_ref, wide_ref, total_ref):
    summed = tree([got_ref[p] for p in range(got_ref.shape[0])], jnp.add)
    half_ref[...] = 0.5 * (half_in[...] - summed)
    spread_rows(pot_ref[...], wide_ref)
    col_adjoint_pass(s_ref, wide_ref, log_ref, half_ref, total_ref, acc_in, acc_ref, out_ref)


def row_adjoint_pass(s_ref, pot_ref, log_wide, weight_wide, acc_in, acc_out, col_ref):
    rows, cols = s_ref.shape
    width, chunks = col_blocking(cols)
    per_step = math.gcd(rows // GROUP, 4)

    def chunk_step(c, carry):
        pots = [
            jnp.broadcast_to(pot_ref[pl.ds(c * width + k, 1), :], (GROUP, LANES))
            for k in range(width)
        ]

        def row_step(step, totals):
            for q in range(per_step):
                r = pl.ds(step * (GROUP * per_step) + q * GROUP, GROUP)
                log = log_wide[r, :]
                weight = weight_wide[r, :]
                fresh = []
                for k in range(width):
                    at = pl.ds(c * (width * LANES) + k * LANES, LANES)
                    value = jnp.exp2(s_ref[r, at] - pots[k] - log) * weight
                    acc_out[r, at] = acc_in[r, at] + value
                    fresh.append(totals[k] + value)
                totals = tuple(fresh)
            return totals

        zero = jnp.zeros((GROUP, LANES), jnp.float32)
        totals = lax.fori_loop(0, rows // (GROUP * per_step), row_step, (zero,) * width)
        for k in range(width):
            col_ref[pl.ds(c * width + k, 1), :] = jnp.sum(totals[k], axis=0, keepdims=True)
        return carry

    lax.fori_loop(0, chunks, chunk_step, 0)


def row_adjoint_kernel_of(parts, last):
    def kernel(*refs):
        s_ref, acc_in = refs[:2]
        part_refs = refs[2 : 2 + parts]
        rest = refs[2 + parts :]
        half_in, pot_ref, log_ref = rest[:3]
        rest = rest[3:]
        if last:
            fw_ref, ff_ref, out_ref, half_ref, acc_ref, log_wide, weight_wide, col_ref, pot_scaled = rest
            pot_scaled[...] = pot_ref[...] * LOG2E
            pot_ref = pot_scaled
        else:
            acc_ref, out_ref, half_ref, log_wide, weight_wide, col_ref = rest
        summed = tree([p[...] for p in part_refs], jnp.add)
        half = 0.5 * (half_in[...] - summed)
        half_ref[...] = half
        spread_rows(log_ref[...], log_wide)
        spread_rows(half, weight_wide)
        row_adjoint_pass(s_ref, pot_ref, log_wide, weight_wide, acc_in, acc_ref, col_ref)
        if not last:
            send_all(col_ref, out_ref)
            return
        grad = contract(acc_ref, fw_ref, ff_ref)
        col_rows = col_ref.shape[0]
        value = col_ref[...]
        for peer in range(out_ref.shape[0]):
            out_ref[peer, :col_rows, :] = value
            out_ref[peer, col_rows:, :] = grad

    return kernel


def contract(acc_ref, fw_ref, ff_ref):
    rows, cols = acc_ref.shape
    rank = ff_ref.shape[0]
    width = math.gcd(cols, 512)

    def halves(value):
        first = value.astype(jnp.bfloat16)
        return first, (value - first.astype(jnp.float32)).astype(jnp.bfloat16)

    def dot_step(c, grad):
        chunk = pl.ds(c * width, width)
        f1, f2 = halves(ff_ref[:, chunk])
        rhs = jnp.concatenate([f1, f2], axis=0)
        a1, a2 = halves(acc_ref[:, chunk])
        dims = (((1,), (1,)), ((), ()))
        grad = grad + lax.dot_general(a1, rhs, dims, preferred_element_type=jnp.float32)
        return grad + lax.dot_general(a2, rhs, dims, preferred_element_type=jnp.float32)

    grad = lax.fori_loop(0, cols // width, dot_step, jnp.zeros((rows, 2 * rank), jnp.float32))
    grad = grad + pltpu.roll(grad, rank, 1)
    both = lax.dot_general(
        fw_ref[...], grad, (((0,), (0,)), ((), ())), precision=HIGHEST,
        preferred_element_type=jnp.float32,
    )
    half = rank // 2
    lanes = lax.broadcasted_iota(jnp.int32, (half, 2 * rank), 1)
    return jnp.where(lanes < rank, both[:half], both[half:])


def peers_of(part, axis):
    size = lax.axis_size(axis)
    if size & (size - 1):
        gathered = lax.all_gather(part, axis)
        return [gathered[i] for i in range(size)]
    return [part] + [
        lax.ppermute(part, axis, [(i, i ^ d) for i in range(size)]) for d in range(1, size)
    ]


def exchange_cols(block):
    return lax.all_to_all(block, "wrk", 0, 0, tiled=True)


def body(feat_wrk, feat_firm, surplus, row_start, col_start, row_mass, col_mass, row_cot, col_cot):
    rows, rank = feat_wrk.shape
    cols = feat_firm.shape[1]
    wrk, firm = lax.axis_size("wrk"), lax.axis_size("firm")
    row_dims = (rows // LANES, LANES)
    col_dims = (cols // LANES, LANES)
    row_start, row_mass, row_cot = (a.reshape(row_dims) for a in (row_start, row_mass, row_cot))
    col_start, col_mass, col_cot = (a.reshape(col_dims) for a in (col_start, col_mass, col_cot))
    wide = pltpu.VMEM((rows, LANES), jnp.float32)
    col_vec = pltpu.VMEM(col_dims, jnp.float32)
    row_out, col_out = shape_of(*row_dims), shape_of(*col_dims)
    send_out = shape_of(wrk, *col_dims)
    acc_out = shape_of(rows, cols)

    scores, part = call(
        first_row_kernel, "row_first", (acc_out, row_out),
        (feat_wrk, feat_firm, surplus, col_start),
        (col_vec, pltpu.VMEM((LANES, LANES), jnp.float32), wide, wide),
    )
    row_pots, col_pots, row_logs, col_logs = [row_start], [col_start], [], []
    for t in range(ITERS):
        parts = peers_of(part, "firm")
        block, log, pot = call(
            col_kernel_of(len(parts), t == 0), f"col_{t}", (send_out, row_out, row_out),
            (scores, *parts, row_pots[-1], row_mass), (wide, col_vec),
        )
        row_logs.append(log)
        row_pots.append(pot)
        got = exchange_cols(block)
        if t == ITERS - 1:
            break
        part, log, pot = call(
            row_kernel_of(t == 0), f"row_{t + 1}", (row_out, col_out, col_out),
            (scores, got, col_pots[-1], col_mass), (wide, wide),
        )
        col_logs.append(log)
        col_pots.append(pot)

    acc, part, col_half = call(
        last_col_adjoint_kernel, f"col_adj_{ITERS - 1}", (acc_out, row_out, col_out),
        (scores, got, col_cot, row_pots[ITERS]), (wide, wide, col_vec),
    )
    row_half = row_cot
    for t in reversed(range(ITERS)):
        parts = peers_of(part, "firm")
        args = (scores, acc, *parts, row_half, col_pots[t], row_logs[t])
        if t == 0:
            break
        acc, block, row_half = call(
            row_adjoint_kernel_of(len(parts), False), f"row_adj_{t}", (acc_out, send_out, row_out),
            args, (wide, wide, col_vec), {1: 0},
        )
        got = exchange_cols(block)
        acc, part, col_half = call(
            col_adjoint_kernel, f"col_adj_{t - 1}", (acc_out, row_out, col_out),
            (scores, acc, got, col_half, row_pots[t], col_logs[t - 1]), (wide, wide), {1: 0},
        )

    grad_rows = rank * rank // LANES
    block, row_half = call(
        row_adjoint_kernel_of(len(parts), True), "row_adj_0",
        (shape_of(wrk, col_dims[0] + grad_rows, LANES), row_out),
        (*args, feat_wrk, feat_firm),
        (pltpu.VMEM((rows, cols), jnp.float32), wide, wide, col_vec, col_vec),
    )
    summed = jnp.sum(exchange_cols(block), axis=0)
    col_bar = col_half - summed[: col_dims[0]]
    grad = tree(peers_of(summed[col_dims[0] :], "firm"), jnp.add)
    grad_surplus = jnp.concatenate([grad[:, :rank], grad[:, rank:]], axis=0)
    return (grad_surplus, row_half.reshape(rows), col_bar.reshape(cols))


def solution(mesh):
    return jax.shard_map(
        body,
        mesh=mesh,
        in_specs=(
            P("wrk", None),
            P(None, "firm"),
            P(),
            P("wrk"),
            P("firm"),
            P("wrk"),
            P("firm"),
            P("wrk"),
            P("firm"),
        ),
        out_specs=(P(), P("wrk"), P("firm")),
        check_vma=False,
    )
```

time: 705 us -> 179 us (0.25)
  blocking collectives: 374 us -> 64.2 us
  matrix products: 170 us -> 0 us
  Pallas kernels: 0 us -> 77.9 us
  local copies, waits for them, and re-layouts: 78.9 us -> 5.19 us
  loops' own time: 67.1 us -> 0 us
  starting transfers between devices: 0 us -> 15 us
  waiting for transfers between devices: 0 us -> 14.2 us
  other arithmetic: 11.6 us -> 1.25 us
    all_gather x12 -> x0, blocking collectives: 216 us -> none  [joined(): gathered = jax.tree.map(lambda a: lax.all_gather(a, axis), part)]
    dot_general x146 -> x0, matrix products: 170 us -> none  [the longest x48 60.1 us: block_step(): scores = jnp.dot(mixed, tile_cols, precision=HIGHEST) - shift_part[None, :]]
    psum x7 -> x0, blocking collectives: 157 us -> none  [the longest x3 103 us: body(): col_bar = col_bar - lax.psum(col_total, 'wrk')]
    pallas_call x0 -> x12, Pallas kernels: none -> 77.9 us  [call(): pl.pallas_call(kernel, name=name, out_shape=outs, in_specs=[WHOLE] * len(...]
    dynamic_slice x239 -> x0, local copies, waits for them, and re-layouts: 67.8 us -> none  [the longest x96 56.3 us: row_local(): (run_max, run_total), unused = lax.scan(block_step, start_state, block_ids)]
    another operation x18 -> x0, loops' own time: 67.1 us -> none  [the longest x3 16.7 us: row_weights(): lax.scan(block_step, jnp.zeros(mixed.shape, jnp.float32), block_ids)]
    all_to_all x0 -> x6, blocking collectives: none -> 64.2 us  [exchange_cols(): return lax.all_to_all(block, 'wrk', 0, 0, tiled=True)]
    ppermute x0 -> x21, starting transfers between devices: none -> 15 us  [peers_of(): lax.ppermute(part, axis, [(i, i ^ d) for i in range(size)])]
  transfers between devices with their start and end apart: 0 -> 21, of which waited for: 0 -> 14; matrix products, arithmetic and copies ran while one was open for 0% -> 0% of each run, Pallas kernels for 0% -> 0%
where the time goes in v1:
time: 179 us; the launch traced here: 178 us
  Pallas kernels  77.9 us (44%)
  blocking collectives  64.2 us (36%)
  starting transfers between devices  15 us (8%)
  waiting for transfers between devices  14.2 us (8%)
  local copies, waits for them, and re-layouts  5.19 us (3%)
    pallas_call x12, Pallas kernels, call(): pl.pallas_call(kernel, name=name, out_shape=outs, in_specs=[WHOLE] * len(...  77.9 us
    all_to_all x6, blocking collectives, exchange_cols(): return lax.all_to_all(block, 'wrk', 0, 0, tiled=True)  64.2 us
    ppermute x21, starting transfers between devices, peers_of(): lax.ppermute(part, axis, [(i, i ^ d) for i in range(size)])  15 us
    ppermute x21, waiting for transfers between devices, peers_of(): lax.ppermute(part, axis, [(i, i ^ d) for i in range(size)])  14.2 us
    unnamed x21, local copies, waits for them, and re-layouts  5.11 us
  transfers between devices with their start and end apart: 21, of which 14 were waited for; matrix products, arithmetic and copies ran while one was open for 0% of the time, Pallas kernels for 0%

profile of v1, /device:TPU:0, one launch (start us, length us, event | category | flops | bytes accessed | tf_op | source)
XLA Modules:
  0.0 178.4 jit_solution(8378793382233520014)
XLA Ops:
  0.6 1.0 copy.16.fw_ref.refs_9_
  1.7 1.2 copy-done
  2.9 0.7 copy-done.1
  3.6 0.8 copy-done.4
  4.4 7.4 %row_first.1 = (f32[512,4096]{1,0:T(8,128)S(1)}, f32[4,128]{1,0:T(4,128)S(1)}) custom-call(f32[512,64]{1,0:T(8,128)S(1)} %copy.16.fw_ref.refs_9_, f32[64,4096]{1,0:T(8,128)S(1)} %copy-done, f32[64,64]{1,0:T(8,128)S(1)} %copy-done.4, f32[32,128]{1,0:T(8,128)S(1)} %bitcast.9), custom_call_target="tpu_custom_call" | custom-call | tf_op jit(solution)/shard_map/row_first/pallas_call | solution.py:34
  11.8 2.5 %collective-permute-start.2 = (f32[4,128]{1,0:T(4,128)S(1)}, f32[4,128]{1,0:T(4,128)S(1)}, u32[]{:S(2)}, u32[]{:S(2)}) collective-permute-start(f32[4,128]{1,0:T(4,128)S(1)} %get-tuple-element.38.refs_1_), channel_id=1, source_target_pairs={{0,3},{1,2},{2,1},{3,0},{4,7},{5,6},{6,5},{7,4},{8,11},{9,10},{10,... | collective-permute-start | bytes 6152 | tf_op jit(solution)/shard_map/ppermute | solution.py:341
  15.6 2.3 %collective-permute-done.1.refs_3_ = f32[4,128]{1,0:T(4,128)S(1)} collective-permute-done((f32[4,128]{1,0:T(4,128)S(1)}, f32[4,128]{1,0:T(4,128)S(1)}, u32[]{:S(2)}, u32[]{:S(2)}) %collective-permute-start.1) | collective-permute-done | bytes 2080 | tf_op jit(solution)/shard_map/ppermute | solution.py:341
  17.9 0.7 copy-done.5
  18.6 0.7 copy-done.8
  19.3 6.1 %col_0.1 = (f32[8,32,128]{2,1,0:T(8,128)S(1)}, f32[4,128]{1,0:T(4,128)S(1)}, f32[4,128]{1,0:T(4,128)S(1)}) custom-call(f32[512,4096]{1,0:T(8,128)S(1)} %get-tuple-element.37.refs_0_.s_ref, f32[4,128]{1,0:T(4,128)S(1)} %get-tuple-element.38.refs_1_, f32[4,128]{1,0:T(4,128)S(1)} %collective-permute-done.refs_2_, f32[4,128]{1,0:T(4,128)S(1)} %collective-permute-done.1.refs_3_, ...), custom_call_target="tpu_custom_call" | custom-call | tf_op jit(solution)/shard_map/col_0/pallas_call | solution.py:34
  25.4 13.0 %all_to_all.30.got_ref = f32[8,32,128]{2,1,0:T(8,128)S(1)} all-to-all(f32[8,32,128]{2,1,0:T(8,128)S(1)} %get-tuple-element.39), channel_id=1, replica_groups=mesh['wrk'=8,'firm'=4] {'wrk'}, dimensions={0} | all-to-all | bytes 262144 | tf_op jit(solution)/shard_map/all_to_all | solution.py:346
  38.4 3.3 %row_1.1 = (f32[4,128]{1,0:T(4,128)S(1)}, f32[32,128]{1,0:T(8,128)S(1)}, f32[32,128]{1,0:T(8,128)S(1)}) custom-call(f32[512,4096]{1,0:T(8,128)S(1)} %get-tuple-element.37.refs_0_.s_ref, f32[8,32,128]{2,1,0:T(8,128)S(1)} %all_to_all.30.got_ref, f32[32,128]{1,0:T(8,128)S(1)} %bitcast.10, f32[32,128]{1,0:T(8,128)S(1)} %bitcast.12), custom_call_target="tpu_custom_call" | custom-call | tf_op jit(solution)/shard_map/row_1/pallas_call | solution.py:34
  41.8 0.7 collective-permute-start.4
  42.5 1.1 collective-permute-start.3
  43.6 1.1 collective-permute-done.5.refs_4_
  44.8 0.7 collective-permute-done.4.refs_3_
  45.4 6.1 %col_1.1 = (f32[8,32,128]{2,1,0:T(8,128)S(1)}, f32[4,128]{1,0:T(4,128)S(1)}, f32[4,128]{1,0:T(4,128)S(1)}) custom-call(f32[512,4096]{1,0:T(8,128)S(1)} %get-tuple-element.37.refs_0_.s_ref, f32[4,128]{1,0:T(4,128)S(1)} %get-tuple-element.40.refs_1_, f32[4,128]{1,0:T(4,128)S(1)} %collective-permute-done.3.refs_2_, ...), custom_call_target="tpu_custom_call" | custom-call | tf_op jit(solution)/shard_map/col_1/pallas_call | solution.py:34
  51.6 9.7 %all_to_all.31.got_ref = f32[8,32,128]{2,1,0:T(8,128)S(1)} all-to-all(f32[8,32,128]{2,1,0:T(8,128)S(1)} %get-tuple-element.42), channel_id=1, replica_groups=mesh['wrk'=8,'firm'=4] {'wrk'}, dimensions={0} | all-to-all | bytes 262144 | tf_op jit(solution)/shard_map/all_to_all | solution.py:346
  61.3 3.5 %row_2.1 = (f32[4,128]{1,0:T(4,128)S(1)}, f32[32,128]{1,0:T(8,128)S(1)}, f32[32,128]{1,0:T(8,128)S(1)}) custom-call(f32[512,4096]{1,0:T(8,128)S(1)} %get-tuple-element.37.refs_0_.s_ref, f32[8,32,128]{2,1,0:T(8,128)S(1)} %all_to_all.31.got_ref, f32[32,128]{1,0:T(8,128)S(1)} %get-tuple-element.43.old_ref.refs_7_, f32[32,128]{1,0:T(8,128)S(1)} %bitcast.13), custom_call_target="tpu_custom_call" | custom-call | tf_op jit(solution)/shard_map/row_2/pallas_call | solution.py:34
  64.9 1.1 collective-permute-start.7
  66.0 0.8 collective-permute-start.6
  66.8 1.1 collective-permute-done.8.refs_4_
  68.6 6.1 %col_2.1 = (f32[8,32,128]{2,1,0:T(8,128)S(1)}, f32[4,128]{1,0:T(4,128)S(1)}, f32[4,128]{1,0:T(4,128)S(1)}) custom-call(f32[512,4096]{1,0:T(8,128)S(1)} %get-tuple-element.37.refs_0_.s_ref, f32[4,128]{1,0:T(4,128)S(1)} %get-tuple-element.44.refs_1_, f32[4,128]{1,0:T(4,128)S(1)} %collective-permute-done.6.refs_2_, ...), custom_call_target="tpu_custom_call" | custom-call | tf_op jit(solution)/shard_map/col_2/pallas_call | solution.py:34
  74.7 10.1 %all_to_all.32.got_ref = f32[8,32,128]{2,1,0:T(8,128)S(1)} all-to-all(f32[8,32,128]{2,1,0:T(8,128)S(1)} %get-tuple-element.46), channel_id=1, replica_groups=mesh['wrk'=8,'firm'=4] {'wrk'}, dimensions={0} | all-to-all | bytes 262144 | tf_op jit(solution)/shard_map/all_to_all | solution.py:346
  84.9 2.0 %col_adj_2.1 = (f32[512,4096]{1,0:T(8,128)S(1)}, f32[4,128]{1,0:T(4,128)S(1)}, f32[32,128]{1,0:T(8,128)S(1)}) custom-call(f32[512,4096]{1,0:T(8,128)S(1)} %get-tuple-element.37.refs_0_.s_ref, f32[8,32,128]{2,1,0:T(8,128)S(1)} %all_to_all.32.got_ref, f32[32,128]{1,0:T(8,128)S(1)} %bitcast.17, f32[4,128]{1,0:T(4,128)S(1)} %get-tuple-element.47.pot_ref), custom_call_target="tpu_custom_call" | custom-call | tf_op jit(solution)/shard_map/col_adj_2/pallas_call | solution.py:34
  87.0 0.9 collective-permute-start.10
  87.8 1.0 collective-permute-start.9
  88.8 1.1 collective-permute-done.11.refs_5_
  90.0 0.7 collective-permute-done.10.refs_4_
  90.6 8.1 %row_adj_2.1 = (f32[512,4096]{1,0:T(8,128)S(1)}, f32[8,32,128]{2,1,0:T(8,128)S(1)}, f32[4,128]{1,0:T(4,128)S(1)}) custom-call(f32[512,4096]{1,0:T(8,128)S(1)} %get-tuple-element.37.refs_0_.s_ref, f32[512,4096]{1,0:T(8,128)S(1)} %get-tuple-element.48.refs_1_, f32[4,128]{1,0:T(4,128)S(1)} %get-tuple-element.49.refs_2_, ...), custom_call_target="tpu_custom_call", output_to_operand_aliasing={{0}: (1, {})} | custom-call | tf_op jit(solution)/shard_map/row_adj_2/pallas_call | solution.py:34
  98.7 9.9 %all_to_all.33.got_ref = f32[8,32,128]{2,1,0:T(8,128)S(1)} all-to-all(f32[8,32,128]{2,1,0:T(8,128)S(1)} %get-tuple-element.53), channel_id=1, replica_groups=mesh['wrk'=8,'firm'=4] {'wrk'}, dimensions={0} | all-to-all | bytes 262144 | tf_op jit(solution)/shard_map/all_to_all | solution.py:346
  108.7 9.2 %col_adj_1.1 = (f32[512,4096]{1,0:T(8,128)S(1)}, f32[4,128]{1,0:T(4,128)S(1)}, f32[32,128]{1,0:T(8,128)S(1)}) custom-call(f32[512,4096]{1,0:T(8,128)S(1)} %get-tuple-element.37.refs_0_.s_ref, f32[512,4096]{1,0:T(8,128)S(1)} %get-tuple-element.52.acc_in, f32[8,32,128]{2,1,0:T(8,128)S(1)} %all_to_all.33.got_ref, ...), custom_call_target="tpu_custom_call", output_to_operand_aliasing={{0}: (1, {})} | custom-call | tf_op jit(solution)/shard_map/col_adj_1/pallas_call | solution.py:34
  117.9 0.9 collective-permute-start.13
  118.8 1.0 collective-permute-start.12
  119.8 1.1 collective-permute-done.14.refs_5_
  120.9 0.7 collective-permute-done.13.refs_4_
  121.6 8.1 %row_adj_1.1 = (f32[512,4096]{1,0:T(8,128)S(1)}, f32[8,32,128]{2,1,0:T(8,128)S(1)}, f32[4,128]{1,0:T(4,128)S(1)}) custom-call(f32[512,4096]{1,0:T(8,128)S(1)} %get-tuple-element.37.refs_0_.s_ref, f32[512,4096]{1,0:T(8,128)S(1)} %get-tuple-element.56.refs_1_, f32[4,128]{1,0:T(4,128)S(1)} %get-tuple-element.57.refs_2_, ...), custom_call_target="tpu_custom_call", output_to_operand_aliasing={{0}: (1, {})} | custom-call | tf_op jit(solution)/shard_map/row_adj_1/pallas_call | solution.py:34
  129.7 9.9 %all_to_all.34.got_ref = f32[8,32,128]{2,1,0:T(8,128)S(1)} all-to-all(f32[8,32,128]{2,1,0:T(8,128)S(1)} %get-tuple-element.61), channel_id=1, replica_groups=mesh['wrk'=8,'firm'=4] {'wrk'}, dimensions={0} | all-to-all | bytes 262144 | tf_op jit(solution)/shard_map/all_to_all | solution.py:346
  139.6 9.2 %col_adj_0.1 = (f32[512,4096]{1,0:T(8,128)S(1)}, f32[4,128]{1,0:T(4,128)S(1)}, f32[32,128]{1,0:T(8,128)S(1)}) custom-call(f32[512,4096]{1,0:T(8,128)S(1)} %get-tuple-element.37.refs_0_.s_ref, f32[512,4096]{1,0:T(8,128)S(1)} %get-tuple-element.60.acc_in, f32[8,32,128]{2,1,0:T(8,128)S(1)} %all_to_all.34.got_ref, ...), custom_call_target="tpu_custom_call", output_to_operand_aliasing={{0}: (1, {})} | custom-call | tf_op jit(solution)/shard_map/col_adj_0/pallas_call | solution.py:34
  148.9 0.9 collective-permute-start.16
  149.7 1.0 collective-permute-start.15
  150.7 1.1 collective-permute-done.17.refs_5_
  151.9 0.7 collective-permute-done.16.refs_4_
  152.5 8.6 %row_adj_0.1 = (f32[8,64,128]{2,1,0:T(8,128)S(1)}, f32[4,128]{1,0:T(4,128)}) custom-call(f32[512,4096]{1,0:T(8,128)S(1)} %get-tuple-element.37.refs_0_.s_ref, f32[512,4096]{1,0:T(8,128)S(1)} %get-tuple-element.64.refs_1_, f32[4,128]{1,0:T(4,128)S(1)} %get-tuple-element.65.refs_2_, f32[4,128]{1,0:T(4,128)S(1)} %collective-permute-done.15.refs_3_, ...), custom_call_target="tpu_custom_call" | custom-call | tf_op jit(solution)/shard_map/row_adj_0/pallas_call | solution.py:34
  161.1 11.5 %all_to_all.35 = f32[8,64,128]{2,1,0:T(8,128)S(1)} all-to-all(f32[8,64,128]{2,1,0:T(8,128)S(1)} %get-tuple-element.68), channel_id=1, replica_groups=mesh['wrk'=8,'firm'=4] {'wrk'}, dimensions={0} | all-to-all | bytes 524288 | tf_op jit(solution)/shard_map/all_to_all | solution.py:346
  172.6 1.3 collective-permute-start.19
  173.9 0.9 collective-permute-start.18
  174.8 1.6 collective-permute-done.19
  (38 shorter events, 4.3 us)
Async XLA Ops:
  0.6 37.7 %copy-start.3 = (f32[4096]{0:T(1024)S(1)}, f32[4096]{0:T(1024)}, u32[]{:S(2)}) copy-start(f32[4096]{0:T(1024)} %param.15) | copy-start | bytes 49156
  1.7 1.2 copy-start
  2.9 0.7 copy-start.1
  3.6 0.8 copy-start.4
  11.8 3.8 %collective-permute-start.2 = (f32[4,128]{1,0:T(4,128)S(1)}, f32[4,128]{1,0:T(4,128)S(1)}, u32[]{:S(2)}, u32[]{:S(2)}) collective-permute-start(f32[4,128]{1,0:T(4,128)S(1)} %get-tuple-element.38.refs_1_), channel_id=1, source_target_pairs={{0,3},{1,2},{2,1},{3,0},{4,7},{5,6},{6,5},{7,4},{8,11},{9,10},{10,... | collective-permute-start | bytes 6152 | tf_op jit(solution)/shard_map/ppermute | solution.py:341
  14.3 3.6 %collective-permute-start.1 = (f32[4,128]{1,0:T(4,128)S(1)}, f32[4,128]{1,0:T(4,128)S(1)}, u32[]{:S(2)}, u32[]{:S(2)}) collective-permute-start(f32[4,128]{1,0:T(4,128)S(1)} %get-tuple-element.38.refs_1_), channel_id=1, source_target_pairs={{0,2},{1,3},{2,0},{3,1},{4,6},{5,7},{6,4},{7,5},{8,10},{9,11},{10,... | collective-permute-start | bytes 6152 | tf_op jit(solution)/shard_map/ppermute | solution.py:341
  14.9 2.9 %collective-permute-start = (f32[4,128]{1,0:T(4,128)S(1)}, f32[4,128]{1,0:T(4,128)S(1)}, u32[]{:S(2)}, u32[]{:S(2)}) collective-permute-start(f32[4,128]{1,0:T(4,128)S(1)} %get-tuple-element.38.refs_1_), channel_id=1, source_target_pairs={{0,1},{1,0},{2,3},{3,2},{4,5},{5,4},{6,7},{7,6},{8,9},{9,8},{10,11... | collective-permute-start | bytes 6152 | tf_op jit(solution)/shard_map/ppermute | solution.py:341
  17.9 0.7 copy-start.5
  18.6 0.7 copy-start.8
  19.3 26.2 %copy-start.6 = (f32[512]{0:T(512)S(1)}, f32[512]{0:T(512)}, u32[]{:S(2)}) copy-start(f32[512]{0:T(512)} %param.14) | copy-start | bytes 6148
  41.7 3.1 %collective-permute-start.5 = (f32[4,128]{1,0:T(4,128)S(1)}, f32[4,128]{1,0:T(4,128)S(1)}, u32[]{:S(2)}, u32[]{:S(2)}) collective-permute-start(f32[4,128]{1,0:T(4,128)S(1)} %get-tuple-element.40.refs_1_), channel_id=1, source_target_pairs={{0,3},{1,2},{2,1},{3,0},{4,7},{5,6},{6,5},{7,4},{8,11},{9,10},{10,... | collective-permute-start | bytes 6152 | tf_op jit(solution)/shard_map/ppermute | solution.py:341
  41.8 3.7 %collective-permute-start.4 = (f32[4,128]{1,0:T(4,128)S(1)}, f32[4,128]{1,0:T(4,128)S(1)}, u32[]{:S(2)}, u32[]{:S(2)}) collective-permute-start(f32[4,128]{1,0:T(4,128)S(1)} %get-tuple-element.40.refs_1_), channel_id=1, source_target_pairs={{0,2},{1,3},{2,0},{3,1},{4,6},{5,7},{6,4},{7,5},{8,10},{9,11},{10,... | collective-permute-start | bytes 6152 | tf_op jit(solution)/shard_map/ppermute | solution.py:341
  42.5 3.0 %collective-permute-start.3 = (f32[4,128]{1,0:T(4,128)S(1)}, f32[4,128]{1,0:T(4,128)S(1)}, u32[]{:S(2)}, u32[]{:S(2)}) collective-permute-start(f32[4,128]{1,0:T(4,128)S(1)} %get-tuple-element.40.refs_1_), channel_id=1, source_target_pairs={{0,1},{1,0},{2,3},{3,2},{4,5},{5,4},{6,7},{7,6},{8,9},{9,8},{10,11... | collective-permute-start | bytes 6152 | tf_op jit(solution)/shard_map/ppermute | solution.py:341
  61.3 23.5 %copy-start.7 = (f32[4096]{0:T(1024)S(1)}, f32[4096]{0:T(1024)}, u32[]{:S(2)}) copy-start(f32[4096]{0:T(1024)} %param.17) | copy-start | bytes 49156
  64.8 3.1 %collective-permute-start.8 = (f32[4,128]{1,0:T(4,128)S(1)}, f32[4,128]{1,0:T(4,128)S(1)}, u32[]{:S(2)}, u32[]{:S(2)}) collective-permute-start(f32[4,128]{1,0:T(4,128)S(1)} %get-tuple-element.44.refs_1_), channel_id=1, source_target_pairs={{0,3},{1,2},{2,1},{3,0},{4,7},{5,6},{6,5},{7,4},{8,11},{9,10},{10,... | collective-permute-start | bytes 6152 | tf_op jit(solution)/shard_map/ppermute | solution.py:341
  64.9 3.7 %collective-permute-start.7 = (f32[4,128]{1,0:T(4,128)S(1)}, f32[4,128]{1,0:T(4,128)S(1)}, u32[]{:S(2)}, u32[]{:S(2)}) collective-permute-start(f32[4,128]{1,0:T(4,128)S(1)} %get-tuple-element.44.refs_1_), channel_id=1, source_target_pairs={{0,2},{1,3},{2,0},{3,1},{4,6},{5,7},{6,4},{7,5},{8,10},{9,11},{10,... | collective-permute-start | bytes 6152 | tf_op jit(solution)/shard_map/ppermute | solution.py:341
  66.0 2.6 %collective-permute-start.6 = (f32[4,128]{1,0:T(4,128)S(1)}, f32[4,128]{1,0:T(4,128)S(1)}, u32[]{:S(2)}, u32[]{:S(2)}) collective-permute-start(f32[4,128]{1,0:T(4,128)S(1)} %get-tuple-element.44.refs_1_), channel_id=1, source_target_pairs={{0,1},{1,0},{2,3},{3,2},{4,5},{5,4},{6,7},{7,6},{8,9},{9,8},{10,11... | collective-permute-start | bytes 6152 | tf_op jit(solution)/shard_map/ppermute | solution.py:341
  68.6 22.1 %copy-start.9 = (f32[512]{0:T(512)S(1)}, f32[512]{0:T(512)}, u32[]{:S(2)}) copy-start(f32[512]{0:T(512)} %param.16) | copy-start | bytes 6148
  86.9 3.1 %collective-permute-start.11 = (f32[4,128]{1,0:T(4,128)S(1)}, f32[4,128]{1,0:T(4,128)S(1)}, u32[]{:S(2)}, u32[]{:S(2)}) collective-permute-start(f32[4,128]{1,0:T(4,128)S(1)} %get-tuple-element.49.refs_2_), channel_id=1, source_target_pairs={{0,3},{1,2},{2,1},{3,0},{4,7},{5,6},{6,5},{7,4},{8,11},{9,10},{10,... | collective-permute-start | bytes 6152 | tf_op jit(solution)/shard_map/ppermute | solution.py:341
  87.0 3.7 %collective-permute-start.10 = (f32[4,128]{1,0:T(4,128)S(1)}, f32[4,128]{1,0:T(4,128)S(1)}, u32[]{:S(2)}, u32[]{:S(2)}) collective-permute-start(f32[4,128]{1,0:T(4,128)S(1)} %get-tuple-element.49.refs_2_), channel_id=1, source_target_pairs={{0,2},{1,3},{2,0},{3,1},{4,6},{5,7},{6,4},{7,5},{8,10},{9,11},{10,... | collective-permute-start | bytes 6152 | tf_op jit(solution)/shard_map/ppermute | solution.py:341
  87.8 2.8 %collective-permute-start.9 = (f32[4,128]{1,0:T(4,128)S(1)}, f32[4,128]{1,0:T(4,128)S(1)}, u32[]{:S(2)}, u32[]{:S(2)}) collective-permute-start(f32[4,128]{1,0:T(4,128)S(1)} %get-tuple-element.49.refs_2_), channel_id=1, source_target_pairs={{0,1},{1,0},{2,3},{3,2},{4,5},{5,4},{6,7},{7,6},{8,9},{9,8},{10,11... | collective-permute-start | bytes 6152 | tf_op jit(solution)/shard_map/ppermute | solution.py:341
  117.8 3.1 %collective-permute-start.14 = (f32[4,128]{1,0:T(4,128)S(1)}, f32[4,128]{1,0:T(4,128)S(1)}, u32[]{:S(2)}, u32[]{:S(2)}) collective-permute-start(f32[4,128]{1,0:T(4,128)S(1)} %get-tuple-element.57.refs_2_), channel_id=1, source_target_pairs={{0,3},{1,2},{2,1},{3,0},{4,7},{5,6},{6,5},{7,4},{8,11},{9,10},{10,... | collective-permute-start | bytes 6152 | tf_op jit(solution)/shard_map/ppermute | solution.py:341
  117.9 3.7 %collective-permute-start.13 = (f32[4,128]{1,0:T(4,128)S(1)}, f32[4,128]{1,0:T(4,128)S(1)}, u32[]{:S(2)}, u32[]{:S(2)}) collective-permute-start(f32[4,128]{1,0:T(4,128)S(1)} %get-tuple-element.57.refs_2_), channel_id=1, source_target_pairs={{0,2},{1,3},{2,0},{3,1},{4,6},{5,7},{6,4},{7,5},{8,10},{9,11},{10,... | collective-permute-start | bytes 6152 | tf_op jit(solution)/shard_map/ppermute | solution.py:341
  118.8 2.8 %collective-permute-start.12 = (f32[4,128]{1,0:T(4,128)S(1)}, f32[4,128]{1,0:T(4,128)S(1)}, u32[]{:S(2)}, u32[]{:S(2)}) collective-permute-start(f32[4,128]{1,0:T(4,128)S(1)} %get-tuple-element.57.refs_2_), channel_id=1, source_target_pairs={{0,1},{1,0},{2,3},{3,2},{4,5},{5,4},{6,7},{7,6},{8,9},{9,8},{10,11... | collective-permute-start | bytes 6152 | tf_op jit(solution)/shard_map/ppermute | solution.py:341
  139.6 12.9 %copy-start.2 = (f32[4096]{0:T(1024)S(1)}, f32[4096]{0:T(1024)}, u32[]{:S(2)}) copy-start(f32[4096]{0:T(1024)} %param.13) | copy-start | bytes 49156
  148.8 3.1 %collective-permute-start.17 = (f32[4,128]{1,0:T(4,128)S(1)}, f32[4,128]{1,0:T(4,128)S(1)}, u32[]{:S(2)}, u32[]{:S(2)}) collective-permute-start(f32[4,128]{1,0:T(4,128)S(1)} %get-tuple-element.65.refs_2_), channel_id=1, source_target_pairs={{0,3},{1,2},{2,1},{3,0},{4,7},{5,6},{6,5},{7,4},{8,11},{9,10},{10,... | collective-permute-start | bytes 6152 | tf_op jit(solution)/shard_map/ppermute | solution.py:341
  148.9 3.7 %collective-permute-start.16 = (f32[4,128]{1,0:T(4,128)S(1)}, f32[4,128]{1,0:T(4,128)S(1)}, u32[]{:S(2)}, u32[]{:S(2)}) collective-permute-start(f32[4,128]{1,0:T(4,128)S(1)} %get-tuple-element.65.refs_2_), channel_id=1, source_target_pairs={{0,2},{1,3},{2,0},{3,1},{4,6},{5,7},{6,4},{7,5},{8,10},{9,11},{10,... | collective-permute-start | bytes 6152 | tf_op jit(solution)/shard_map/ppermute | solution.py:341
  149.7 2.8 %collective-permute-start.15 = (f32[4,128]{1,0:T(4,128)S(1)}, f32[4,128]{1,0:T(4,128)S(1)}, u32[]{:S(2)}, u32[]{:S(2)}) collective-permute-start(f32[4,128]{1,0:T(4,128)S(1)} %get-tuple-element.65.refs_2_), channel_id=1, source_target_pairs={{0,1},{1,0},{2,3},{3,2},{4,5},{5,4},{6,7},{7,6},{8,9},{9,8},{10,11... | collective-permute-start | bytes 6152 | tf_op jit(solution)/shard_map/ppermute | solution.py:341
  172.6 3.8 %collective-permute-start.19 = (f32[32,128]{1,0:T(8,128)S(1)}, f32[32,128]{1,0:T(8,128)S(1)}, u32[]{:S(2)}, u32[]{:S(2)}) collective-permute-start(f32[32,128]{1,0:T(8,128)S(1)} %slice.16), channel_id=1, source_target_pairs={{0,2},{1,3},{2,0},{3,1},{4,6},{5,7},{6,4},{7,5},{8,10},{9,11},{10,... | collective-permute-start | bytes 49160 | tf_op jit(solution)/shard_map/ppermute | solution.py:341
  173.9 3.2 %collective-permute-start.20 = (f32[32,128]{1,0:T(8,128)S(1)}, f32[32,128]{1,0:T(8,128)S(1)}, u32[]{:S(2)}, u32[]{:S(2)}) collective-permute-start(f32[32,128]{1,0:T(8,128)S(1)} %slice.16), channel_id=1, source_target_pairs={{0,3},{1,2},{2,1},{3,0},{4,7},{5,6},{6,5},{7,4},{8,11},{9,10},{10,... | collective-permute-start | bytes 49160 | tf_op jit(solution)/shard_map/ppermute | solution.py:341
  173.9 3.2 %collective-permute-start.18 = (f32[32,128]{1,0:T(8,128)S(1)}, f32[32,128]{1,0:T(8,128)S(1)}, u32[]{:S(2)}, u32[]{:S(2)}) collective-permute-start(f32[32,128]{1,0:T(8,128)S(1)} %slice.16), channel_id=1, source_target_pairs={{0,1},{1,0},{2,3},{3,2},{4,5},{5,4},{6,7},{7,6},{8,9},{9,8},{10,11... | collective-permute-start | bytes 49160 | tf_op jit(solution)/shard_map/ppermute | solution.py:341

commit v2 on v1

--- a/solution.py
+++ b/solution.py
@@ -13,7 +13,7 @@
 LANES = 128
 GROUP = 8
 WHOLE = pl.BlockSpec(memory_space=pltpu.VMEM)
-VMEM_LIMIT = 24 * 1024 * 1024
+VMEM_LIMIT = 14 * 1024 * 1024
 
 
 def tree(values, combine):
@@ -30,15 +30,14 @@
     return jax.ShapeDtypeStruct(dims, jnp.float32)
 
 
-def call(kernel, name, outs, args, scratch=(), aliases=None):
+def call(kernel, name, outs, args, scratch=(), space=pltpu.VMEM):
     return pl.pallas_call(
         kernel,
         name=name,
         out_shape=outs,
-        in_specs=[WHOLE] * len(args),
+        in_specs=[pl.BlockSpec(memory_space=space)] * len(args),
         out_specs=jax.tree.map(lambda _: WHOLE, outs),
         scratch_shapes=scratch,
-        input_output_aliases=aliases or {},
         compiler_params=pltpu.CompilerParams(vmem_limit_bytes=VMEM_LIMIT),
     )(*args)
 
@@ -61,16 +60,21 @@
 def row_lse(s_ref, shift_ref, max_ref, sum_ref, out_ref):
     rows, cols = s_ref.shape
     tiles = cols // LANES
-
-    def group_step(g, carry):
+    last = rows // GROUP - 1
+
+    def terms_of(g):
         r = pl.ds(g * GROUP, GROUP)
         terms = [s_ref[r, lane(k)] - shift_ref[k : k + 1, :] for k in range(tiles)]
-        largest = tree(terms, jnp.maximum)
+        return tuple(terms), tree(terms, jnp.maximum)
+
+    def group_step(g, carry):
+        terms, largest = carry
+        r = pl.ds(g * GROUP, GROUP)
         max_ref[r, :] = largest
         sum_ref[r, :] = tree([jnp.exp2(t - largest) for t in terms], jnp.add)
-        return carry
-
-    lax.fori_loop(0, rows // GROUP, group_step, 0)
+        return terms_of(jnp.minimum(g + 1, last))
+
+    lax.fori_loop(0, rows // GROUP, group_step, terms_of(0))
     for block in range(rows // LANES):
         b = pl.ds(block * LANES, LANES)
         maxes = max_ref[b, :].T
@@ -97,46 +101,53 @@
     width, chunks = col_blocking(cols)
     per_step = math.gcd(rows // GROUP, 8)
     steps = rows // (GROUP * per_step)
-
-    def chunk_step(c, carry):
-        def terms_of(step, q):
-            r = pl.ds(step * (GROUP * per_step) + q * GROUP, GROUP)
-            shift = shift_ref[r, :]
-            return [
-                s_ref[r, pl.ds(c * (width * LANES) + k * LANES, LANES)] - shift
-                for k in range(width)
-            ]
-
-        def max_step(step, maxes):
+    low = jnp.full((GROUP, LANES), -jnp.inf, jnp.float32)
+    zero = jnp.zeros((GROUP, LANES), jnp.float32)
+    largest = None
+    for chunk in range(chunks + 1):
+        summing, taking = chunk > 0, chunk < chunks
+
+        def step(i, carry):
+            sums, maxes = carry
             for q in range(per_step):
-                terms = terms_of(step, q)
-                maxes = tuple(jnp.maximum(m, t) for m, t in zip(maxes, terms))
-            return maxes
-
-        low = jnp.full((GROUP, LANES), -jnp.inf, jnp.float32)
-        maxes = lax.fori_loop(0, steps, max_step, (low,) * width)
-
-        def sum_step(step, sums):
-            for q in range(per_step):
-                terms = terms_of(step, q)
-                sums = tuple(s + jnp.exp2(t - m) for s, t, m in zip(sums, terms, maxes))
-            return sums
-
-        zero = jnp.zeros((GROUP, LANES), jnp.float32)
-        sums = lax.fori_loop(0, steps, sum_step, (zero,) * width)
-        for k in range(width):
-            largest = jnp.max(maxes[k], axis=0, keepdims=True)
-            total = jnp.sum(sums[k] * jnp.exp2(maxes[k] - largest), axis=0, keepdims=True)
-            col_ref[pl.ds(c * width + k, 1), :] = largest + jnp.log2(total)
-        return carry
-
-    lax.fori_loop(0, chunks, chunk_step, 0)
-
-
-def first_row_kernel(fw_ref, ff_ref, sp_ref, start_ref, s_ref, out_ref, cp_ref, rhs_ref, max_ref, sum_ref):
+                r = pl.ds(i * (GROUP * per_step) + q * GROUP, GROUP)
+                shift = shift_ref[r, :]
+                if summing:
+                    terms = [s_ref[r, lane((chunk - 1) * width + k)] - shift for k in range(width)]
+                    sums = tuple(s + jnp.exp2(t - m) for s, t, m in zip(sums, terms, largest))
+                if taking:
+                    terms = [s_ref[r, lane(chunk * width + k)] - shift for k in range(width)]
+                    maxes = tuple(jnp.maximum(m, t) for m, t in zip(maxes, terms))
+            return sums, maxes
+
+        sums, maxes = lax.fori_loop(
+            0, steps, step, ((zero,) * width if summing else (), (low,) * width if taking else ())
+        )
+        for k in range(width if summing else 0):
+            most = jnp.max(largest[k], axis=0, keepdims=True)
+            total = jnp.sum(sums[k] * jnp.exp2(largest[k] - most), axis=0, keepdims=True)
+            at = (chunk - 1) * width + k
+            col_ref[at : at + 1, :] = most + jnp.log2(total)
+        largest = maxes
+
+
+def first_row_kernel(*refs):
+    count = 9
+    sources, refs = refs[:count], refs[count:]
+    s_ref, out_ref = refs[:2]
+    held, (cp_ref, max_ref, sum_ref, sems) = refs[2 : 2 + count], refs[2 + count :]
+    copies = [
+        pltpu.make_async_copy(source, target, sems.at[i])
+        for i, (source, target) in enumerate(zip(sources, held))
+    ]
+    for copy in copies:
+        copy.start()
+    fw_ref, ff_ref, sp_ref, start_ref = held[:4]
+    for copy in copies[:3]:
+        copy.wait()
     rank, cols = ff_ref.shape
     mixed = lax.dot_general(
-        sp_ref[...], fw_ref[...], (((0,), (1,)), ((), ())), precision=HIGHEST,
+        sp_ref[...], fw_ref[...], (((0,), (0,)), ((), ())), precision=HIGHEST,
         preferred_element_type=jnp.float32,
     ) * LOG2E
 
@@ -161,6 +172,8 @@
         return carry
 
     lax.fori_loop(0, cols // width, dot_step, 0)
+    for copy in copies[3:]:
+        copy.wait()
     cp_ref[...] = start_ref[...] * LOG2E
     row_lse(s_ref, cp_ref, max_ref, sum_ref, out_ref)
 
@@ -242,9 +255,10 @@
     width, chunks = col_blocking(cols)
     per_step = math.gcd(rows // GROUP, 4)
 
-    def chunk_step(c, carry):
+    for c in range(chunks):
+        first = c * width
         pots = [
-            jnp.broadcast_to(pot_ref[pl.ds(c * width + k, 1), :], (GROUP, LANES))
+            jnp.broadcast_to(pot_ref[first + k : first + k + 1, :], (GROUP, LANES))
             for k in range(width)
         ]
 
@@ -255,9 +269,8 @@
                 weight = weight_wide[r, :]
                 fresh = []
                 for k in range(width):
-                    at = pl.ds(c * (width * LANES) + k * LANES, LANES)
-                    value = jnp.exp2(s_ref[r, at] - pots[k] - log) * weight
-                    acc_out[r, at] = acc_in[r, at] + value
+                    value = jnp.exp2(s_ref[r, lane(first + k)] - pots[k] - log) * weight
+                    acc_out[r, lane(first + k)] = acc_in[r, lane(first + k)] + value
                     fresh.append(totals[k] + value)
                 totals = tuple(fresh)
             return totals
@@ -265,10 +278,7 @@
         zero = jnp.zeros((GROUP, LANES), jnp.float32)
         totals = lax.fori_loop(0, rows // (GROUP * per_step), row_step, (zero,) * width)
         for k in range(width):
-            col_ref[pl.ds(c * width + k, 1), :] = jnp.sum(totals[k], axis=0, keepdims=True)
-        return carry
-
-    lax.fori_loop(0, chunks, chunk_step, 0)
+            col_ref[first + k : first + k + 1, :] = jnp.sum(totals[k], axis=0, keepdims=True)
 
 
 def row_adjoint_kernel_of(parts, last):
@@ -324,7 +334,7 @@
     grad = lax.fori_loop(0, cols // width, dot_step, jnp.zeros((rows, 2 * rank), jnp.float32))
     grad = grad + pltpu.roll(grad, rank, 1)
     both = lax.dot_general(
-        fw_ref[...], grad, (((0,), (0,)), ((), ())), precision=HIGHEST,
+        fw_ref[...], grad, (((1,), (0,)), ((), ())), precision=HIGHEST,
         preferred_element_type=jnp.float32,
     )
     half = rank // 2
@@ -360,11 +370,13 @@
     send_out = shape_of(wrk, *col_dims)
     acc_out = shape_of(rows, cols)
 
-    scores, part = call(
-        first_row_kernel, "row_first", (acc_out, row_out),
-        (feat_wrk, feat_firm, surplus, col_start),
-        (col_vec, pltpu.VMEM((LANES, LANES), jnp.float32), wide, wide),
+    inputs = (feat_wrk.T, feat_firm, surplus, col_start, row_start, row_mass, col_mass, row_cot, col_cot)
+    inputs = tuple(pltpu.with_memory_space_constraint(a, pltpu.HBM) for a in inputs)
+    scores, part, *held = call(
+        first_row_kernel, "row_first", (acc_out, row_out, *(shape_of(*a.shape) for a in inputs)), inputs,
+        (col_vec, wide, wide, pltpu.SemaphoreType.DMA((len(inputs),))), pltpu.HBM,
     )
+    feat_wrk, feat_firm, surplus, col_start, row_start, row_mass, col_mass, row_cot, col_cot = held
     row_pots, col_pots, row_logs, col_logs = [row_start], [col_start], [], []
     for t in range(ITERS):
         parts = peers_of(part, "firm")
@@ -396,12 +408,12 @@
             break
         acc, block, row_half = call(
             row_adjoint_kernel_of(len(parts), False), f"row_adj_{t}", (acc_out, send_out, row_out),
-            args, (wide, wide, col_vec), {1: 0},
+            args, (wide, wide, col_vec),
         )
         got = exchange_cols(block)
         acc, part, col_half = call(
             col_adjoint_kernel, f"col_adj_{t - 1}", (acc_out, row_out, col_out),
-            (scores, acc, got, col_half, row_pots[t], col_logs[t - 1]), (wide, wide), {1: 0},
+            (scores, acc, got, col_half, row_pots[t], col_logs[t - 1]), (wide, wide),
         )
 
     grad_rows = rank * rank // LANES

time: 179 us -> 136 us (0.76)
  Pallas kernels: 77.9 us -> 40.6 us
  local copies, waits for them, and re-layouts: 5.19 us -> 0.08 us
    pallas_call x12, Pallas kernels: 77.9 us -> 40.6 us  [call(): pl.pallas_call(kernel, name=name, out_shape=outs, in_specs=[pl.BlockSpec(...]
    unnamed x21 -> x0, local copies, waits for them, and re-layouts: 5.11 us -> none
where the time goes in v2:
time: 136 us
  blocking collectives  64.2 us (47%)
  Pallas kernels  40.6 us (30%)
  starting transfers between devices  15 us (11%)
  waiting for transfers between devices  14.2 us (10%)
    all_to_all x6, blocking collectives, exchange_cols(): return lax.all_to_all(block, 'wrk', 0, 0, tiled=True)  64.2 us
    pallas_call x12, Pallas kernels, call(): pl.pallas_call(kernel, name=name, out_shape=outs, in_specs=[pl.BlockSpec(...  40.6 us
    ppermute x21, starting transfers between devices, peers_of(): lax.ppermute(part, axis, [(i, i ^ d) for i in range(size)])  15 us
    ppermute x21, waiting for transfers between devices, peers_of(): lax.ppermute(part, axis, [(i, i ^ d) for i in range(size)])  14.2 us
  transfers between devices with their start and end apart: 21, of which 14 were waited for; matrix products, arithmetic and copies ran while one was open for 0% of the time, Pallas kernels for 0%

profile of v2, /device:TPU:0, one launch (start us, length us, event | category | flops | bytes accessed | tf_op | source)
XLA Modules:
  0.0 136.0 jit_solution(2512355453585115521)
XLA Ops:
  0.6 8.8 %row_first.1 = (f32[512,4096]{1,0:T(8,128)S(1)}, f32[4,128]{1,0:T(4,128)S(1)}, f32[64,512]{1,0:T(8,128)S(1)}, f32[64,4096]{1,0:T(8,128)S(1)}, f32[64,64]{1,0:T(8...) custom-call(f32[64,512]{1,0:T(8,128)} %bitcast.10, ...), custom_call_target="tpu_custom_call" | custom-call | tf_op jit(solution)/shard_map/row_first/pallas_call | solution.py:34
  9.4 2.5 %collective-permute-start.2 = (f32[4,128]{1,0:T(4,128)S(1)}, f32[4,128]{1,0:T(4,128)S(1)}, u32[]{:S(2)}, u32[]{:S(2)}) collective-permute-start(f32[4,128]{1,0:T(4,128)S(1)} %get-tuple-element.46.refs_1_), channel_id=1, source_target_pairs={{0,3},{1,2},{2,1},{3,0},{4,7},{5,6},{6,5},{7,4},{8,11},{9,10},{10,... | collective-permute-start | bytes 6152 | tf_op jit(solution)/shard_map/ppermute | solution.py:351
  11.9 0.6 collective-permute-start.1
  12.6 0.6 collective-permute-done.2.refs_4_
  13.2 2.3 %collective-permute-done.1.refs_3_ = f32[4,128]{1,0:T(4,128)S(1)} collective-permute-done((f32[4,128]{1,0:T(4,128)S(1)}, f32[4,128]{1,0:T(4,128)S(1)}, u32[]{:S(2)}, u32[]{:S(2)}) %collective-permute-start.1) | collective-permute-done | bytes 2080 | tf_op jit(solution)/shard_map/ppermute | solution.py:351
  15.5 2.2 %col_0.1 = (f32[8,32,128]{2,1,0:T(8,128)S(1)}, f32[4,128]{1,0:T(4,128)S(1)}, f32[4,128]{1,0:T(4,128)S(1)}) custom-call(f32[512,4096]{1,0:T(8,128)S(1)} %get-tuple-element.45.refs_0_.s_ref, f32[4,128]{1,0:T(4,128)S(1)} %get-tuple-element.46.refs_1_, f32[4,128]{1,0:T(4,128)S(1)} %collective-permute-done.refs_2_, f32[4,128]{1,0:T(4,128)S(1)} %collective-permute-done.1.refs_3_, ...), custom_call_target="tpu_custom_call" | custom-call | tf_op jit(solution)/shard_map/col_0/pallas_call | solution.py:34
  17.7 13.0 %all_to_all.30.got_ref = f32[8,32,128]{2,1,0:T(8,128)S(1)} all-to-all(f32[8,32,128]{2,1,0:T(8,128)S(1)} %get-tuple-element.49), channel_id=1, replica_groups=mesh['wrk'=8,'firm'=4] {'wrk'}, dimensions={0} | all-to-all | bytes 262144 | tf_op jit(solution)/shard_map/all_to_all | solution.py:356
  30.7 3.0 %row_1.1 = (f32[4,128]{1,0:T(4,128)S(1)}, f32[32,128]{1,0:T(8,128)S(1)}, f32[32,128]{1,0:T(8,128)S(1)}) custom-call(f32[512,4096]{1,0:T(8,128)S(1)} %get-tuple-element.45.refs_0_.s_ref, f32[8,32,128]{2,1,0:T(8,128)S(1)} %all_to_all.30.got_ref, f32[32,128]{1,0:T(8,128)S(1)} %get-tuple-element.50.old_ref.refs_7_, f32[32,128]{1,0:T(8,128)S(1)} %get-tuple-element.51.mass_ref), custom_call_target="tpu_custom_call" | custom-call | tf_op jit(solution)/shard_map/row_1/pallas_call | solution.py:34
  33.7 0.7 collective-permute-start.4
  34.4 1.1 collective-permute-start.3
  35.6 1.1 collective-permute-done.5.refs_4_
  36.7 0.7 collective-permute-done.4.refs_3_
  37.4 2.2 %col_1.1 = (f32[8,32,128]{2,1,0:T(8,128)S(1)}, f32[4,128]{1,0:T(4,128)S(1)}, f32[4,128]{1,0:T(4,128)S(1)}) custom-call(f32[512,4096]{1,0:T(8,128)S(1)} %get-tuple-element.45.refs_0_.s_ref, f32[4,128]{1,0:T(4,128)S(1)} %get-tuple-element.52.refs_1_, f32[4,128]{1,0:T(4,128)S(1)} %collective-permute-done.3.refs_2_, ...), custom_call_target="tpu_custom_call" | custom-call | tf_op jit(solution)/shard_map/col_1/pallas_call | solution.py:34
  39.6 9.7 %all_to_all.31.got_ref = f32[8,32,128]{2,1,0:T(8,128)S(1)} all-to-all(f32[8,32,128]{2,1,0:T(8,128)S(1)} %get-tuple-element.54), channel_id=1, replica_groups=mesh['wrk'=8,'firm'=4] {'wrk'}, dimensions={0} | all-to-all | bytes 262144 | tf_op jit(solution)/shard_map/all_to_all | solution.py:356
  49.4 3.0 %row_2.1 = (f32[4,128]{1,0:T(4,128)S(1)}, f32[32,128]{1,0:T(8,128)S(1)}, f32[32,128]{1,0:T(8,128)S(1)}) custom-call(f32[512,4096]{1,0:T(8,128)S(1)} %get-tuple-element.45.refs_0_.s_ref, f32[8,32,128]{2,1,0:T(8,128)S(1)} %all_to_all.31.got_ref, f32[32,128]{1,0:T(8,128)S(1)} %get-tuple-element.55.old_ref.refs_7_, f32[32,128]{1,0:T(8,128)S(1)} %get-tuple-element.51.mass_ref), custom_call_target="tpu_custom_call" | custom-call | tf_op jit(solution)/shard_map/row_2/pallas_call | solution.py:34
  52.4 1.1 collective-permute-start.7
  53.5 0.8 collective-permute-start.6
  54.3 1.1 collective-permute-done.8.refs_4_
  55.4 0.7 collective-permute-done.7.refs_3_
  56.1 2.2 %col_2.1 = (f32[8,32,128]{2,1,0:T(8,128)S(1)}, f32[4,128]{1,0:T(4,128)S(1)}, f32[4,128]{1,0:T(4,128)S(1)}) custom-call(f32[512,4096]{1,0:T(8,128)S(1)} %get-tuple-element.45.refs_0_.s_ref, f32[4,128]{1,0:T(4,128)S(1)} %get-tuple-element.56.refs_1_, f32[4,128]{1,0:T(4,128)S(1)} %collective-permute-done.6.refs_2_, ...), custom_call_target="tpu_custom_call" | custom-call | tf_op jit(solution)/shard_map/col_2/pallas_call | solution.py:34
  58.3 10.1 %all_to_all.32.got_ref = f32[8,32,128]{2,1,0:T(8,128)S(1)} all-to-all(f32[8,32,128]{2,1,0:T(8,128)S(1)} %get-tuple-element.58), channel_id=1, replica_groups=mesh['wrk'=8,'firm'=4] {'wrk'}, dimensions={0} | all-to-all | bytes 262144 | tf_op jit(solution)/shard_map/all_to_all | solution.py:356
  68.4 2.1 %col_adj_2.1 = (f32[512,4096]{1,0:T(8,128)S(1)}, f32[4,128]{1,0:T(4,128)S(1)}, f32[32,128]{1,0:T(8,128)S(1)}) custom-call(f32[512,4096]{1,0:T(8,128)S(1)} %get-tuple-element.45.refs_0_.s_ref, f32[8,32,128]{2,1,0:T(8,128)S(1)} %all_to_all.32.got_ref, f32[32,128]{1,0:T(8,128)S(1)} %get-tuple-element.59.cot_ref, f32[4,128]{1,0:T(4,128)S(1)} %get-tuple-element.60.pot_ref), custom_call_target="tpu_custom_call" | custom-call | tf_op jit(solution)/shard_map/col_adj_2/pallas_call | solution.py:34
  70.6 0.9 collective-permute-start.10
  71.4 1.0 collective-permute-start.9
  72.4 1.1 collective-permute-done.11.refs_5_
  73.6 0.7 collective-permute-done.10.refs_4_
  74.2 2.8 %row_adj_2.1 = (f32[512,4096]{1,0:T(8,128)S(1)}, f32[8,32,128]{2,1,0:T(8,128)S(1)}, f32[4,128]{1,0:T(4,128)S(1)}) custom-call(f32[512,4096]{1,0:T(8,128)S(1)} %get-tuple-element.45.refs_0_.s_ref, f32[512,4096]{1,0:T(8,128)S(1)} %get-tuple-element.61.refs_1_, f32[4,128]{1,0:T(4,128)S(1)} %get-tuple-element.62.refs_2_, ...), custom_call_target="tpu_custom_call" | custom-call | tf_op jit(solution)/shard_map/row_adj_2/pallas_call | solution.py:34
  77.0 9.9 %all_to_all.33.got_ref = f32[8,32,128]{2,1,0:T(8,128)S(1)} all-to-all(f32[8,32,128]{2,1,0:T(8,128)S(1)} %get-tuple-element.67), channel_id=1, replica_groups=mesh['wrk'=8,'firm'=4] {'wrk'}, dimensions={0} | all-to-all | bytes 262144 | tf_op jit(solution)/shard_map/all_to_all | solution.py:356
  86.9 2.3 %col_adj_1.1 = (f32[512,4096]{1,0:T(8,128)S(1)}, f32[4,128]{1,0:T(4,128)S(1)}, f32[32,128]{1,0:T(8,128)S(1)}) custom-call(f32[512,4096]{1,0:T(8,128)S(1)} %get-tuple-element.45.refs_0_.s_ref, f32[512,4096]{1,0:T(8,128)S(1)} %get-tuple-element.66.acc_in, f32[8,32,128]{2,1,0:T(8,128)S(1)} %all_to_all.33.got_ref, f32[32,128]{1,0:T(8,128)S(1)} %get-tuple-element.68.half_in, ...), custom_call_target="tpu_custom_call" | custom-call | tf_op jit(solution)/shard_map/col_adj_1/pallas_call | solution.py:34
  89.3 0.9 collective-permute-start.13
  90.2 1.0 collective-permute-start.12
  91.1 1.1 collective-permute-done.14.refs_5_
  92.3 0.7 collective-permute-done.13.refs_4_
  92.9 2.8 %row_adj_1.1 = (f32[512,4096]{1,0:T(8,128)S(1)}, f32[8,32,128]{2,1,0:T(8,128)S(1)}, f32[4,128]{1,0:T(4,128)S(1)}) custom-call(f32[512,4096]{1,0:T(8,128)S(1)} %get-tuple-element.45.refs_0_.s_ref, f32[512,4096]{1,0:T(8,128)S(1)} %get-tuple-element.70.refs_1_, f32[4,128]{1,0:T(4,128)S(1)} %get-tuple-element.71.refs_2_, ...), custom_call_target="tpu_custom_call" | custom-call | tf_op jit(solution)/shard_map/row_adj_1/pallas_call | solution.py:34
  95.7 9.9 %all_to_all.34.got_ref = f32[8,32,128]{2,1,0:T(8,128)S(1)} all-to-all(f32[8,32,128]{2,1,0:T(8,128)S(1)} %get-tuple-element.75), channel_id=1, replica_groups=mesh['wrk'=8,'firm'=4] {'wrk'}, dimensions={0} | all-to-all | bytes 262144 | tf_op jit(solution)/shard_map/all_to_all | solution.py:356
  105.6 2.3 %col_adj_0.1 = (f32[512,4096]{1,0:T(8,128)S(1)}, f32[4,128]{1,0:T(4,128)S(1)}, f32[32,128]{1,0:T(8,128)S(1)}) custom-call(f32[512,4096]{1,0:T(8,128)S(1)} %get-tuple-element.45.refs_0_.s_ref, f32[512,4096]{1,0:T(8,128)S(1)} %get-tuple-element.74.acc_in, f32[8,32,128]{2,1,0:T(8,128)S(1)} %all_to_all.34.got_ref, f32[32,128]{1,0:T(8,128)S(1)} %get-tuple-element.76.half_in, ...), custom_call_target="tpu_custom_call" | custom-call | tf_op jit(solution)/shard_map/col_adj_0/pallas_call | solution.py:34
  108.0 0.9 collective-permute-start.16
  108.9 1.0 collective-permute-start.15
  109.9 1.1 collective-permute-done.17.refs_5_
  111.0 0.7 collective-permute-done.16.refs_4_
  111.7 7.0 %row_adj_0.1 = (f32[8,64,128]{2,1,0:T(8,128)S(1)}, f32[4,128]{1,0:T(4,128)}) custom-call(f32[512,4096]{1,0:T(8,128)S(1)} %get-tuple-element.45.refs_0_.s_ref, f32[512,4096]{1,0:T(8,128)S(1)} %get-tuple-element.78.refs_1_, f32[4,128]{1,0:T(4,128)S(1)} %get-tuple-element.79.refs_2_, f32[4,128]{1,0:T(4,128)S(1)} %collective-permute-done.15.refs_3_, ...), custom_call_target="tpu_custom_call" | custom-call | tf_op jit(solution)/shard_map/row_adj_0/pallas_call | solution.py:34
  118.7 11.5 %all_to_all.35 = f32[8,64,128]{2,1,0:T(8,128)S(1)} all-to-all(f32[8,64,128]{2,1,0:T(8,128)S(1)} %get-tuple-element.84), channel_id=1, replica_groups=mesh['wrk'=8,'firm'=4] {'wrk'}, dimensions={0} | all-to-all | bytes 524288 | tf_op jit(solution)/shard_map/all_to_all | solution.py:356
  130.2 1.3 collective-permute-start.19
  131.5 0.9 collective-permute-start.18
  132.4 1.6 %collective-permute-done.19 = f32[32,128]{1,0:T(8,128)S(1)} collective-permute-done((f32[32,128]{1,0:T(8,128)S(1)}, f32[32,128]{1,0:T(8,128)S(1)}, u32[]{:S(2)}, u32[]{:S(2)}) %collective-permute-start.19) | collective-permute-done | bytes 16416 | tf_op jit(solution)/shard_map/ppermute | solution.py:351
  134.0 0.7 collective-permute-done.20
  134.7 0.6 fusion
  135.4 0.6 pad_maximum_fusion
  (17 shorter events, 0.5 us)
Async XLA Ops:
  9.4 3.8 %collective-permute-start.2 = (f32[4,128]{1,0:T(4,128)S(1)}, f32[4,128]{1,0:T(4,128)S(1)}, u32[]{:S(2)}, u32[]{:S(2)}) collective-permute-start(f32[4,128]{1,0:T(4,128)S(1)} %get-tuple-element.46.refs_1_), channel_id=1, source_target_pairs={{0,3},{1,2},{2,1},{3,0},{4,7},{5,6},{6,5},{7,4},{8,11},{9,10},{10,... | collective-permute-start | bytes 6152 | tf_op jit(solution)/shard_map/ppermute | solution.py:351
  11.9 3.6 %collective-permute-start.1 = (f32[4,128]{1,0:T(4,128)S(1)}, f32[4,128]{1,0:T(4,128)S(1)}, u32[]{:S(2)}, u32[]{:S(2)}) collective-permute-start(f32[4,128]{1,0:T(4,128)S(1)} %get-tuple-element.46.refs_1_), channel_id=1, source_target_pairs={{0,2},{1,3},{2,0},{3,1},{4,6},{5,7},{6,4},{7,5},{8,10},{9,11},{10,... | collective-permute-start | bytes 6152 | tf_op jit(solution)/shard_map/ppermute | solution.py:351
  12.5 2.9 %collective-permute-start = (f32[4,128]{1,0:T(4,128)S(1)}, f32[4,128]{1,0:T(4,128)S(1)}, u32[]{:S(2)}, u32[]{:S(2)}) collective-permute-start(f32[4,128]{1,0:T(4,128)S(1)} %get-tuple-element.46.refs_1_), channel_id=1, source_target_pairs={{0,1},{1,0},{2,3},{3,2},{4,5},{5,4},{6,7},{7,6},{8,9},{9,8},{10,11... | collective-permute-start | bytes 6152 | tf_op jit(solution)/shard_map/ppermute | solution.py:351
  33.6 3.1 %collective-permute-start.5 = (f32[4,128]{1,0:T(4,128)S(1)}, f32[4,128]{1,0:T(4,128)S(1)}, u32[]{:S(2)}, u32[]{:S(2)}) collective-permute-start(f32[4,128]{1,0:T(4,128)S(1)} %get-tuple-element.52.refs_1_), channel_id=1, source_target_pairs={{0,3},{1,2},{2,1},{3,0},{4,7},{5,6},{6,5},{7,4},{8,11},{9,10},{10,... | collective-permute-start | bytes 6152 | tf_op jit(solution)/shard_map/ppermute | solution.py:351
  33.7 3.7 %collective-permute-start.4 = (f32[4,128]{1,0:T(4,128)S(1)}, f32[4,128]{1,0:T(4,128)S(1)}, u32[]{:S(2)}, u32[]{:S(2)}) collective-permute-start(f32[4,128]{1,0:T(4,128)S(1)} %get-tuple-element.52.refs_1_), channel_id=1, source_target_pairs={{0,2},{1,3},{2,0},{3,1},{4,6},{5,7},{6,4},{7,5},{8,10},{9,11},{10,... | collective-permute-start | bytes 6152 | tf_op jit(solution)/shard_map/ppermute | solution.py:351
  34.4 2.9 %collective-permute-start.3 = (f32[4,128]{1,0:T(4,128)S(1)}, f32[4,128]{1,0:T(4,128)S(1)}, u32[]{:S(2)}, u32[]{:S(2)}) collective-permute-start(f32[4,128]{1,0:T(4,128)S(1)} %get-tuple-element.52.refs_1_), channel_id=1, source_target_pairs={{0,1},{1,0},{2,3},{3,2},{4,5},{5,4},{6,7},{7,6},{8,9},{9,8},{10,11... | collective-permute-start | bytes 6152 | tf_op jit(solution)/shard_map/ppermute | solution.py:351
  52.3 3.1 %collective-permute-start.8 = (f32[4,128]{1,0:T(4,128)S(1)}, f32[4,128]{1,0:T(4,128)S(1)}, u32[]{:S(2)}, u32[]{:S(2)}) collective-permute-start(f32[4,128]{1,0:T(4,128)S(1)} %get-tuple-element.56.refs_1_), channel_id=1, source_target_pairs={{0,3},{1,2},{2,1},{3,0},{4,7},{5,6},{6,5},{7,4},{8,11},{9,10},{10,... | collective-permute-start | bytes 6152 | tf_op jit(solution)/shard_map/ppermute | solution.py:351
  52.4 3.7 %collective-permute-start.7 = (f32[4,128]{1,0:T(4,128)S(1)}, f32[4,128]{1,0:T(4,128)S(1)}, u32[]{:S(2)}, u32[]{:S(2)}) collective-permute-start(f32[4,128]{1,0:T(4,128)S(1)} %get-tuple-element.56.refs_1_), channel_id=1, source_target_pairs={{0,2},{1,3},{2,0},{3,1},{4,6},{5,7},{6,4},{7,5},{8,10},{9,11},{10,... | collective-permute-start | bytes 6152 | tf_op jit(solution)/shard_map/ppermute | solution.py:351
  53.5 2.6 %collective-permute-start.6 = (f32[4,128]{1,0:T(4,128)S(1)}, f32[4,128]{1,0:T(4,128)S(1)}, u32[]{:S(2)}, u32[]{:S(2)}) collective-permute-start(f32[4,128]{1,0:T(4,128)S(1)} %get-tuple-element.56.refs_1_), channel_id=1, source_target_pairs={{0,1},{1,0},{2,3},{3,2},{4,5},{5,4},{6,7},{7,6},{8,9},{9,8},{10,11... | collective-permute-start | bytes 6152 | tf_op jit(solution)/shard_map/ppermute | solution.py:351
  70.5 3.1 %collective-permute-start.11 = (f32[4,128]{1,0:T(4,128)S(1)}, f32[4,128]{1,0:T(4,128)S(1)}, u32[]{:S(2)}, u32[]{:S(2)}) collective-permute-start(f32[4,128]{1,0:T(4,128)S(1)} %get-tuple-element.62.refs_2_), channel_id=1, source_target_pairs={{0,3},{1,2},{2,1},{3,0},{4,7},{5,6},{6,5},{7,4},{8,11},{9,10},{10,... | collective-permute-start | bytes 6152 | tf_op jit(solution)/shard_map/ppermute | solution.py:351
  70.6 3.7 %collective-permute-start.10 = (f32[4,128]{1,0:T(4,128)S(1)}, f32[4,128]{1,0:T(4,128)S(1)}, u32[]{:S(2)}, u32[]{:S(2)}) collective-permute-start(f32[4,128]{1,0:T(4,128)S(1)} %get-tuple-element.62.refs_2_), channel_id=1, source_target_pairs={{0,2},{1,3},{2,0},{3,1},{4,6},{5,7},{6,4},{7,5},{8,10},{9,11},{10,... | collective-permute-start | bytes 6152 | tf_op jit(solution)/shard_map/ppermute | solution.py:351
  71.4 2.8 %collective-permute-start.9 = (f32[4,128]{1,0:T(4,128)S(1)}, f32[4,128]{1,0:T(4,128)S(1)}, u32[]{:S(2)}, u32[]{:S(2)}) collective-permute-start(f32[4,128]{1,0:T(4,128)S(1)} %get-tuple-element.62.refs_2_), channel_id=1, source_target_pairs={{0,1},{1,0},{2,3},{3,2},{4,5},{5,4},{6,7},{7,6},{8,9},{9,8},{10,11... | collective-permute-start | bytes 6152 | tf_op jit(solution)/shard_map/ppermute | solution.py:351
  89.2 3.1 %collective-permute-start.14 = (f32[4,128]{1,0:T(4,128)S(1)}, f32[4,128]{1,0:T(4,128)S(1)}, u32[]{:S(2)}, u32[]{:S(2)}) collective-permute-start(f32[4,128]{1,0:T(4,128)S(1)} %get-tuple-element.71.refs_2_), channel_id=1, source_target_pairs={{0,3},{1,2},{2,1},{3,0},{4,7},{5,6},{6,5},{7,4},{8,11},{9,10},{10,... | collective-permute-start | bytes 6152 | tf_op jit(solution)/shard_map/ppermute | solution.py:351
  89.3 3.7 %collective-permute-start.13 = (f32[4,128]{1,0:T(4,128)S(1)}, f32[4,128]{1,0:T(4,128)S(1)}, u32[]{:S(2)}, u32[]{:S(2)}) collective-permute-start(f32[4,128]{1,0:T(4,128)S(1)} %get-tuple-element.71.refs_2_), channel_id=1, source_target_pairs={{0,2},{1,3},{2,0},{3,1},{4,6},{5,7},{6,4},{7,5},{8,10},{9,11},{10,... | collective-permute-start | bytes 6152 | tf_op jit(solution)/shard_map/ppermute | solution.py:351
  90.2 2.8 %collective-permute-start.12 = (f32[4,128]{1,0:T(4,128)S(1)}, f32[4,128]{1,0:T(4,128)S(1)}, u32[]{:S(2)}, u32[]{:S(2)}) collective-permute-start(f32[4,128]{1,0:T(4,128)S(1)} %get-tuple-element.71.refs_2_), channel_id=1, source_target_pairs={{0,1},{1,0},{2,3},{3,2},{4,5},{5,4},{6,7},{7,6},{8,9},{9,8},{10,11... | collective-permute-start | bytes 6152 | tf_op jit(solution)/shard_map/ppermute | solution.py:351
  107.9 3.1 %collective-permute-start.17 = (f32[4,128]{1,0:T(4,128)S(1)}, f32[4,128]{1,0:T(4,128)S(1)}, u32[]{:S(2)}, u32[]{:S(2)}) collective-permute-start(f32[4,128]{1,0:T(4,128)S(1)} %get-tuple-element.79.refs_2_), channel_id=1, source_target_pairs={{0,3},{1,2},{2,1},{3,0},{4,7},{5,6},{6,5},{7,4},{8,11},{9,10},{10,... | collective-permute-start | bytes 6152 | tf_op jit(solution)/shard_map/ppermute | solution.py:351
  108.0 3.7 %collective-permute-start.16 = (f32[4,128]{1,0:T(4,128)S(1)}, f32[4,128]{1,0:T(4,128)S(1)}, u32[]{:S(2)}, u32[]{:S(2)}) collective-permute-start(f32[4,128]{1,0:T(4,128)S(1)} %get-tuple-element.79.refs_2_), channel_id=1, source_target_pairs={{0,2},{1,3},{2,0},{3,1},{4,6},{5,7},{6,4},{7,5},{8,10},{9,11},{10,... | collective-permute-start | bytes 6152 | tf_op jit(solution)/shard_map/ppermute | solution.py:351
  108.9 2.8 %collective-permute-start.15 = (f32[4,128]{1,0:T(4,128)S(1)}, f32[4,128]{1,0:T(4,128)S(1)}, u32[]{:S(2)}, u32[]{:S(2)}) collective-permute-start(f32[4,128]{1,0:T(4,128)S(1)} %get-tuple-element.79.refs_2_), channel_id=1, source_target_pairs={{0,1},{1,0},{2,3},{3,2},{4,5},{5,4},{6,7},{7,6},{8,9},{9,8},{10,11... | collective-permute-start | bytes 6152 | tf_op jit(solution)/shard_map/ppermute | solution.py:351
  130.2 3.8 %collective-permute-start.19 = (f32[32,128]{1,0:T(8,128)S(1)}, f32[32,128]{1,0:T(8,128)S(1)}, u32[]{:S(2)}, u32[]{:S(2)}) collective-permute-start(f32[32,128]{1,0:T(8,128)S(1)} %slice.16), channel_id=1, source_target_pairs={{0,2},{1,3},{2,0},{3,1},{4,6},{5,7},{6,4},{7,5},{8,10},{9,11},{10,... | collective-permute-start | bytes 49160 | tf_op jit(solution)/shard_map/ppermute | solution.py:351
  131.5 3.2 %collective-permute-start.20 = (f32[32,128]{1,0:T(8,128)S(1)}, f32[32,128]{1,0:T(8,128)S(1)}, u32[]{:S(2)}, u32[]{:S(2)}) collective-permute-start(f32[32,128]{1,0:T(8,128)S(1)} %slice.16), channel_id=1, source_target_pairs={{0,3},{1,2},{2,1},{3,0},{4,7},{5,6},{6,5},{7,4},{8,11},{9,10},{10,... | collective-permute-start | bytes 49160 | tf_op jit(solution)/shard_map/ppermute | solution.py:351
  131.5 3.2 %collective-permute-start.18 = (f32[32,128]{1,0:T(8,128)S(1)}, f32[32,128]{1,0:T(8,128)S(1)}, u32[]{:S(2)}, u32[]{:S(2)}) collective-permute-start(f32[32,128]{1,0:T(8,128)S(1)} %slice.16), channel_id=1, source_target_pairs={{0,1},{1,0},{2,3},{3,2},{4,5},{5,4},{6,7},{7,6},{8,9},{9,8},{10,11... | collective-permute-start | bytes 49160 | tf_op jit(solution)/shard_map/ppermute | solution.py:351

commit v3 on v2

--- a/solution.py
+++ b/solution.py
@@ -42,6 +42,12 @@
     )(*args)
 
 
+def loop(count, body, init):
+    for i in range(count):
+        init = body(i, init)
+    return init
+
+
 def lane(k):
     return pl.ds(k * LANES, LANES)
 
@@ -57,25 +63,24 @@
         ref[pl.ds(block * LANES, LANES), :] = wide.T
 
 
-def row_lse(s_ref, shift_ref, max_ref, sum_ref, out_ref):
-    rows, cols = s_ref.shape
-    tiles = cols // LANES
-    last = rows // GROUP - 1
-
-    def terms_of(g):
+def row_lse_chunk(s_ref, shift_ref, max_ref, sum_ref, first, width, groups, later):
+    shifts = [wide_lane(shift_ref, first + k) for k in range(width)]
+    for g in groups:
         r = pl.ds(g * GROUP, GROUP)
-        terms = [s_ref[r, lane(k)] - shift_ref[k : k + 1, :] for k in range(tiles)]
-        return tuple(terms), tree(terms, jnp.maximum)
-
-    def group_step(g, carry):
-        terms, largest = carry
-        r = pl.ds(g * GROUP, GROUP)
+        terms = [s_ref[r, lane(first + k)] - shifts[k] for k in range(width)]
+        largest = tree(terms, jnp.maximum)
+        if later:
+            before = max_ref[r, :]
+            largest = jnp.maximum(largest, before)
+        total = tree([jnp.exp2(t - largest) for t in terms], jnp.add)
+        if later:
+            total = total + sum_ref[r, :] * jnp.exp2(before - largest)
         max_ref[r, :] = largest
-        sum_ref[r, :] = tree([jnp.exp2(t - largest) for t in terms], jnp.add)
-        return terms_of(jnp.minimum(g + 1, last))
-
-    lax.fori_loop(0, rows // GROUP, group_step, terms_of(0))
-    for block in range(rows // LANES):
+        sum_ref[r, :] = total
+
+
+def row_lse_end(max_ref, sum_ref, out_ref):
+    for block in range(max_ref.shape[0] // LANES):
         b = pl.ds(block * LANES, LANES)
         maxes = max_ref[b, :].T
         sums = sum_ref[b, :].T
@@ -84,10 +89,29 @@
         out_ref[block : block + 1, :] = largest + jnp.log2(total)
 
 
-def col_blocking(cols):
+def row_lse(s_ref, shift_ref, max_ref, sum_ref, out_ref):
+    rows, cols = s_ref.shape
+    width, chunks = col_blocking(cols, 8)
+    per_step = math.gcd(rows // GROUP, 8)
+    for chunk in range(chunks):
+
+        def step(i, carry):
+            groups = [i * per_step + q for q in range(per_step)]
+            row_lse_chunk(s_ref, shift_ref, max_ref, sum_ref, chunk * width, width, groups, chunk > 0)
+            return carry
+
+        loop(rows // (GROUP * per_step), step, 0)
+    row_lse_end(max_ref, sum_ref, out_ref)
+
+
+def col_blocking(cols, most):
     tiles = cols // LANES
-    width = math.gcd(tiles, 8)
+    width = math.gcd(tiles, most)
     return width, tiles // width
+
+
+def wide_lane(ref, k):
+    return jnp.broadcast_to(ref[k : k + 1, :], (GROUP, LANES))
 
 
 def send_all(col_ref, out_ref):
@@ -98,7 +122,7 @@
 
 def col_lse(s_ref, shift_ref, col_ref):
     rows, cols = s_ref.shape
-    width, chunks = col_blocking(cols)
+    width, chunks = col_blocking(cols, 8)
     per_step = math.gcd(rows // GROUP, 8)
     steps = rows // (GROUP * per_step)
     low = jnp.full((GROUP, LANES), -jnp.inf, jnp.float32)
@@ -120,8 +144,8 @@
                     maxes = tuple(jnp.maximum(m, t) for m, t in zip(maxes, terms))
             return sums, maxes
 
-        sums, maxes = lax.fori_loop(
-            0, steps, step, ((zero,) * width if summing else (), (low,) * width if taking else ())
+        sums, maxes = loop(
+            steps, step, ((zero,) * width if summing else (), (low,) * width if taking else ())
         )
         for k in range(width if summing else 0):
             most = jnp.max(largest[k], axis=0, keepdims=True)
@@ -135,7 +159,7 @@
     count = 9
     sources, refs = refs[:count], refs[count:]
     s_ref, out_ref = refs[:2]
-    held, (cp_ref, max_ref, sum_ref, sems) = refs[2 : 2 + count], refs[2 + count :]
+    held, (lhs_ref, cp_ref, max_ref, sum_ref, sems) = refs[2 : 2 + count], refs[2 + count :]
     copies = [
         pltpu.make_async_copy(source, target, sems.at[i])
         for i, (source, target) in enumerate(zip(sources, held))
@@ -143,8 +167,8 @@
     for copy in copies:
         copy.start()
     fw_ref, ff_ref, sp_ref, start_ref = held[:4]
-    for copy in copies[:3]:
-        copy.wait()
+    copies[0].wait()
+    copies[2].wait()
     rank, cols = ff_ref.shape
     mixed = lax.dot_general(
         sp_ref[...], fw_ref[...], (((0,), (0,)), ((), ())), precision=HIGHEST,
@@ -159,23 +183,31 @@
         return first, second, third
 
     m1, m2, m3 = split(mixed)
-    lhs = jnp.concatenate([m1, m2, m1, m2, m3, m1], axis=0)
+    stacked = jnp.concatenate([m.astype(jnp.float32) for m in (m1, m2, m1, m2, m3, m1)], axis=0)
+    lhs_ref[...] = stacked.T.astype(jnp.bfloat16)
+    copies[1].wait()
     width = math.gcd(cols, 512)
-
-    def dot_step(c, carry):
+    copies[3].wait()
+    cp_ref[...] = start_ref[...] * LOG2E
+
+    def dot_step(c):
         chunk = pl.ds(c * width, width)
         f1, f2, f3 = split(ff_ref[:, chunk])
         rhs = jnp.concatenate([f1, f1, f2, f2, f1, f3], axis=0)
         s_ref[:, chunk] = lax.dot_general(
-            lhs, rhs, (((0,), (0,)), ((), ())), preferred_element_type=jnp.float32
-        )
-        return carry
-
-    lax.fori_loop(0, cols // width, dot_step, 0)
-    for copy in copies[3:]:
+            lhs_ref[...], rhs, (((1,), (0,)), ((), ())), preferred_element_type=jnp.float32
+        )
+
+    tiles = width // LANES
+    rows = s_ref.shape[0]
+    for c in range(cols // width + 1):
+        if c < cols // width:
+            dot_step(c)
+        if c:
+            row_lse_chunk(s_ref, cp_ref, max_ref, sum_ref, (c - 1) * tiles, tiles, range(rows // GROUP), c > 1)
+    row_lse_end(max_ref, sum_ref, out_ref)
+    for copy in copies[4:]:
         copy.wait()
-    cp_ref[...] = start_ref[...] * LOG2E
-    row_lse(s_ref, cp_ref, max_ref, sum_ref, out_ref)
 
 
 def damped(old, log, mass):
@@ -211,26 +243,22 @@
 
 def col_adjoint_pass(s_ref, wide_ref, log_ref, weight_ref, total_ref, acc_in, acc_out, out_ref):
     rows, cols = s_ref.shape
-    tiles = cols // LANES
-    per_step = math.gcd(rows // GROUP, 4)
-
-    def group_step(g, carry):
-        rs = [pl.ds(g * (GROUP * per_step) + q * GROUP, GROUP) for q in range(per_step)]
-        shifts = [wide_ref[r, :] for r in rs]
-        totals = [None] * per_step
-        for k in range(tiles):
-            log = log_ref[k : k + 1, :]
-            weight = weight_ref[k : k + 1, :]
-            for q in range(per_step):
-                value = jnp.exp2(s_ref[rs[q], lane(k)] - shifts[q] - log) * weight
-                totals[q] = value if totals[q] is None else totals[q] + value
-                kept = value if acc_in is None else acc_in[rs[q], lane(k)] + value
-                acc_out[rs[q], lane(k)] = kept
-        for q in range(per_step):
-            total_ref[rs[q], :] = totals[q]
-        return carry
-
-    lax.fori_loop(0, rows // (GROUP * per_step), group_step, 0)
+    width, chunks = col_blocking(cols, 8)
+    for c in range(chunks):
+        first = c * width
+        logs = [wide_lane(log_ref, first + k) for k in range(width)]
+        weights = [wide_lane(weight_ref, first + k) for k in range(width)]
+        for g in range(rows // GROUP):
+            r = pl.ds(g * GROUP, GROUP)
+            shift = wide_ref[r, :]
+            values = []
+            for k in range(width):
+                at = lane(first + k)
+                value = jnp.exp2(s_ref[r, at] - shift - logs[k]) * weights[k]
+                acc_out[r, at] = value if acc_in is None else acc_in[r, at] + value
+                values.append(value)
+            total = tree(values, jnp.add)
+            total_ref[r, :] = total_ref[r, :] + total if c else total
     for block in range(rows // LANES):
         part = total_ref[pl.ds(block * LANES, LANES), :].T
         out_ref[block : block + 1, :] = jnp.sum(part, axis=0, keepdims=True)
@@ -252,15 +280,12 @@
 
 def row_adjoint_pass(s_ref, pot_ref, log_wide, weight_wide, acc_in, acc_out, col_ref):
     rows, cols = s_ref.shape
-    width, chunks = col_blocking(cols)
-    per_step = math.gcd(rows // GROUP, 4)
+    width, chunks = col_blocking(cols, 8)
+    per_step = math.gcd(rows // GROUP, 8)
 
     for c in range(chunks):
         first = c * width
-        pots = [
-            jnp.broadcast_to(pot_ref[first + k : first + k + 1, :], (GROUP, LANES))
-            for k in range(width)
-        ]
+        pots = [wide_lane(pot_ref, first + k) for k in range(width)]
 
         def row_step(step, totals):
             for q in range(per_step):
@@ -276,7 +301,7 @@
             return totals
 
         zero = jnp.zeros((GROUP, LANES), jnp.float32)
-        totals = lax.fori_loop(0, rows // (GROUP * per_step), row_step, (zero,) * width)
+        totals = loop(rows // (GROUP * per_step), row_step, (zero,) * width)
         for k in range(width):
             col_ref[first + k : first + k + 1, :] = jnp.sum(totals[k], axis=0, keepdims=True)
 
@@ -326,10 +351,11 @@
         chunk = pl.ds(c * width, width)
         f1, f2 = halves(ff_ref[:, chunk])
         rhs = jnp.concatenate([f1, f2], axis=0)
-        a1, a2 = halves(acc_ref[:, chunk])
-        dims = (((1,), (1,)), ((), ()))
-        grad = grad + lax.dot_general(a1, rhs, dims, preferred_element_type=jnp.float32)
-        return grad + lax.dot_general(a2, rhs, dims, preferred_element_type=jnp.float32)
+        lhs = jnp.concatenate(halves(acc_ref[:, chunk]), axis=1)
+        return grad + lax.dot_general(
+            lhs, jnp.concatenate([rhs, rhs], axis=1), (((1,), (1,)), ((), ())),
+            preferred_element_type=jnp.float32,
+        )
 
     grad = lax.fori_loop(0, cols // width, dot_step, jnp.zeros((rows, 2 * rank), jnp.float32))
     grad = grad + pltpu.roll(grad, rank, 1)
@@ -340,6 +366,14 @@
     half = rank // 2
     lanes = lax.broadcasted_iota(jnp.int32, (half, 2 * rank), 1)
     return jnp.where(lanes < rank, both[:half], both[half:])
+
+
+def unfold_kernel(*refs):
+    grad = tree([ref[...] for ref in refs[:-1]], jnp.add)
+    half, lanes = grad.shape
+    rank = lanes // 2
+    refs[-1][:half, :] = grad[:, :rank]
+    refs[-1][half:, :] = pltpu.roll(grad, rank, 1)[:, :rank]
 
 
 def peers_of(part, axis):
@@ -374,7 +408,11 @@
     inputs = tuple(pltpu.with_memory_space_constraint(a, pltpu.HBM) for a in inputs)
     scores, part, *held = call(
         first_row_kernel, "row_first", (acc_out, row_out, *(shape_of(*a.shape) for a in inputs)), inputs,
-        (col_vec, wide, wide, pltpu.SemaphoreType.DMA((len(inputs),))), pltpu.HBM,
+        (
+            pltpu.VMEM((rows, 6 * rank), jnp.bfloat16), col_vec, wide, wide,
+            pltpu.SemaphoreType.DMA((len(inputs),)),
+        ),
+        pltpu.HBM,
     )
     feat_wrk, feat_firm, surplus, col_start, row_start, row_mass, col_mass, row_cot, col_cot = held
     row_pots, col_pots, row_logs, col_logs = [row_start], [col_start], [], []
@@ -424,10 +462,12 @@
         (pltpu.VMEM((rows, cols), jnp.float32), wide, wide, col_vec, col_vec),
     )
     summed = jnp.sum(exchange_cols(block), axis=0)
-    col_bar = col_half - summed[: col_dims[0]]
-    grad = tree(peers_of(summed[col_dims[0] :], "firm"), jnp.add)
-    grad_surplus = jnp.concatenate([grad[:, :rank], grad[:, rank:]], axis=0)
-    return (grad_surplus, row_half.reshape(rows), col_bar.reshape(cols))
+    col_bar = (col_half - summed[: col_dims[0]]).reshape(cols)
+    summed = summed[col_dims[0] :]
+    grad_surplus = call(
+        unfold_kernel, "unfold", shape_of(rank, rank), peers_of(summed, "firm")
+    )
+    return (grad_surplus, row_half.reshape(rows), col_bar)
 
 
 def solution(mesh):

time: 136 us -> 126 us (0.926)
  Pallas kernels: 40.6 us -> 32.1 us
    pallas_call x12 -> x13, Pallas kernels: 40.6 us -> 32.1 us  [call(): pl.pallas_call(kernel, name=name, out_shape=outs, in_specs=[pl.BlockSpec(...]
where the time goes in v3:
time: 126 us
  blocking collectives  64.3 us (51%)
  Pallas kernels  32.1 us (25%)
  starting transfers between devices  14.6 us (12%)
  waiting for transfers between devices  13.8 us (11%)
    all_to_all x6, blocking collectives, exchange_cols(): return lax.all_to_all(block, 'wrk', 0, 0, tiled=True)  64.3 us
    pallas_call x13, Pallas kernels, call(): pl.pallas_call(kernel, name=name, out_shape=outs, in_specs=[pl.BlockSpec(...  32.1 us
    ppermute x21, starting transfers between devices, peers_of(): lax.ppermute(part, axis, [(i, i ^ d) for i in range(size)])  14.6 us
    ppermute x21, waiting for transfers between devices, peers_of(): lax.ppermute(part, axis, [(i, i ^ d) for i in range(size)])  13.8 us
  transfers between devices with their start and end apart: 21, of which 14 were waited for; matrix products, arithmetic and copies ran while one was open for 0% of the time, Pallas kernels for 0%

profile of v3, /device:TPU:0, one launch (start us, length us, event | category | flops | bytes accessed | tf_op | source)
XLA Modules:
  0.0 126.1 jit_solution(16639944264699218255)
XLA Ops:
  0.6 5.1 %row_first.1 = (f32[512,4096]{1,0:T(8,128)S(1)}, f32[4,128]{1,0:T(4,128)S(1)}, f32[64,512]{1,0:T(8,128)S(1)}, f32[64,4096]{1,0:T(8,128)S(1)}, f32[64,64]{1,0:T(8...) custom-call(f32[64,512]{1,0:T(8,128)} %bitcast.10, ...), custom_call_target="tpu_custom_call" | custom-call | tf_op jit(solution)/shard_map/row_first/pallas_call | solution.py:34
  5.8 2.5 %collective-permute-start.2 = (f32[4,128]{1,0:T(4,128)S(1)}, f32[4,128]{1,0:T(4,128)S(1)}, u32[]{:S(2)}, u32[]{:S(2)}) collective-permute-start(f32[4,128]{1,0:T(4,128)S(1)} %get-tuple-element.46.refs_1_), channel_id=1, source_target_pairs={{0,3},{1,2},{2,1},{3,0},{4,7},{5,6},{6,5},{7,4},{8,11},{9,10},{10,... | collective-permute-start | bytes 6152 | tf_op jit(solution)/shard_map/ppermute | solution.py:385
  8.2 0.6 collective-permute-start.1
  8.9 0.6 collective-permute-done.2.refs_4_
  9.5 2.3 %collective-permute-done.1.refs_3_ = f32[4,128]{1,0:T(4,128)S(1)} collective-permute-done((f32[4,128]{1,0:T(4,128)S(1)}, f32[4,128]{1,0:T(4,128)S(1)}, u32[]{:S(2)}, u32[]{:S(2)}) %collective-permute-start.1) | collective-permute-done | bytes 2080 | tf_op jit(solution)/shard_map/ppermute | solution.py:385
  11.8 1.9 %col_0.1 = (f32[8,32,128]{2,1,0:T(8,128)S(1)}, f32[4,128]{1,0:T(4,128)S(1)}, f32[4,128]{1,0:T(4,128)S(1)}) custom-call(f32[512,4096]{1,0:T(8,128)S(1)} %get-tuple-element.45.refs_0_.s_ref, f32[4,128]{1,0:T(4,128)S(1)} %get-tuple-element.46.refs_1_, f32[4,128]{1,0:T(4,128)S(1)} %collective-permute-done.refs_2_, f32[4,128]{1,0:T(4,128)S(1)} %collective-permute-done.1.refs_3_, ...), custom_call_target="tpu_custom_call" | custom-call | tf_op jit(solution)/shard_map/col_0/pallas_call | solution.py:34
  13.7 13.0 %all_to_all.30.got_ref = f32[8,32,128]{2,1,0:T(8,128)S(1)} all-to-all(f32[8,32,128]{2,1,0:T(8,128)S(1)} %get-tuple-element.49), channel_id=1, replica_groups=mesh['wrk'=8,'firm'=4] {'wrk'}, dimensions={0} | all-to-all | bytes 262144 | tf_op jit(solution)/shard_map/all_to_all | solution.py:390
  26.7 1.9 %row_1.1 = (f32[4,128]{1,0:T(4,128)S(1)}, f32[32,128]{1,0:T(8,128)S(1)}, f32[32,128]{1,0:T(8,128)S(1)}) custom-call(f32[512,4096]{1,0:T(8,128)S(1)} %get-tuple-element.45.refs_0_.s_ref, f32[8,32,128]{2,1,0:T(8,128)S(1)} %all_to_all.30.got_ref, f32[32,128]{1,0:T(8,128)S(1)} %get-tuple-element.50.old_ref.refs_7_, f32[32,128]{1,0:T(8,128)S(1)} %get-tuple-element.51.mass_ref), custom_call_target="tpu_custom_call" | custom-call | tf_op jit(solution)/shard_map/row_1/pallas_call | solution.py:34
  28.7 0.7 collective-permute-start.4
  29.4 1.1 collective-permute-start.3
  30.5 1.1 collective-permute-done.5.refs_4_
  31.7 0.7 collective-permute-done.4.refs_3_
  32.3 1.9 %col_1.1 = (f32[8,32,128]{2,1,0:T(8,128)S(1)}, f32[4,128]{1,0:T(4,128)S(1)}, f32[4,128]{1,0:T(4,128)S(1)}) custom-call(f32[512,4096]{1,0:T(8,128)S(1)} %get-tuple-element.45.refs_0_.s_ref, f32[4,128]{1,0:T(4,128)S(1)} %get-tuple-element.52.refs_1_, f32[4,128]{1,0:T(4,128)S(1)} %collective-permute-done.3.refs_2_, ...), custom_call_target="tpu_custom_call" | custom-call | tf_op jit(solution)/shard_map/col_1/pallas_call | solution.py:34
  34.2 9.7 %all_to_all.31.got_ref = f32[8,32,128]{2,1,0:T(8,128)S(1)} all-to-all(f32[8,32,128]{2,1,0:T(8,128)S(1)} %get-tuple-element.54), channel_id=1, replica_groups=mesh['wrk'=8,'firm'=4] {'wrk'}, dimensions={0} | all-to-all | bytes 262144 | tf_op jit(solution)/shard_map/all_to_all | solution.py:390
  43.9 1.9 %row_2.1 = (f32[4,128]{1,0:T(4,128)S(1)}, f32[32,128]{1,0:T(8,128)S(1)}, f32[32,128]{1,0:T(8,128)S(1)}) custom-call(f32[512,4096]{1,0:T(8,128)S(1)} %get-tuple-element.45.refs_0_.s_ref, f32[8,32,128]{2,1,0:T(8,128)S(1)} %all_to_all.31.got_ref, f32[32,128]{1,0:T(8,128)S(1)} %get-tuple-element.55.old_ref.refs_7_, f32[32,128]{1,0:T(8,128)S(1)} %get-tuple-element.51.mass_ref), custom_call_target="tpu_custom_call" | custom-call | tf_op jit(solution)/shard_map/row_2/pallas_call | solution.py:34
  45.9 1.1 collective-permute-start.7
  47.0 0.8 collective-permute-start.6
  47.8 1.1 collective-permute-done.8.refs_4_
  48.9 0.7 collective-permute-done.7.refs_3_
  49.6 1.9 %col_2.1 = (f32[8,32,128]{2,1,0:T(8,128)S(1)}, f32[4,128]{1,0:T(4,128)S(1)}, f32[4,128]{1,0:T(4,128)S(1)}) custom-call(f32[512,4096]{1,0:T(8,128)S(1)} %get-tuple-element.45.refs_0_.s_ref, f32[4,128]{1,0:T(4,128)S(1)} %get-tuple-element.56.refs_1_, f32[4,128]{1,0:T(4,128)S(1)} %collective-permute-done.6.refs_2_, ...), custom_call_target="tpu_custom_call" | custom-call | tf_op jit(solution)/shard_map/col_2/pallas_call | solution.py:34
  51.5 10.2 %all_to_all.32.got_ref = f32[8,32,128]{2,1,0:T(8,128)S(1)} all-to-all(f32[8,32,128]{2,1,0:T(8,128)S(1)} %get-tuple-element.58), channel_id=1, replica_groups=mesh['wrk'=8,'firm'=4] {'wrk'}, dimensions={0} | all-to-all | bytes 262144 | tf_op jit(solution)/shard_map/all_to_all | solution.py:390
  61.7 1.6 %col_adj_2.1 = (f32[512,4096]{1,0:T(8,128)S(1)}, f32[4,128]{1,0:T(4,128)S(1)}, f32[32,128]{1,0:T(8,128)S(1)}) custom-call(f32[512,4096]{1,0:T(8,128)S(1)} %get-tuple-element.45.refs_0_.s_ref, f32[8,32,128]{2,1,0:T(8,128)S(1)} %all_to_all.32.got_ref, f32[32,128]{1,0:T(8,128)S(1)} %get-tuple-element.59.cot_ref, f32[4,128]{1,0:T(4,128)S(1)} %get-tuple-element.60.pot_ref), custom_call_target="tpu_custom_call" | custom-call | tf_op jit(solution)/shard_map/col_adj_2/pallas_call | solution.py:34
  63.4 0.8 collective-permute-start.10
  64.1 1.1 collective-permute-start.9
  65.2 1.1 collective-permute-done.11.refs_5_
  66.4 0.7 collective-permute-done.10.refs_4_
  67.0 1.9 %row_adj_2.1 = (f32[512,4096]{1,0:T(8,128)S(1)}, f32[8,32,128]{2,1,0:T(8,128)S(1)}, f32[4,128]{1,0:T(4,128)S(1)}) custom-call(f32[512,4096]{1,0:T(8,128)S(1)} %get-tuple-element.45.refs_0_.s_ref, f32[512,4096]{1,0:T(8,128)S(1)} %get-tuple-element.61.refs_1_, f32[4,128]{1,0:T(4,128)S(1)} %get-tuple-element.62.refs_2_, ...), custom_call_target="tpu_custom_call" | custom-call | tf_op jit(solution)/shard_map/row_adj_2/pallas_call | solution.py:34
  68.9 9.8 %all_to_all.33.got_ref = f32[8,32,128]{2,1,0:T(8,128)S(1)} all-to-all(f32[8,32,128]{2,1,0:T(8,128)S(1)} %get-tuple-element.67), channel_id=1, replica_groups=mesh['wrk'=8,'firm'=4] {'wrk'}, dimensions={0} | all-to-all | bytes 262144 | tf_op jit(solution)/shard_map/all_to_all | solution.py:390
  78.8 2.5 %col_adj_1.1 = (f32[512,4096]{1,0:T(8,128)S(1)}, f32[4,128]{1,0:T(4,128)S(1)}, f32[32,128]{1,0:T(8,128)S(1)}) custom-call(f32[512,4096]{1,0:T(8,128)S(1)} %get-tuple-element.45.refs_0_.s_ref, f32[512,4096]{1,0:T(8,128)S(1)} %get-tuple-element.66.acc_in, f32[8,32,128]{2,1,0:T(8,128)S(1)} %all_to_all.33.got_ref, f32[32,128]{1,0:T(8,128)S(1)} %get-tuple-element.68.half_in, ...), custom_call_target="tpu_custom_call" | custom-call | tf_op jit(solution)/shard_map/col_adj_1/pallas_call | solution.py:34
  81.4 1.0 collective-permute-start.13
  82.3 0.9 collective-permute-start.12
  83.2 1.1 collective-permute-done.14.refs_5_
  84.4 0.7 collective-permute-done.13.refs_4_
  85.0 1.9 %row_adj_1.1 = (f32[512,4096]{1,0:T(8,128)S(1)}, f32[8,32,128]{2,1,0:T(8,128)S(1)}, f32[4,128]{1,0:T(4,128)S(1)}) custom-call(f32[512,4096]{1,0:T(8,128)S(1)} %get-tuple-element.45.refs_0_.s_ref, f32[512,4096]{1,0:T(8,128)S(1)} %get-tuple-element.70.refs_1_, f32[4,128]{1,0:T(4,128)S(1)} %get-tuple-element.71.refs_2_, ...), custom_call_target="tpu_custom_call" | custom-call | tf_op jit(solution)/shard_map/row_adj_1/pallas_call | solution.py:34
  87.0 10.0 %all_to_all.34.got_ref = f32[8,32,128]{2,1,0:T(8,128)S(1)} all-to-all(f32[8,32,128]{2,1,0:T(8,128)S(1)} %get-tuple-element.75), channel_id=1, replica_groups=mesh['wrk'=8,'firm'=4] {'wrk'}, dimensions={0} | all-to-all | bytes 262144 | tf_op jit(solution)/shard_map/all_to_all | solution.py:390
  97.0 2.6 %col_adj_0.1 = (f32[512,4096]{1,0:T(8,128)S(1)}, f32[4,128]{1,0:T(4,128)S(1)}, f32[32,128]{1,0:T(8,128)S(1)}) custom-call(f32[512,4096]{1,0:T(8,128)S(1)} %get-tuple-element.45.refs_0_.s_ref, f32[512,4096]{1,0:T(8,128)S(1)} %get-tuple-element.74.acc_in, f32[8,32,128]{2,1,0:T(8,128)S(1)} %all_to_all.34.got_ref, f32[32,128]{1,0:T(8,128)S(1)} %get-tuple-element.76.half_in, ...), custom_call_target="tpu_custom_call" | custom-call | tf_op jit(solution)/shard_map/col_adj_0/pallas_call | solution.py:34
  99.6 0.9 collective-permute-start.16
  100.5 1.0 collective-permute-start.15
  101.5 1.1 collective-permute-done.17.refs_5_
  102.6 0.7 collective-permute-done.16.refs_4_
  103.3 6.3 %row_adj_0.1 = (f32[8,64,128]{2,1,0:T(8,128)S(1)}, f32[4,128]{1,0:T(4,128)}) custom-call(f32[512,4096]{1,0:T(8,128)S(1)} %get-tuple-element.45.refs_0_.s_ref, f32[512,4096]{1,0:T(8,128)S(1)} %get-tuple-element.78.refs_1_, f32[4,128]{1,0:T(4,128)S(1)} %get-tuple-element.79.refs_2_, f32[4,128]{1,0:T(4,128)S(1)} %collective-permute-done.15.refs_3_, ...), custom_call_target="tpu_custom_call" | custom-call | tf_op jit(solution)/shard_map/row_adj_0/pallas_call | solution.py:34
  109.6 11.5 %all_to_all.35 = f32[8,64,128]{2,1,0:T(8,128)S(1)} all-to-all(f32[8,64,128]{2,1,0:T(8,128)S(1)} %get-tuple-element.84), channel_id=1, replica_groups=mesh['wrk'=8,'firm'=4] {'wrk'}, dimensions={0} | all-to-all | bytes 524288 | tf_op jit(solution)/shard_map/all_to_all | solution.py:390
  121.1 0.6 fusion
  121.7 1.2 collective-permute-start.19
  122.9 0.6 collective-permute-start.18
  123.6 1.3 %collective-permute-done.20.refs_3_ = f32[32,128]{1,0:T(8,128)S(1)} collective-permute-done((f32[32,128]{1,0:T(8,128)S(1)}, f32[32,128]{1,0:T(8,128)S(1)}, u32[]{:S(2)}, u32[]{:S(2)}) %collective-permute-start.20) | collective-permute-done | bytes 16416 | tf_op jit(solution)/shard_map/ppermute | solution.py:385
  124.9 0.6 collective-permute-done.19.refs_2_
  125.4 0.7 unfold.1
  (15 shorter events, 0.4 us)
Async XLA Ops:
  5.8 3.8 %collective-permute-start.2 = (f32[4,128]{1,0:T(4,128)S(1)}, f32[4,128]{1,0:T(4,128)S(1)}, u32[]{:S(2)}, u32[]{:S(2)}) collective-permute-start(f32[4,128]{1,0:T(4,128)S(1)} %get-tuple-element.46.refs_1_), channel_id=1, source_target_pairs={{0,3},{1,2},{2,1},{3,0},{4,7},{5,6},{6,5},{7,4},{8,11},{9,10},{10,... | collective-permute-start | bytes 6152 | tf_op jit(solution)/shard_map/ppermute | solution.py:385
  8.2 3.6 %collective-permute-start.1 = (f32[4,128]{1,0:T(4,128)S(1)}, f32[4,128]{1,0:T(4,128)S(1)}, u32[]{:S(2)}, u32[]{:S(2)}) collective-permute-start(f32[4,128]{1,0:T(4,128)S(1)} %get-tuple-element.46.refs_1_), channel_id=1, source_target_pairs={{0,2},{1,3},{2,0},{3,1},{4,6},{5,7},{6,4},{7,5},{8,10},{9,11},{10,... | collective-permute-start | bytes 6152 | tf_op jit(solution)/shard_map/ppermute | solution.py:385
  8.9 3.0 %collective-permute-start = (f32[4,128]{1,0:T(4,128)S(1)}, f32[4,128]{1,0:T(4,128)S(1)}, u32[]{:S(2)}, u32[]{:S(2)}) collective-permute-start(f32[4,128]{1,0:T(4,128)S(1)} %get-tuple-element.46.refs_1_), channel_id=1, source_target_pairs={{0,1},{1,0},{2,3},{3,2},{4,5},{5,4},{6,7},{7,6},{8,9},{9,8},{10,11... | collective-permute-start | bytes 6152 | tf_op jit(solution)/shard_map/ppermute | solution.py:385
  28.6 3.1 %collective-permute-start.5 = (f32[4,128]{1,0:T(4,128)S(1)}, f32[4,128]{1,0:T(4,128)S(1)}, u32[]{:S(2)}, u32[]{:S(2)}) collective-permute-start(f32[4,128]{1,0:T(4,128)S(1)} %get-tuple-element.52.refs_1_), channel_id=1, source_target_pairs={{0,3},{1,2},{2,1},{3,0},{4,7},{5,6},{6,5},{7,4},{8,11},{9,10},{10,... | collective-permute-start | bytes 6152 | tf_op jit(solution)/shard_map/ppermute | solution.py:385
  28.7 3.7 %collective-permute-start.4 = (f32[4,128]{1,0:T(4,128)S(1)}, f32[4,128]{1,0:T(4,128)S(1)}, u32[]{:S(2)}, u32[]{:S(2)}) collective-permute-start(f32[4,128]{1,0:T(4,128)S(1)} %get-tuple-element.52.refs_1_), channel_id=1, source_target_pairs={{0,2},{1,3},{2,0},{3,1},{4,6},{5,7},{6,4},{7,5},{8,10},{9,11},{10,... | collective-permute-start | bytes 6152 | tf_op jit(solution)/shard_map/ppermute | solution.py:385
  29.4 2.9 %collective-permute-start.3 = (f32[4,128]{1,0:T(4,128)S(1)}, f32[4,128]{1,0:T(4,128)S(1)}, u32[]{:S(2)}, u32[]{:S(2)}) collective-permute-start(f32[4,128]{1,0:T(4,128)S(1)} %get-tuple-element.52.refs_1_), channel_id=1, source_target_pairs={{0,1},{1,0},{2,3},{3,2},{4,5},{5,4},{6,7},{7,6},{8,9},{9,8},{10,11... | collective-permute-start | bytes 6152 | tf_op jit(solution)/shard_map/ppermute | solution.py:385
  45.9 3.1 %collective-permute-start.8 = (f32[4,128]{1,0:T(4,128)S(1)}, f32[4,128]{1,0:T(4,128)S(1)}, u32[]{:S(2)}, u32[]{:S(2)}) collective-permute-start(f32[4,128]{1,0:T(4,128)S(1)} %get-tuple-element.56.refs_1_), channel_id=1, source_target_pairs={{0,3},{1,2},{2,1},{3,0},{4,7},{5,6},{6,5},{7,4},{8,11},{9,10},{10,... | collective-permute-start | bytes 6152 | tf_op jit(solution)/shard_map/ppermute | solution.py:385
  45.9 3.7 %collective-permute-start.7 = (f32[4,128]{1,0:T(4,128)S(1)}, f32[4,128]{1,0:T(4,128)S(1)}, u32[]{:S(2)}, u32[]{:S(2)}) collective-permute-start(f32[4,128]{1,0:T(4,128)S(1)} %get-tuple-element.56.refs_1_), channel_id=1, source_target_pairs={{0,2},{1,3},{2,0},{3,1},{4,6},{5,7},{6,4},{7,5},{8,10},{9,11},{10,... | collective-permute-start | bytes 6152 | tf_op jit(solution)/shard_map/ppermute | solution.py:385
  47.0 2.6 %collective-permute-start.6 = (f32[4,128]{1,0:T(4,128)S(1)}, f32[4,128]{1,0:T(4,128)S(1)}, u32[]{:S(2)}, u32[]{:S(2)}) collective-permute-start(f32[4,128]{1,0:T(4,128)S(1)} %get-tuple-element.56.refs_1_), channel_id=1, source_target_pairs={{0,1},{1,0},{2,3},{3,2},{4,5},{5,4},{6,7},{7,6},{8,9},{9,8},{10,11... | collective-permute-start | bytes 6152 | tf_op jit(solution)/shard_map/ppermute | solution.py:385
  63.3 3.1 %collective-permute-start.11 = (f32[4,128]{1,0:T(4,128)S(1)}, f32[4,128]{1,0:T(4,128)S(1)}, u32[]{:S(2)}, u32[]{:S(2)}) collective-permute-start(f32[4,128]{1,0:T(4,128)S(1)} %get-tuple-element.62.refs_2_), channel_id=1, source_target_pairs={{0,3},{1,2},{2,1},{3,0},{4,7},{5,6},{6,5},{7,4},{8,11},{9,10},{10,... | collective-permute-start | bytes 6152 | tf_op jit(solution)/shard_map/ppermute | solution.py:385
  63.4 3.7 %collective-permute-start.10 = (f32[4,128]{1,0:T(4,128)S(1)}, f32[4,128]{1,0:T(4,128)S(1)}, u32[]{:S(2)}, u32[]{:S(2)}) collective-permute-start(f32[4,128]{1,0:T(4,128)S(1)} %get-tuple-element.62.refs_2_), channel_id=1, source_target_pairs={{0,2},{1,3},{2,0},{3,1},{4,6},{5,7},{6,4},{7,5},{8,10},{9,11},{10,... | collective-permute-start | bytes 6152 | tf_op jit(solution)/shard_map/ppermute | solution.py:385
  64.1 2.9 %collective-permute-start.9 = (f32[4,128]{1,0:T(4,128)S(1)}, f32[4,128]{1,0:T(4,128)S(1)}, u32[]{:S(2)}, u32[]{:S(2)}) collective-permute-start(f32[4,128]{1,0:T(4,128)S(1)} %get-tuple-element.62.refs_2_), channel_id=1, source_target_pairs={{0,1},{1,0},{2,3},{3,2},{4,5},{5,4},{6,7},{7,6},{8,9},{9,8},{10,11... | collective-permute-start | bytes 6152 | tf_op jit(solution)/shard_map/ppermute | solution.py:385
  81.3 3.1 %collective-permute-start.14 = (f32[4,128]{1,0:T(4,128)S(1)}, f32[4,128]{1,0:T(4,128)S(1)}, u32[]{:S(2)}, u32[]{:S(2)}) collective-permute-start(f32[4,128]{1,0:T(4,128)S(1)} %get-tuple-element.71.refs_2_), channel_id=1, source_target_pairs={{0,3},{1,2},{2,1},{3,0},{4,7},{5,6},{6,5},{7,4},{8,11},{9,10},{10,... | collective-permute-start | bytes 6152 | tf_op jit(solution)/shard_map/ppermute | solution.py:385
  81.4 3.7 %collective-permute-start.13 = (f32[4,128]{1,0:T(4,128)S(1)}, f32[4,128]{1,0:T(4,128)S(1)}, u32[]{:S(2)}, u32[]{:S(2)}) collective-permute-start(f32[4,128]{1,0:T(4,128)S(1)} %get-tuple-element.71.refs_2_), channel_id=1, source_target_pairs={{0,2},{1,3},{2,0},{3,1},{4,6},{5,7},{6,4},{7,5},{8,10},{9,11},{10,... | collective-permute-start | bytes 6152 | tf_op jit(solution)/shard_map/ppermute | solution.py:385
  82.3 2.7 %collective-permute-start.12 = (f32[4,128]{1,0:T(4,128)S(1)}, f32[4,128]{1,0:T(4,128)S(1)}, u32[]{:S(2)}, u32[]{:S(2)}) collective-permute-start(f32[4,128]{1,0:T(4,128)S(1)} %get-tuple-element.71.refs_2_), channel_id=1, source_target_pairs={{0,1},{1,0},{2,3},{3,2},{4,5},{5,4},{6,7},{7,6},{8,9},{9,8},{10,11... | collective-permute-start | bytes 6152 | tf_op jit(solution)/shard_map/ppermute | solution.py:385
  99.5 3.1 %collective-permute-start.17 = (f32[4,128]{1,0:T(4,128)S(1)}, f32[4,128]{1,0:T(4,128)S(1)}, u32[]{:S(2)}, u32[]{:S(2)}) collective-permute-start(f32[4,128]{1,0:T(4,128)S(1)} %get-tuple-element.79.refs_2_), channel_id=1, source_target_pairs={{0,3},{1,2},{2,1},{3,0},{4,7},{5,6},{6,5},{7,4},{8,11},{9,10},{10,... | collective-permute-start | bytes 6152 | tf_op jit(solution)/shard_map/ppermute | solution.py:385
  99.6 3.7 %collective-permute-start.16 = (f32[4,128]{1,0:T(4,128)S(1)}, f32[4,128]{1,0:T(4,128)S(1)}, u32[]{:S(2)}, u32[]{:S(2)}) collective-permute-start(f32[4,128]{1,0:T(4,128)S(1)} %get-tuple-element.79.refs_2_), channel_id=1, source_target_pairs={{0,2},{1,3},{2,0},{3,1},{4,6},{5,7},{6,4},{7,5},{8,10},{9,11},{10,... | collective-permute-start | bytes 6152 | tf_op jit(solution)/shard_map/ppermute | solution.py:385
  100.5 2.8 %collective-permute-start.15 = (f32[4,128]{1,0:T(4,128)S(1)}, f32[4,128]{1,0:T(4,128)S(1)}, u32[]{:S(2)}, u32[]{:S(2)}) collective-permute-start(f32[4,128]{1,0:T(4,128)S(1)} %get-tuple-element.79.refs_2_), channel_id=1, source_target_pairs={{0,1},{1,0},{2,3},{3,2},{4,5},{5,4},{6,7},{7,6},{8,9},{9,8},{10,11... | collective-permute-start | bytes 6152 | tf_op jit(solution)/shard_map/ppermute | solution.py:385
  121.7 3.2 %collective-permute-start.20 = (f32[32,128]{1,0:T(8,128)S(1)}, f32[32,128]{1,0:T(8,128)S(1)}, u32[]{:S(2)}, u32[]{:S(2)}) collective-permute-start(f32[32,128]{1,0:T(8,128)S(1)} %get-tuple-element.88.refs_0_), channel_id=1, source_target_pairs={{0,3},{1,2},{2,1},{3,0},{4,7},{5,6},{6,5},{7,4},{8,11},{9,10},{10,... | collective-permute-start | bytes 49160 | tf_op jit(solution)/shard_map/ppermute | solution.py:385
  121.7 3.7 %collective-permute-start.19 = (f32[32,128]{1,0:T(8,128)S(1)}, f32[32,128]{1,0:T(8,128)S(1)}, u32[]{:S(2)}, u32[]{:S(2)}) collective-permute-start(f32[32,128]{1,0:T(8,128)S(1)} %get-tuple-element.88.refs_0_), channel_id=1, source_target_pairs={{0,2},{1,3},{2,0},{3,1},{4,6},{5,7},{6,4},{7,5},{8,10},{9,11},{10,... | collective-permute-start | bytes 49160 | tf_op jit(solution)/shard_map/ppermute | solution.py:385
  122.9 2.5 %collective-permute-start.18 = (f32[32,128]{1,0:T(8,128)S(1)}, f32[32,128]{1,0:T(8,128)S(1)}, u32[]{:S(2)}, u32[]{:S(2)}) collective-permute-start(f32[32,128]{1,0:T(8,128)S(1)} %get-tuple-element.88.refs_0_), channel_id=1, source_target_pairs={{0,1},{1,0},{2,3},{3,2},{4,5},{5,4},{6,7},{7,6},{8,9},{9,8},{10,11... | collective-permute-start | bytes 49160 | tf_op jit(solution)/shard_map/ppermute | solution.py:385

commit v4 on v3

--- a/solution.py
+++ b/solution.py
@@ -40,12 +40,6 @@
         scratch_shapes=scratch,
         compiler_params=pltpu.CompilerParams(vmem_limit_bytes=VMEM_LIMIT),
     )(*args)
-
-
-def loop(count, body, init):
-    for i in range(count):
-        init = body(i, init)
-    return init
 
 
 def lane(k):
@@ -100,7 +94,7 @@
             row_lse_chunk(s_ref, shift_ref, max_ref, sum_ref, chunk * width, width, groups, chunk > 0)
             return carry
 
-        loop(rows // (GROUP * per_step), step, 0)
+        lax.fori_loop(0, rows // (GROUP * per_step), step, 0)
     row_lse_end(max_ref, sum_ref, out_ref)
 
 
@@ -144,8 +138,8 @@
                     maxes = tuple(jnp.maximum(m, t) for m, t in zip(maxes, terms))
             return sums, maxes
 
-        sums, maxes = loop(
-            steps, step, ((zero,) * width if summing else (), (low,) * width if taking else ())
+        sums, maxes = lax.fori_loop(
+            0, steps, step, ((zero,) * width if summing else (), (low,) * width if taking else ())
         )
         for k in range(width if summing else 0):
             most = jnp.max(largest[k], axis=0, keepdims=True)
@@ -243,22 +237,26 @@
 
 def col_adjoint_pass(s_ref, wide_ref, log_ref, weight_ref, total_ref, acc_in, acc_out, out_ref):
     rows, cols = s_ref.shape
-    width, chunks = col_blocking(cols, 8)
-    for c in range(chunks):
-        first = c * width
-        logs = [wide_lane(log_ref, first + k) for k in range(width)]
-        weights = [wide_lane(weight_ref, first + k) for k in range(width)]
-        for g in range(rows // GROUP):
-            r = pl.ds(g * GROUP, GROUP)
-            shift = wide_ref[r, :]
-            values = []
-            for k in range(width):
-                at = lane(first + k)
-                value = jnp.exp2(s_ref[r, at] - shift - logs[k]) * weights[k]
-                acc_out[r, at] = value if acc_in is None else acc_in[r, at] + value
-                values.append(value)
-            total = tree(values, jnp.add)
-            total_ref[r, :] = total_ref[r, :] + total if c else total
+    tiles = cols // LANES
+    per_step = math.gcd(rows // GROUP, 4)
+
+    def group_step(g, carry):
+        rs = [pl.ds(g * (GROUP * per_step) + q * GROUP, GROUP) for q in range(per_step)]
+        shifts = [wide_ref[r, :] for r in rs]
+        totals = [None] * per_step
+        for k in range(tiles):
+            log = log_ref[k : k + 1, :]
+            weight = weight_ref[k : k + 1, :]
+            for q in range(per_step):
+                value = jnp.exp2(s_ref[rs[q], lane(k)] - shifts[q] - log) * weight
+                totals[q] = value if totals[q] is None else totals[q] + value
+                kept = value if acc_in is None else acc_in[rs[q], lane(k)] + value
+                acc_out[rs[q], lane(k)] = kept
+        for q in range(per_step):
+            total_ref[rs[q], :] = totals[q]
+        return carry
+
+    lax.fori_loop(0, rows // (GROUP * per_step), group_step, 0)
     for block in range(rows // LANES):
         part = total_ref[pl.ds(block * LANES, LANES), :].T
         out_ref[block : block + 1, :] = jnp.sum(part, axis=0, keepdims=True)
@@ -301,7 +299,7 @@
             return totals
 
         zero = jnp.zeros((GROUP, LANES), jnp.float32)
-        totals = loop(rows // (GROUP * per_step), row_step, (zero,) * width)
+        totals = lax.fori_loop(0, rows // (GROUP * per_step), row_step, (zero,) * width)
         for k in range(width):
             col_ref[first + k : first + k + 1, :] = jnp.sum(totals[k], axis=0, keepdims=True)
 
@@ -347,22 +345,25 @@
         first = value.astype(jnp.bfloat16)
         return first, (value - first.astype(jnp.float32)).astype(jnp.bfloat16)
 
+    w1, w2 = halves(fw_ref[...])
+    left = jnp.concatenate([w1, w2], axis=0)
+    left = jnp.concatenate([left, left], axis=1)
+
     def dot_step(c, grad):
         chunk = pl.ds(c * width, width)
-        f1, f2 = halves(ff_ref[:, chunk])
-        rhs = jnp.concatenate([f1, f2], axis=0)
-        lhs = jnp.concatenate(halves(acc_ref[:, chunk]), axis=1)
+        weights = jnp.concatenate(halves(acc_ref[:, chunk]), axis=0)
+        rows_done = jnp.dot(left, weights, preferred_element_type=jnp.float32)
+        rows_done = rows_done[:rank] + rows_done[rank:]
         return grad + lax.dot_general(
-            lhs, jnp.concatenate([rhs, rhs], axis=1), (((1,), (1,)), ((), ())),
-            preferred_element_type=jnp.float32,
-        )
-
-    grad = lax.fori_loop(0, cols // width, dot_step, jnp.zeros((rows, 2 * rank), jnp.float32))
-    grad = grad + pltpu.roll(grad, rank, 1)
-    both = lax.dot_general(
-        fw_ref[...], grad, (((1,), (0,)), ((), ())), precision=HIGHEST,
-        preferred_element_type=jnp.float32,
-    )
+            jnp.concatenate(halves(rows_done), axis=0),
+            jnp.concatenate(halves(ff_ref[:, chunk]), axis=0),
+            (((1,), (1,)), ((), ())), preferred_element_type=jnp.float32,
+        )
+
+    zero = jnp.zeros((2 * rank, 2 * rank), jnp.float32)
+    grad = lax.fori_loop(0, cols // width, dot_step, zero)
+    grad = grad[:rank] + grad[rank:]
+    both = grad + pltpu.roll(grad, rank, 1)
     half = rank // 2
     lanes = lax.broadcasted_iota(jnp.int32, (half, 2 * rank), 1)
     return jnp.where(lanes < rank, both[:half], both[half:])

time: 126 us -> 130 us (1.032)
  Pallas kernels: 32.1 us -> 35.9 us
    pallas_call x13, Pallas kernels: 32.1 us -> 35.9 us  [call(): pl.pallas_call(kernel, name=name, out_shape=outs, in_specs=[pl.BlockSpec(...]
where the time goes in v4:
time: 130 us
  blocking collectives  64.2 us (49%)
  Pallas kernels  35.9 us (28%)
  starting transfers between devices  14.6 us (11%)
  waiting for transfers between devices  13.8 us (11%)
    all_to_all x6, blocking collectives, exchange_cols(): return lax.all_to_all(block, 'wrk', 0, 0, tiled=True)  64.2 us
    pallas_call x13, Pallas kernels, call(): pl.pallas_call(kernel, name=name, out_shape=outs, in_specs=[pl.BlockSpec(...  35.9 us
    ppermute x21, starting transfers between devices, peers_of(): lax.ppermute(part, axis, [(i, i ^ d) for i in range(size)])  14.6 us
    ppermute x21, waiting for transfers between devices, peers_of(): lax.ppermute(part, axis, [(i, i ^ d) for i in range(size)])  13.8 us
  transfers between devices with their start and end apart: 21, of which 14 were waited for; matrix products, arithmetic and copies ran while one was open for 0% of the time, Pallas kernels for 0%

profile of v4, /device:TPU:0, one launch (start us, length us, event | category | flops | bytes accessed | tf_op | source)
XLA Modules:
  0.0 129.8 jit_solution(13336278048423894076)
XLA Ops:
  0.6 5.1 %row_first.1 = (f32[512,4096]{1,0:T(8,128)S(1)}, f32[4,128]{1,0:T(4,128)S(1)}, f32[64,512]{1,0:T(8,128)S(1)}, f32[64,4096]{1,0:T(8,128)S(1)}, f32[64,64]{1,0:T(8...) custom-call(f32[64,512]{1,0:T(8,128)} %bitcast.10, ...), custom_call_target="tpu_custom_call" | custom-call | tf_op jit(solution)/shard_map/row_first/pallas_call | solution.py:34
  5.8 2.5 %collective-permute-start.2 = (f32[4,128]{1,0:T(4,128)S(1)}, f32[4,128]{1,0:T(4,128)S(1)}, u32[]{:S(2)}, u32[]{:S(2)}) collective-permute-start(f32[4,128]{1,0:T(4,128)S(1)} %get-tuple-element.46.refs_1_), channel_id=1, source_target_pairs={{0,3},{1,2},{2,1},{3,0},{4,7},{5,6},{6,5},{7,4},{8,11},{9,10},{10,... | collective-permute-start | bytes 6152 | tf_op jit(solution)/shard_map/ppermute | solution.py:386
  8.2 0.6 collective-permute-start.1
  8.9 0.6 collective-permute-done.2.refs_4_
  9.5 2.3 %collective-permute-done.1.refs_3_ = f32[4,128]{1,0:T(4,128)S(1)} collective-permute-done((f32[4,128]{1,0:T(4,128)S(1)}, f32[4,128]{1,0:T(4,128)S(1)}, u32[]{:S(2)}, u32[]{:S(2)}) %collective-permute-start.1) | collective-permute-done | bytes 2080 | tf_op jit(solution)/shard_map/ppermute | solution.py:386
  11.8 2.2 %col_0.1 = (f32[8,32,128]{2,1,0:T(8,128)S(1)}, f32[4,128]{1,0:T(4,128)S(1)}, f32[4,128]{1,0:T(4,128)S(1)}) custom-call(f32[512,4096]{1,0:T(8,128)S(1)} %get-tuple-element.45.refs_0_.s_ref, f32[4,128]{1,0:T(4,128)S(1)} %get-tuple-element.46.refs_1_, f32[4,128]{1,0:T(4,128)S(1)} %collective-permute-done.refs_2_, f32[4,128]{1,0:T(4,128)S(1)} %collective-permute-done.1.refs_3_, ...), custom_call_target="tpu_custom_call" | custom-call | tf_op jit(solution)/shard_map/col_0/pallas_call | solution.py:34
  14.1 13.0 %all_to_all.30.got_ref = f32[8,32,128]{2,1,0:T(8,128)S(1)} all-to-all(f32[8,32,128]{2,1,0:T(8,128)S(1)} %get-tuple-element.49), channel_id=1, replica_groups=mesh['wrk'=8,'firm'=4] {'wrk'}, dimensions={0} | all-to-all | bytes 262144 | tf_op jit(solution)/shard_map/all_to_all | solution.py:391
  27.0 2.2 %row_1.1 = (f32[4,128]{1,0:T(4,128)S(1)}, f32[32,128]{1,0:T(8,128)S(1)}, f32[32,128]{1,0:T(8,128)S(1)}) custom-call(f32[512,4096]{1,0:T(8,128)S(1)} %get-tuple-element.45.refs_0_.s_ref, f32[8,32,128]{2,1,0:T(8,128)S(1)} %all_to_all.30.got_ref, f32[32,128]{1,0:T(8,128)S(1)} %get-tuple-element.50.old_ref.refs_7_, f32[32,128]{1,0:T(8,128)S(1)} %get-tuple-element.51.mass_ref), custom_call_target="tpu_custom_call" | custom-call | tf_op jit(solution)/shard_map/row_1/pallas_call | solution.py:34
  29.3 0.7 collective-permute-start.4
  30.0 1.1 collective-permute-start.3
  31.1 1.1 collective-permute-done.5.refs_4_
  32.3 0.7 collective-permute-done.4.refs_3_
  32.9 2.2 %col_1.1 = (f32[8,32,128]{2,1,0:T(8,128)S(1)}, f32[4,128]{1,0:T(4,128)S(1)}, f32[4,128]{1,0:T(4,128)S(1)}) custom-call(f32[512,4096]{1,0:T(8,128)S(1)} %get-tuple-element.45.refs_0_.s_ref, f32[4,128]{1,0:T(4,128)S(1)} %get-tuple-element.52.refs_1_, f32[4,128]{1,0:T(4,128)S(1)} %collective-permute-done.3.refs_2_, ...), custom_call_target="tpu_custom_call" | custom-call | tf_op jit(solution)/shard_map/col_1/pallas_call | solution.py:34
  35.2 9.7 %all_to_all.31.got_ref = f32[8,32,128]{2,1,0:T(8,128)S(1)} all-to-all(f32[8,32,128]{2,1,0:T(8,128)S(1)} %get-tuple-element.54), channel_id=1, replica_groups=mesh['wrk'=8,'firm'=4] {'wrk'}, dimensions={0} | all-to-all | bytes 262144 | tf_op jit(solution)/shard_map/all_to_all | solution.py:391
  44.9 2.2 %row_2.1 = (f32[4,128]{1,0:T(4,128)S(1)}, f32[32,128]{1,0:T(8,128)S(1)}, f32[32,128]{1,0:T(8,128)S(1)}) custom-call(f32[512,4096]{1,0:T(8,128)S(1)} %get-tuple-element.45.refs_0_.s_ref, f32[8,32,128]{2,1,0:T(8,128)S(1)} %all_to_all.31.got_ref, f32[32,128]{1,0:T(8,128)S(1)} %get-tuple-element.55.old_ref.refs_7_, f32[32,128]{1,0:T(8,128)S(1)} %get-tuple-element.51.mass_ref), custom_call_target="tpu_custom_call" | custom-call | tf_op jit(solution)/shard_map/row_2/pallas_call | solution.py:34
  47.2 1.1 collective-permute-start.7
  48.2 0.8 collective-permute-start.6
  49.0 1.1 collective-permute-done.8.refs_4_
  50.2 0.7 collective-permute-done.7.refs_3_
  50.8 2.2 %col_2.1 = (f32[8,32,128]{2,1,0:T(8,128)S(1)}, f32[4,128]{1,0:T(4,128)S(1)}, f32[4,128]{1,0:T(4,128)S(1)}) custom-call(f32[512,4096]{1,0:T(8,128)S(1)} %get-tuple-element.45.refs_0_.s_ref, f32[4,128]{1,0:T(4,128)S(1)} %get-tuple-element.56.refs_1_, f32[4,128]{1,0:T(4,128)S(1)} %collective-permute-done.6.refs_2_, ...), custom_call_target="tpu_custom_call" | custom-call | tf_op jit(solution)/shard_map/col_2/pallas_call | solution.py:34
  53.1 10.1 %all_to_all.32.got_ref = f32[8,32,128]{2,1,0:T(8,128)S(1)} all-to-all(f32[8,32,128]{2,1,0:T(8,128)S(1)} %get-tuple-element.58), channel_id=1, replica_groups=mesh['wrk'=8,'firm'=4] {'wrk'}, dimensions={0} | all-to-all | bytes 262144 | tf_op jit(solution)/shard_map/all_to_all | solution.py:391
  63.2 2.1 %col_adj_2.1 = (f32[512,4096]{1,0:T(8,128)S(1)}, f32[4,128]{1,0:T(4,128)S(1)}, f32[32,128]{1,0:T(8,128)S(1)}) custom-call(f32[512,4096]{1,0:T(8,128)S(1)} %get-tuple-element.45.refs_0_.s_ref, f32[8,32,128]{2,1,0:T(8,128)S(1)} %all_to_all.32.got_ref, f32[32,128]{1,0:T(8,128)S(1)} %get-tuple-element.59.cot_ref, f32[4,128]{1,0:T(4,128)S(1)} %get-tuple-element.60.pot_ref), custom_call_target="tpu_custom_call" | custom-call | tf_op jit(solution)/shard_map/col_adj_2/pallas_call | solution.py:34
  65.3 0.9 collective-permute-start.10
  66.2 1.0 collective-permute-start.9
  67.2 1.1 collective-permute-done.11.refs_5_
  68.3 0.7 collective-permute-done.10.refs_4_
  69.0 2.7 %row_adj_2.1 = (f32[512,4096]{1,0:T(8,128)S(1)}, f32[8,32,128]{2,1,0:T(8,128)S(1)}, f32[4,128]{1,0:T(4,128)S(1)}) custom-call(f32[512,4096]{1,0:T(8,128)S(1)} %get-tuple-element.45.refs_0_.s_ref, f32[512,4096]{1,0:T(8,128)S(1)} %get-tuple-element.61.refs_1_, f32[4,128]{1,0:T(4,128)S(1)} %get-tuple-element.62.refs_2_, ...), custom_call_target="tpu_custom_call" | custom-call | tf_op jit(solution)/shard_map/row_adj_2/pallas_call | solution.py:34
  71.7 9.9 %all_to_all.33.got_ref = f32[8,32,128]{2,1,0:T(8,128)S(1)} all-to-all(f32[8,32,128]{2,1,0:T(8,128)S(1)} %get-tuple-element.67), channel_id=1, replica_groups=mesh['wrk'=8,'firm'=4] {'wrk'}, dimensions={0} | all-to-all | bytes 262144 | tf_op jit(solution)/shard_map/all_to_all | solution.py:391
  81.6 2.3 %col_adj_1.1 = (f32[512,4096]{1,0:T(8,128)S(1)}, f32[4,128]{1,0:T(4,128)S(1)}, f32[32,128]{1,0:T(8,128)S(1)}) custom-call(f32[512,4096]{1,0:T(8,128)S(1)} %get-tuple-element.45.refs_0_.s_ref, f32[512,4096]{1,0:T(8,128)S(1)} %get-tuple-element.66.acc_in, f32[8,32,128]{2,1,0:T(8,128)S(1)} %all_to_all.33.got_ref, f32[32,128]{1,0:T(8,128)S(1)} %get-tuple-element.68.half_in, ...), custom_call_target="tpu_custom_call" | custom-call | tf_op jit(solution)/shard_map/col_adj_1/pallas_call | solution.py:34
  84.0 0.9 collective-permute-start.13
  84.9 1.0 collective-permute-start.12
  85.9 1.1 collective-permute-done.14.refs_5_
  87.0 0.7 collective-permute-done.13.refs_4_
  87.7 2.7 %row_adj_1.1 = (f32[512,4096]{1,0:T(8,128)S(1)}, f32[8,32,128]{2,1,0:T(8,128)S(1)}, f32[4,128]{1,0:T(4,128)S(1)}) custom-call(f32[512,4096]{1,0:T(8,128)S(1)} %get-tuple-element.45.refs_0_.s_ref, f32[512,4096]{1,0:T(8,128)S(1)} %get-tuple-element.70.refs_1_, f32[4,128]{1,0:T(4,128)S(1)} %get-tuple-element.71.refs_2_, ...), custom_call_target="tpu_custom_call" | custom-call | tf_op jit(solution)/shard_map/row_adj_1/pallas_call | solution.py:34
  90.4 9.9 %all_to_all.34.got_ref = f32[8,32,128]{2,1,0:T(8,128)S(1)} all-to-all(f32[8,32,128]{2,1,0:T(8,128)S(1)} %get-tuple-element.75), channel_id=1, replica_groups=mesh['wrk'=8,'firm'=4] {'wrk'}, dimensions={0} | all-to-all | bytes 262144 | tf_op jit(solution)/shard_map/all_to_all | solution.py:391
  100.3 2.3 %col_adj_0.1 = (f32[512,4096]{1,0:T(8,128)S(1)}, f32[4,128]{1,0:T(4,128)S(1)}, f32[32,128]{1,0:T(8,128)S(1)}) custom-call(f32[512,4096]{1,0:T(8,128)S(1)} %get-tuple-element.45.refs_0_.s_ref, f32[512,4096]{1,0:T(8,128)S(1)} %get-tuple-element.74.acc_in, f32[8,32,128]{2,1,0:T(8,128)S(1)} %all_to_all.34.got_ref, f32[32,128]{1,0:T(8,128)S(1)} %get-tuple-element.76.half_in, ...), custom_call_target="tpu_custom_call" | custom-call | tf_op jit(solution)/shard_map/col_adj_0/pallas_call | solution.py:34
  102.7 0.9 collective-permute-start.16
  103.6 1.0 collective-permute-start.15
  104.6 1.1 collective-permute-done.17.refs_5_
  105.7 0.7 collective-permute-done.16.refs_4_
  106.4 6.9 %row_adj_0.1 = (f32[8,64,128]{2,1,0:T(8,128)S(1)}, f32[4,128]{1,0:T(4,128)}) custom-call(f32[512,4096]{1,0:T(8,128)S(1)} %get-tuple-element.45.refs_0_.s_ref, f32[512,4096]{1,0:T(8,128)S(1)} %get-tuple-element.78.refs_1_, f32[4,128]{1,0:T(4,128)S(1)} %get-tuple-element.79.refs_2_, f32[4,128]{1,0:T(4,128)S(1)} %collective-permute-done.15.refs_3_, ...), custom_call_target="tpu_custom_call" | custom-call | tf_op jit(solution)/shard_map/row_adj_0/pallas_call | solution.py:34
  113.3 11.5 %all_to_all.35 = f32[8,64,128]{2,1,0:T(8,128)S(1)} all-to-all(f32[8,64,128]{2,1,0:T(8,128)S(1)} %get-tuple-element.84), channel_id=1, replica_groups=mesh['wrk'=8,'firm'=4] {'wrk'}, dimensions={0} | all-to-all | bytes 524288 | tf_op jit(solution)/shard_map/all_to_all | solution.py:391
  124.8 0.6 fusion
  125.4 1.2 collective-permute-start.19
  126.6 0.6 collective-permute-start.18
  127.2 1.3 %collective-permute-done.20.refs_3_ = f32[32,128]{1,0:T(8,128)S(1)} collective-permute-done((f32[32,128]{1,0:T(8,128)S(1)}, f32[32,128]{1,0:T(8,128)S(1)}, u32[]{:S(2)}, u32[]{:S(2)}) %collective-permute-start.20) | collective-permute-done | bytes 16416 | tf_op jit(solution)/shard_map/ppermute | solution.py:386
  128.5 0.6 collective-permute-done.19.refs_2_
  129.1 0.7 unfold.1
  (15 shorter events, 0.4 us)
Async XLA Ops:
  5.8 3.8 %collective-permute-start.2 = (f32[4,128]{1,0:T(4,128)S(1)}, f32[4,128]{1,0:T(4,128)S(1)}, u32[]{:S(2)}, u32[]{:S(2)}) collective-permute-start(f32[4,128]{1,0:T(4,128)S(1)} %get-tuple-element.46.refs_1_), channel_id=1, source_target_pairs={{0,3},{1,2},{2,1},{3,0},{4,7},{5,6},{6,5},{7,4},{8,11},{9,10},{10,... | collective-permute-start | bytes 6152 | tf_op jit(solution)/shard_map/ppermute | solution.py:386
  8.2 3.6 %collective-permute-start.1 = (f32[4,128]{1,0:T(4,128)S(1)}, f32[4,128]{1,0:T(4,128)S(1)}, u32[]{:S(2)}, u32[]{:S(2)}) collective-permute-start(f32[4,128]{1,0:T(4,128)S(1)} %get-tuple-element.46.refs_1_), channel_id=1, source_target_pairs={{0,2},{1,3},{2,0},{3,1},{4,6},{5,7},{6,4},{7,5},{8,10},{9,11},{10,... | collective-permute-start | bytes 6152 | tf_op jit(solution)/shard_map/ppermute | solution.py:386
  8.9 2.9 %collective-permute-start = (f32[4,128]{1,0:T(4,128)S(1)}, f32[4,128]{1,0:T(4,128)S(1)}, u32[]{:S(2)}, u32[]{:S(2)}) collective-permute-start(f32[4,128]{1,0:T(4,128)S(1)} %get-tuple-element.46.refs_1_), channel_id=1, source_target_pairs={{0,1},{1,0},{2,3},{3,2},{4,5},{5,4},{6,7},{7,6},{8,9},{9,8},{10,11... | collective-permute-start | bytes 6152 | tf_op jit(solution)/shard_map/ppermute | solution.py:386
  29.2 3.1 %collective-permute-start.5 = (f32[4,128]{1,0:T(4,128)S(1)}, f32[4,128]{1,0:T(4,128)S(1)}, u32[]{:S(2)}, u32[]{:S(2)}) collective-permute-start(f32[4,128]{1,0:T(4,128)S(1)} %get-tuple-element.52.refs_1_), channel_id=1, source_target_pairs={{0,3},{1,2},{2,1},{3,0},{4,7},{5,6},{6,5},{7,4},{8,11},{9,10},{10,... | collective-permute-start | bytes 6152 | tf_op jit(solution)/shard_map/ppermute | solution.py:386
  29.3 3.7 %collective-permute-start.4 = (f32[4,128]{1,0:T(4,128)S(1)}, f32[4,128]{1,0:T(4,128)S(1)}, u32[]{:S(2)}, u32[]{:S(2)}) collective-permute-start(f32[4,128]{1,0:T(4,128)S(1)} %get-tuple-element.52.refs_1_), channel_id=1, source_target_pairs={{0,2},{1,3},{2,0},{3,1},{4,6},{5,7},{6,4},{7,5},{8,10},{9,11},{10,... | collective-permute-start | bytes 6152 | tf_op jit(solution)/shard_map/ppermute | solution.py:386
  30.0 3.0 %collective-permute-start.3 = (f32[4,128]{1,0:T(4,128)S(1)}, f32[4,128]{1,0:T(4,128)S(1)}, u32[]{:S(2)}, u32[]{:S(2)}) collective-permute-start(f32[4,128]{1,0:T(4,128)S(1)} %get-tuple-element.52.refs_1_), channel_id=1, source_target_pairs={{0,1},{1,0},{2,3},{3,2},{4,5},{5,4},{6,7},{7,6},{8,9},{9,8},{10,11... | collective-permute-start | bytes 6152 | tf_op jit(solution)/shard_map/ppermute | solution.py:386
  47.1 3.1 %collective-permute-start.8 = (f32[4,128]{1,0:T(4,128)S(1)}, f32[4,128]{1,0:T(4,128)S(1)}, u32[]{:S(2)}, u32[]{:S(2)}) collective-permute-start(f32[4,128]{1,0:T(4,128)S(1)} %get-tuple-element.56.refs_1_), channel_id=1, source_target_pairs={{0,3},{1,2},{2,1},{3,0},{4,7},{5,6},{6,5},{7,4},{8,11},{9,10},{10,... | collective-permute-start | bytes 6152 | tf_op jit(solution)/shard_map/ppermute | solution.py:386
  47.2 3.7 %collective-permute-start.7 = (f32[4,128]{1,0:T(4,128)S(1)}, f32[4,128]{1,0:T(4,128)S(1)}, u32[]{:S(2)}, u32[]{:S(2)}) collective-permute-start(f32[4,128]{1,0:T(4,128)S(1)} %get-tuple-element.56.refs_1_), channel_id=1, source_target_pairs={{0,2},{1,3},{2,0},{3,1},{4,6},{5,7},{6,4},{7,5},{8,10},{9,11},{10,... | collective-permute-start | bytes 6152 | tf_op jit(solution)/shard_map/ppermute | solution.py:386
  48.2 2.6 %collective-permute-start.6 = (f32[4,128]{1,0:T(4,128)S(1)}, f32[4,128]{1,0:T(4,128)S(1)}, u32[]{:S(2)}, u32[]{:S(2)}) collective-permute-start(f32[4,128]{1,0:T(4,128)S(1)} %get-tuple-element.56.refs_1_), channel_id=1, source_target_pairs={{0,1},{1,0},{2,3},{3,2},{4,5},{5,4},{6,7},{7,6},{8,9},{9,8},{10,11... | collective-permute-start | bytes 6152 | tf_op jit(solution)/shard_map/ppermute | solution.py:386
  65.2 3.1 %collective-permute-start.11 = (f32[4,128]{1,0:T(4,128)S(1)}, f32[4,128]{1,0:T(4,128)S(1)}, u32[]{:S(2)}, u32[]{:S(2)}) collective-permute-start(f32[4,128]{1,0:T(4,128)S(1)} %get-tuple-element.62.refs_2_), channel_id=1, source_target_pairs={{0,3},{1,2},{2,1},{3,0},{4,7},{5,6},{6,5},{7,4},{8,11},{9,10},{10,... | collective-permute-start | bytes 6152 | tf_op jit(solution)/shard_map/ppermute | solution.py:386
  65.3 3.7 %collective-permute-start.10 = (f32[4,128]{1,0:T(4,128)S(1)}, f32[4,128]{1,0:T(4,128)S(1)}, u32[]{:S(2)}, u32[]{:S(2)}) collective-permute-start(f32[4,128]{1,0:T(4,128)S(1)} %get-tuple-element.62.refs_2_), channel_id=1, source_target_pairs={{0,2},{1,3},{2,0},{3,1},{4,6},{5,7},{6,4},{7,5},{8,10},{9,11},{10,... | collective-permute-start | bytes 6152 | tf_op jit(solution)/shard_map/ppermute | solution.py:386
  66.2 2.8 %collective-permute-start.9 = (f32[4,128]{1,0:T(4,128)S(1)}, f32[4,128]{1,0:T(4,128)S(1)}, u32[]{:S(2)}, u32[]{:S(2)}) collective-permute-start(f32[4,128]{1,0:T(4,128)S(1)} %get-tuple-element.62.refs_2_), channel_id=1, source_target_pairs={{0,1},{1,0},{2,3},{3,2},{4,5},{5,4},{6,7},{7,6},{8,9},{9,8},{10,11... | collective-permute-start | bytes 6152 | tf_op jit(solution)/shard_map/ppermute | solution.py:386
  83.9 3.1 %collective-permute-start.14 = (f32[4,128]{1,0:T(4,128)S(1)}, f32[4,128]{1,0:T(4,128)S(1)}, u32[]{:S(2)}, u32[]{:S(2)}) collective-permute-start(f32[4,128]{1,0:T(4,128)S(1)} %get-tuple-element.71.refs_2_), channel_id=1, source_target_pairs={{0,3},{1,2},{2,1},{3,0},{4,7},{5,6},{6,5},{7,4},{8,11},{9,10},{10,... | collective-permute-start | bytes 6152 | tf_op jit(solution)/shard_map/ppermute | solution.py:386
  84.0 3.7 %collective-permute-start.13 = (f32[4,128]{1,0:T(4,128)S(1)}, f32[4,128]{1,0:T(4,128)S(1)}, u32[]{:S(2)}, u32[]{:S(2)}) collective-permute-start(f32[4,128]{1,0:T(4,128)S(1)} %get-tuple-element.71.refs_2_), channel_id=1, source_target_pairs={{0,2},{1,3},{2,0},{3,1},{4,6},{5,7},{6,4},{7,5},{8,10},{9,11},{10,... | collective-permute-start | bytes 6152 | tf_op jit(solution)/shard_map/ppermute | solution.py:386
  84.9 2.8 %collective-permute-start.12 = (f32[4,128]{1,0:T(4,128)S(1)}, f32[4,128]{1,0:T(4,128)S(1)}, u32[]{:S(2)}, u32[]{:S(2)}) collective-permute-start(f32[4,128]{1,0:T(4,128)S(1)} %get-tuple-element.71.refs_2_), channel_id=1, source_target_pairs={{0,1},{1,0},{2,3},{3,2},{4,5},{5,4},{6,7},{7,6},{8,9},{9,8},{10,11... | collective-permute-start | bytes 6152 | tf_op jit(solution)/shard_map/ppermute | solution.py:386
  102.7 3.1 %collective-permute-start.17 = (f32[4,128]{1,0:T(4,128)S(1)}, f32[4,128]{1,0:T(4,128)S(1)}, u32[]{:S(2)}, u32[]{:S(2)}) collective-permute-start(f32[4,128]{1,0:T(4,128)S(1)} %get-tuple-element.79.refs_2_), channel_id=1, source_target_pairs={{0,3},{1,2},{2,1},{3,0},{4,7},{5,6},{6,5},{7,4},{8,11},{9,10},{10,... | collective-permute-start | bytes 6152 | tf_op jit(solution)/shard_map/ppermute | solution.py:386
  102.7 3.7 %collective-permute-start.16 = (f32[4,128]{1,0:T(4,128)S(1)}, f32[4,128]{1,0:T(4,128)S(1)}, u32[]{:S(2)}, u32[]{:S(2)}) collective-permute-start(f32[4,128]{1,0:T(4,128)S(1)} %get-tuple-element.79.refs_2_), channel_id=1, source_target_pairs={{0,2},{1,3},{2,0},{3,1},{4,6},{5,7},{6,4},{7,5},{8,10},{9,11},{10,... | collective-permute-start | bytes 6152 | tf_op jit(solution)/shard_map/ppermute | solution.py:386
  103.6 2.8 %collective-permute-start.15 = (f32[4,128]{1,0:T(4,128)S(1)}, f32[4,128]{1,0:T(4,128)S(1)}, u32[]{:S(2)}, u32[]{:S(2)}) collective-permute-start(f32[4,128]{1,0:T(4,128)S(1)} %get-tuple-element.79.refs_2_), channel_id=1, source_target_pairs={{0,1},{1,0},{2,3},{3,2},{4,5},{5,4},{6,7},{7,6},{8,9},{9,8},{10,11... | collective-permute-start | bytes 6152 | tf_op jit(solution)/shard_map/ppermute | solution.py:386
  125.4 3.2 %collective-permute-start.20 = (f32[32,128]{1,0:T(8,128)S(1)}, f32[32,128]{1,0:T(8,128)S(1)}, u32[]{:S(2)}, u32[]{:S(2)}) collective-permute-start(f32[32,128]{1,0:T(8,128)S(1)} %get-tuple-element.88.refs_0_), channel_id=1, source_target_pairs={{0,3},{1,2},{2,1},{3,0},{4,7},{5,6},{6,5},{7,4},{8,11},{9,10},{10,... | collective-permute-start | bytes 49160 | tf_op jit(solution)/shard_map/ppermute | solution.py:386
  125.4 3.7 %collective-permute-start.19 = (f32[32,128]{1,0:T(8,128)S(1)}, f32[32,128]{1,0:T(8,128)S(1)}, u32[]{:S(2)}, u32[]{:S(2)}) collective-permute-start(f32[32,128]{1,0:T(8,128)S(1)} %get-tuple-element.88.refs_0_), channel_id=1, source_target_pairs={{0,2},{1,3},{2,0},{3,1},{4,6},{5,7},{6,4},{7,5},{8,10},{9,11},{10,... | collective-permute-start | bytes 49160 | tf_op jit(solution)/shard_map/ppermute | solution.py:386
  126.6 2.5 %collective-permute-start.18 = (f32[32,128]{1,0:T(8,128)S(1)}, f32[32,128]{1,0:T(8,128)S(1)}, u32[]{:S(2)}, u32[]{:S(2)}) collective-permute-start(f32[32,128]{1,0:T(8,128)S(1)} %get-tuple-element.88.refs_0_), channel_id=1, source_target_pairs={{0,1},{1,0},{2,3},{3,2},{4,5},{5,4},{6,7},{7,6},{8,9},{9,8},{10,11... | collective-permute-start | bytes 49160 | tf_op jit(solution)/shard_map/ppermute | solution.py:386

commit v5 on v4

--- a/solution.py
+++ b/solution.py
@@ -370,11 +370,13 @@
 
 
 def unfold_kernel(*refs):
-    grad = tree([ref[...] for ref in refs[:-1]], jnp.add)
+    col_half_ref, summed_ref, *part_refs, grad_ref, col_ref = refs
+    col_ref[...] = col_half_ref[...] - summed_ref[: col_ref.shape[0], :]
+    grad = tree([ref[...] for ref in part_refs], jnp.add)
     half, lanes = grad.shape
     rank = lanes // 2
-    refs[-1][:half, :] = grad[:, :rank]
-    refs[-1][half:, :] = pltpu.roll(grad, rank, 1)[:, :rank]
+    grad_ref[:half, :] = grad[:, :rank]
+    grad_ref[half:, :] = pltpu.roll(grad, rank, 1)[:, :rank]
 
 
 def peers_of(part, axis):
@@ -463,12 +465,11 @@
         (pltpu.VMEM((rows, cols), jnp.float32), wide, wide, col_vec, col_vec),
     )
     summed = jnp.sum(exchange_cols(block), axis=0)
-    col_bar = (col_half - summed[: col_dims[0]]).reshape(cols)
-    summed = summed[col_dims[0] :]
-    grad_surplus = call(
-        unfold_kernel, "unfold", shape_of(rank, rank), peers_of(summed, "firm")
+    grad_surplus, col_bar = call(
+        unfold_kernel, "unfold", (shape_of(rank, rank), col_out),
+        (col_half, summed, *peers_of(summed[col_dims[0] :], "firm")),
     )
-    return (grad_surplus, row_half.reshape(rows), col_bar)
+    return (grad_surplus, row_half.reshape(rows), col_bar.reshape(cols))
 
 
 def solution(mesh):

time: 130 us -> 130 us (level)
  no operation moved by 1% of the time
where the time goes in v5:
time: 130 us; the launch traced here: 129 us
  blocking collectives  64.2 us (49%)
  Pallas kernels  35.9 us (28%)
  starting transfers between devices  14.7 us (11%)
  waiting for transfers between devices  13.9 us (11%)
    all_to_all x6, blocking collectives, exchange_cols(): return lax.all_to_all(block, 'wrk', 0, 0, tiled=True)  64.2 us
    pallas_call x13, Pallas kernels, call(): pl.pallas_call(kernel, name=name, out_shape=outs, in_specs=[pl.BlockSpec(...  35.9 us
    ppermute x21, starting transfers between devices, peers_of(): lax.ppermute(part, axis, [(i, i ^ d) for i in range(size)])  14.7 us
    ppermute x21, waiting for transfers between devices, peers_of(): lax.ppermute(part, axis, [(i, i ^ d) for i in range(size)])  13.9 us
  transfers between devices with their start and end apart: 21, of which 14 were waited for; matrix products, arithmetic and copies ran while one was open for 0% of the time, Pallas kernels for 0%

profile of v5, /device:TPU:0, one launch (start us, length us, event | category | flops | bytes accessed | tf_op | source)
XLA Modules:
  0.0 129.3 jit_solution(7783218742514201903)
XLA Ops:
  0.6 5.1 %row_first.1 = (f32[512,4096]{1,0:T(8,128)S(1)}, f32[4,128]{1,0:T(4,128)S(1)}, f32[64,512]{1,0:T(8,128)S(1)}, f32[64,4096]{1,0:T(8,128)S(1)}, f32[64,64]{1,0:T(8...) custom-call(f32[64,512]{1,0:T(8,128)} %bitcast.9, ...), custom_call_target="tpu_custom_call" | custom-call | tf_op jit(solution)/shard_map/row_first/pallas_call | solution.py:34
  5.8 2.5 %collective-permute-start.2 = (f32[4,128]{1,0:T(4,128)S(1)}, f32[4,128]{1,0:T(4,128)S(1)}, u32[]{:S(2)}, u32[]{:S(2)}) collective-permute-start(f32[4,128]{1,0:T(4,128)S(1)} %get-tuple-element.48.refs_1_), channel_id=1, source_target_pairs={{0,3},{1,2},{2,1},{3,0},{4,7},{5,6},{6,5},{7,4},{8,11},{9,10},{10,... | collective-permute-start | bytes 6152 | tf_op jit(solution)/shard_map/ppermute | solution.py:388
  8.2 0.6 collective-permute-start.1
  8.9 0.6 collective-permute-done.2.refs_4_
  9.5 2.3 %collective-permute-done.1.refs_3_ = f32[4,128]{1,0:T(4,128)S(1)} collective-permute-done((f32[4,128]{1,0:T(4,128)S(1)}, f32[4,128]{1,0:T(4,128)S(1)}, u32[]{:S(2)}, u32[]{:S(2)}) %collective-permute-start.1) | collective-permute-done | bytes 2080 | tf_op jit(solution)/shard_map/ppermute | solution.py:388
  11.8 2.2 %col_0.1 = (f32[8,32,128]{2,1,0:T(8,128)S(1)}, f32[4,128]{1,0:T(4,128)S(1)}, f32[4,128]{1,0:T(4,128)S(1)}) custom-call(f32[512,4096]{1,0:T(8,128)S(1)} %get-tuple-element.47.refs_0_.s_ref, f32[4,128]{1,0:T(4,128)S(1)} %get-tuple-element.48.refs_1_, f32[4,128]{1,0:T(4,128)S(1)} %collective-permute-done.refs_2_, f32[4,128]{1,0:T(4,128)S(1)} %collective-permute-done.1.refs_3_, ...), custom_call_target="tpu_custom_call" | custom-call | tf_op jit(solution)/shard_map/col_0/pallas_call | solution.py:34
  14.1 13.0 %all_to_all.30.got_ref = f32[8,32,128]{2,1,0:T(8,128)S(1)} all-to-all(f32[8,32,128]{2,1,0:T(8,128)S(1)} %get-tuple-element.51), channel_id=1, replica_groups=mesh['wrk'=8,'firm'=4] {'wrk'}, dimensions={0} | all-to-all | bytes 262144 | tf_op jit(solution)/shard_map/all_to_all | solution.py:393
  27.0 2.2 %row_1.1 = (f32[4,128]{1,0:T(4,128)S(1)}, f32[32,128]{1,0:T(8,128)S(1)}, f32[32,128]{1,0:T(8,128)S(1)}) custom-call(f32[512,4096]{1,0:T(8,128)S(1)} %get-tuple-element.47.refs_0_.s_ref, f32[8,32,128]{2,1,0:T(8,128)S(1)} %all_to_all.30.got_ref, f32[32,128]{1,0:T(8,128)S(1)} %get-tuple-element.52.old_ref.refs_7_, f32[32,128]{1,0:T(8,128)S(1)} %get-tuple-element.53.mass_ref), custom_call_target="tpu_custom_call" | custom-call | tf_op jit(solution)/shard_map/row_1/pallas_call | solution.py:34
  29.2 0.1 collective-permute-start.5
  29.3 0.7 collective-permute-start.4
  30.0 1.1 collective-permute-start.3
  31.1 1.1 collective-permute-done.5.refs_4_
  32.3 0.7 collective-permute-done.4.refs_3_
  32.9 2.2 %col_1.1 = (f32[8,32,128]{2,1,0:T(8,128)S(1)}, f32[4,128]{1,0:T(4,128)S(1)}, f32[4,128]{1,0:T(4,128)S(1)}) custom-call(f32[512,4096]{1,0:T(8,128)S(1)} %get-tuple-element.47.refs_0_.s_ref, f32[4,128]{1,0:T(4,128)S(1)} %get-tuple-element.54.refs_1_, f32[4,128]{1,0:T(4,128)S(1)} %collective-permute-done.3.refs_2_, ...), custom_call_target="tpu_custom_call" | custom-call | tf_op jit(solution)/shard_map/col_1/pallas_call | solution.py:34
  35.2 9.7 %all_to_all.31.got_ref = f32[8,32,128]{2,1,0:T(8,128)S(1)} all-to-all(f32[8,32,128]{2,1,0:T(8,128)S(1)} %get-tuple-element.56), channel_id=1, replica_groups=mesh['wrk'=8,'firm'=4] {'wrk'}, dimensions={0} | all-to-all | bytes 262144 | tf_op jit(solution)/shard_map/all_to_all | solution.py:393
  44.9 2.2 %row_2.1 = (f32[4,128]{1,0:T(4,128)S(1)}, f32[32,128]{1,0:T(8,128)S(1)}, f32[32,128]{1,0:T(8,128)S(1)}) custom-call(f32[512,4096]{1,0:T(8,128)S(1)} %get-tuple-element.47.refs_0_.s_ref, f32[8,32,128]{2,1,0:T(8,128)S(1)} %all_to_all.31.got_ref, f32[32,128]{1,0:T(8,128)S(1)} %get-tuple-element.57.old_ref.refs_7_, f32[32,128]{1,0:T(8,128)S(1)} %get-tuple-element.53.mass_ref), custom_call_target="tpu_custom_call" | custom-call | tf_op jit(solution)/shard_map/row_2/pallas_call | solution.py:34
  47.2 1.1 collective-permute-start.7
  48.2 0.8 collective-permute-start.6
  49.0 1.1 collective-permute-done.8.refs_4_
  50.2 0.7 collective-permute-done.7.refs_3_
  50.8 2.2 %col_2.1 = (f32[8,32,128]{2,1,0:T(8,128)S(1)}, f32[4,128]{1,0:T(4,128)S(1)}, f32[4,128]{1,0:T(4,128)S(1)}) custom-call(f32[512,4096]{1,0:T(8,128)S(1)} %get-tuple-element.47.refs_0_.s_ref, f32[4,128]{1,0:T(4,128)S(1)} %get-tuple-element.58.refs_1_, f32[4,128]{1,0:T(4,128)S(1)} %collective-permute-done.6.refs_2_, ...), custom_call_target="tpu_custom_call" | custom-call | tf_op jit(solution)/shard_map/col_2/pallas_call | solution.py:34
  53.1 10.1 %all_to_all.32.got_ref = f32[8,32,128]{2,1,0:T(8,128)S(1)} all-to-all(f32[8,32,128]{2,1,0:T(8,128)S(1)} %get-tuple-element.60), channel_id=1, replica_groups=mesh['wrk'=8,'firm'=4] {'wrk'}, dimensions={0} | all-to-all | bytes 262144 | tf_op jit(solution)/shard_map/all_to_all | solution.py:393
  63.2 2.1 %col_adj_2.1 = (f32[512,4096]{1,0:T(8,128)S(1)}, f32[4,128]{1,0:T(4,128)S(1)}, f32[32,128]{1,0:T(8,128)S(1)}) custom-call(f32[512,4096]{1,0:T(8,128)S(1)} %get-tuple-element.47.refs_0_.s_ref, f32[8,32,128]{2,1,0:T(8,128)S(1)} %all_to_all.32.got_ref, f32[32,128]{1,0:T(8,128)S(1)} %get-tuple-element.61.cot_ref, f32[4,128]{1,0:T(4,128)S(1)} %get-tuple-element.62.pot_ref), custom_call_target="tpu_custom_call" | custom-call | tf_op jit(solution)/shard_map/col_adj_2/pallas_call | solution.py:34
  65.3 0.9 collective-permute-start.10
  66.2 1.0 collective-permute-start.9
  67.2 1.1 collective-permute-done.11.refs_5_
  68.3 0.7 collective-permute-done.10.refs_4_
  69.0 2.7 %row_adj_2.1 = (f32[512,4096]{1,0:T(8,128)S(1)}, f32[8,32,128]{2,1,0:T(8,128)S(1)}, f32[4,128]{1,0:T(4,128)S(1)}) custom-call(f32[512,4096]{1,0:T(8,128)S(1)} %get-tuple-element.47.refs_0_.s_ref, f32[512,4096]{1,0:T(8,128)S(1)} %get-tuple-element.63.refs_1_, f32[4,128]{1,0:T(4,128)S(1)} %get-tuple-element.64.refs_2_, ...), custom_call_target="tpu_custom_call" | custom-call | tf_op jit(solution)/shard_map/row_adj_2/pallas_call | solution.py:34
  71.7 9.9 %all_to_all.33.got_ref = f32[8,32,128]{2,1,0:T(8,128)S(1)} all-to-all(f32[8,32,128]{2,1,0:T(8,128)S(1)} %get-tuple-element.69), channel_id=1, replica_groups=mesh['wrk'=8,'firm'=4] {'wrk'}, dimensions={0} | all-to-all | bytes 262144 | tf_op jit(solution)/shard_map/all_to_all | solution.py:393
  81.6 2.3 %col_adj_1.1 = (f32[512,4096]{1,0:T(8,128)S(1)}, f32[4,128]{1,0:T(4,128)S(1)}, f32[32,128]{1,0:T(8,128)S(1)}) custom-call(f32[512,4096]{1,0:T(8,128)S(1)} %get-tuple-element.47.refs_0_.s_ref, f32[512,4096]{1,0:T(8,128)S(1)} %get-tuple-element.68.acc_in, f32[8,32,128]{2,1,0:T(8,128)S(1)} %all_to_all.33.got_ref, f32[32,128]{1,0:T(8,128)S(1)} %get-tuple-element.70.half_in, ...), custom_call_target="tpu_custom_call" | custom-call | tf_op jit(solution)/shard_map/col_adj_1/pallas_call | solution.py:34
  84.0 0.9 collective-permute-start.13
  84.9 1.0 collective-permute-start.12
  85.9 1.1 collective-permute-done.14.refs_5_
  87.0 0.7 collective-permute-done.13.refs_4_
  87.7 2.7 %row_adj_1.1 = (f32[512,4096]{1,0:T(8,128)S(1)}, f32[8,32,128]{2,1,0:T(8,128)S(1)}, f32[4,128]{1,0:T(4,128)S(1)}) custom-call(f32[512,4096]{1,0:T(8,128)S(1)} %get-tuple-element.47.refs_0_.s_ref, f32[512,4096]{1,0:T(8,128)S(1)} %get-tuple-element.72.refs_1_, f32[4,128]{1,0:T(4,128)S(1)} %get-tuple-element.73.refs_2_, ...), custom_call_target="tpu_custom_call" | custom-call | tf_op jit(solution)/shard_map/row_adj_1/pallas_call | solution.py:34
  90.4 9.9 %all_to_all.34.got_ref = f32[8,32,128]{2,1,0:T(8,128)S(1)} all-to-all(f32[8,32,128]{2,1,0:T(8,128)S(1)} %get-tuple-element.77), channel_id=1, replica_groups=mesh['wrk'=8,'firm'=4] {'wrk'}, dimensions={0} | all-to-all | bytes 262144 | tf_op jit(solution)/shard_map/all_to_all | solution.py:393
  100.3 2.3 %col_adj_0.1 = (f32[512,4096]{1,0:T(8,128)S(1)}, f32[4,128]{1,0:T(4,128)S(1)}, f32[32,128]{1,0:T(8,128)S(1)}) custom-call(f32[512,4096]{1,0:T(8,128)S(1)} %get-tuple-element.47.refs_0_.s_ref, f32[512,4096]{1,0:T(8,128)S(1)} %get-tuple-element.76.acc_in, f32[8,32,128]{2,1,0:T(8,128)S(1)} %all_to_all.34.got_ref, f32[32,128]{1,0:T(8,128)S(1)} %get-tuple-element.78.half_in, ...), custom_call_target="tpu_custom_call" | custom-call | tf_op jit(solution)/shard_map/col_adj_0/pallas_call | solution.py:34
  102.7 0.9 collective-permute-start.16
  103.6 1.0 collective-permute-start.15
  104.6 1.1 collective-permute-done.17.refs_5_
  105.7 0.7 collective-permute-done.16.refs_4_
  106.4 6.9 %row_adj_0.1 = (f32[8,64,128]{2,1,0:T(8,128)S(1)}, f32[4,128]{1,0:T(4,128)}) custom-call(f32[512,4096]{1,0:T(8,128)S(1)} %get-tuple-element.47.refs_0_.s_ref, f32[512,4096]{1,0:T(8,128)S(1)} %get-tuple-element.81.refs_1_, f32[4,128]{1,0:T(4,128)S(1)} %get-tuple-element.82.refs_2_, f32[4,128]{1,0:T(4,128)S(1)} %collective-permute-done.15.refs_3_, ...), custom_call_target="tpu_custom_call" | custom-call | tf_op jit(solution)/shard_map/row_adj_0/pallas_call | solution.py:34
  113.3 11.5 %all_to_all.35 = f32[8,64,128]{2,1,0:T(8,128)S(1)} all-to-all(f32[8,64,128]{2,1,0:T(8,128)S(1)} %get-tuple-element.87), channel_id=1, replica_groups=mesh['wrk'=8,'firm'=4] {'wrk'}, dimensions={0} | all-to-all | bytes 524288 | tf_op jit(solution)/shard_map/all_to_all | solution.py:393
  124.8 1.3 collective-permute-start.19
  126.1 0.6 collective-permute-start.18
  126.7 1.3 %collective-permute-done.20.refs_5_ = f32[32,128]{1,0:T(8,128)S(1)} collective-permute-done((f32[32,128]{1,0:T(8,128)S(1)}, f32[32,128]{1,0:T(8,128)S(1)}, u32[]{:S(2)}, u32[]{:S(2)}) %collective-permute-start.20) | collective-permute-done | bytes 16416 | tf_op jit(solution)/shard_map/ppermute | solution.py:388
  128.0 0.7 collective-permute-done.19.refs_4_
  128.7 0.7 unfold.1
  (15 shorter events, 0.4 us)
Async XLA Ops:
  5.8 3.8 %collective-permute-start.2 = (f32[4,128]{1,0:T(4,128)S(1)}, f32[4,128]{1,0:T(4,128)S(1)}, u32[]{:S(2)}, u32[]{:S(2)}) collective-permute-start(f32[4,128]{1,0:T(4,128)S(1)} %get-tuple-element.48.refs_1_), channel_id=1, source_target_pairs={{0,3},{1,2},{2,1},{3,0},{4,7},{5,6},{6,5},{7,4},{8,11},{9,10},{10,... | collective-permute-start | bytes 6152 | tf_op jit(solution)/shard_map/ppermute | solution.py:388
  8.2 3.6 %collective-permute-start.1 = (f32[4,128]{1,0:T(4,128)S(1)}, f32[4,128]{1,0:T(4,128)S(1)}, u32[]{:S(2)}, u32[]{:S(2)}) collective-permute-start(f32[4,128]{1,0:T(4,128)S(1)} %get-tuple-element.48.refs_1_), channel_id=1, source_target_pairs={{0,2},{1,3},{2,0},{3,1},{4,6},{5,7},{6,4},{7,5},{8,10},{9,11},{10,... | collective-permute-start | bytes 6152 | tf_op jit(solution)/shard_map/ppermute | solution.py:388
  8.9 2.9 %collective-permute-start = (f32[4,128]{1,0:T(4,128)S(1)}, f32[4,128]{1,0:T(4,128)S(1)}, u32[]{:S(2)}, u32[]{:S(2)}) collective-permute-start(f32[4,128]{1,0:T(4,128)S(1)} %get-tuple-element.48.refs_1_), channel_id=1, source_target_pairs={{0,1},{1,0},{2,3},{3,2},{4,5},{5,4},{6,7},{7,6},{8,9},{9,8},{10,11... | collective-permute-start | bytes 6152 | tf_op jit(solution)/shard_map/ppermute | solution.py:388
  29.2 3.1 %collective-permute-start.5 = (f32[4,128]{1,0:T(4,128)S(1)}, f32[4,128]{1,0:T(4,128)S(1)}, u32[]{:S(2)}, u32[]{:S(2)}) collective-permute-start(f32[4,128]{1,0:T(4,128)S(1)} %get-tuple-element.54.refs_1_), channel_id=1, source_target_pairs={{0,3},{1,2},{2,1},{3,0},{4,7},{5,6},{6,5},{7,4},{8,11},{9,10},{10,... | collective-permute-start | bytes 6152 | tf_op jit(solution)/shard_map/ppermute | solution.py:388
  29.3 3.7 %collective-permute-start.4 = (f32[4,128]{1,0:T(4,128)S(1)}, f32[4,128]{1,0:T(4,128)S(1)}, u32[]{:S(2)}, u32[]{:S(2)}) collective-permute-start(f32[4,128]{1,0:T(4,128)S(1)} %get-tuple-element.54.refs_1_), channel_id=1, source_target_pairs={{0,2},{1,3},{2,0},{3,1},{4,6},{5,7},{6,4},{7,5},{8,10},{9,11},{10,... | collective-permute-start | bytes 6152 | tf_op jit(solution)/shard_map/ppermute | solution.py:388
  30.0 3.0 %collective-permute-start.3 = (f32[4,128]{1,0:T(4,128)S(1)}, f32[4,128]{1,0:T(4,128)S(1)}, u32[]{:S(2)}, u32[]{:S(2)}) collective-permute-start(f32[4,128]{1,0:T(4,128)S(1)} %get-tuple-element.54.refs_1_), channel_id=1, source_target_pairs={{0,1},{1,0},{2,3},{3,2},{4,5},{5,4},{6,7},{7,6},{8,9},{9,8},{10,11... | collective-permute-start | bytes 6152 | tf_op jit(solution)/shard_map/ppermute | solution.py:388
  47.1 3.1 %collective-permute-start.8 = (f32[4,128]{1,0:T(4,128)S(1)}, f32[4,128]{1,0:T(4,128)S(1)}, u32[]{:S(2)}, u32[]{:S(2)}) collective-permute-start(f32[4,128]{1,0:T(4,128)S(1)} %get-tuple-element.58.refs_1_), channel_id=1, source_target_pairs={{0,3},{1,2},{2,1},{3,0},{4,7},{5,6},{6,5},{7,4},{8,11},{9,10},{10,... | collective-permute-start | bytes 6152 | tf_op jit(solution)/shard_map/ppermute | solution.py:388
  47.2 3.7 %collective-permute-start.7 = (f32[4,128]{1,0:T(4,128)S(1)}, f32[4,128]{1,0:T(4,128)S(1)}, u32[]{:S(2)}, u32[]{:S(2)}) collective-permute-start(f32[4,128]{1,0:T(4,128)S(1)} %get-tuple-element.58.refs_1_), channel_id=1, source_target_pairs={{0,2},{1,3},{2,0},{3,1},{4,6},{5,7},{6,4},{7,5},{8,10},{9,11},{10,... | collective-permute-start | bytes 6152 | tf_op jit(solution)/shard_map/ppermute | solution.py:388
  48.2 2.6 %collective-permute-start.6 = (f32[4,128]{1,0:T(4,128)S(1)}, f32[4,128]{1,0:T(4,128)S(1)}, u32[]{:S(2)}, u32[]{:S(2)}) collective-permute-start(f32[4,128]{1,0:T(4,128)S(1)} %get-tuple-element.58.refs_1_), channel_id=1, source_target_pairs={{0,1},{1,0},{2,3},{3,2},{4,5},{5,4},{6,7},{7,6},{8,9},{9,8},{10,11... | collective-permute-start | bytes 6152 | tf_op jit(solution)/shard_map/ppermute | solution.py:388
  65.2 3.1 %collective-permute-start.11 = (f32[4,128]{1,0:T(4,128)S(1)}, f32[4,128]{1,0:T(4,128)S(1)}, u32[]{:S(2)}, u32[]{:S(2)}) collective-permute-start(f32[4,128]{1,0:T(4,128)S(1)} %get-tuple-element.64.refs_2_), channel_id=1, source_target_pairs={{0,3},{1,2},{2,1},{3,0},{4,7},{5,6},{6,5},{7,4},{8,11},{9,10},{10,... | collective-permute-start | bytes 6152 | tf_op jit(solution)/shard_map/ppermute | solution.py:388
  65.3 3.7 %collective-permute-start.10 = (f32[4,128]{1,0:T(4,128)S(1)}, f32[4,128]{1,0:T(4,128)S(1)}, u32[]{:S(2)}, u32[]{:S(2)}) collective-permute-start(f32[4,128]{1,0:T(4,128)S(1)} %get-tuple-element.64.refs_2_), channel_id=1, source_target_pairs={{0,2},{1,3},{2,0},{3,1},{4,6},{5,7},{6,4},{7,5},{8,10},{9,11},{10,... | collective-permute-start | bytes 6152 | tf_op jit(solution)/shard_map/ppermute | solution.py:388
  66.2 2.8 %collective-permute-start.9 = (f32[4,128]{1,0:T(4,128)S(1)}, f32[4,128]{1,0:T(4,128)S(1)}, u32[]{:S(2)}, u32[]{:S(2)}) collective-permute-start(f32[4,128]{1,0:T(4,128)S(1)} %get-tuple-element.64.refs_2_), channel_id=1, source_target_pairs={{0,1},{1,0},{2,3},{3,2},{4,5},{5,4},{6,7},{7,6},{8,9},{9,8},{10,11... | collective-permute-start | bytes 6152 | tf_op jit(solution)/shard_map/ppermute | solution.py:388
  83.9 3.1 %collective-permute-start.14 = (f32[4,128]{1,0:T(4,128)S(1)}, f32[4,128]{1,0:T(4,128)S(1)}, u32[]{:S(2)}, u32[]{:S(2)}) collective-permute-start(f32[4,128]{1,0:T(4,128)S(1)} %get-tuple-element.73.refs_2_), channel_id=1, source_target_pairs={{0,3},{1,2},{2,1},{3,0},{4,7},{5,6},{6,5},{7,4},{8,11},{9,10},{10,... | collective-permute-start | bytes 6152 | tf_op jit(solution)/shard_map/ppermute | solution.py:388
  84.0 3.7 %collective-permute-start.13 = (f32[4,128]{1,0:T(4,128)S(1)}, f32[4,128]{1,0:T(4,128)S(1)}, u32[]{:S(2)}, u32[]{:S(2)}) collective-permute-start(f32[4,128]{1,0:T(4,128)S(1)} %get-tuple-element.73.refs_2_), channel_id=1, source_target_pairs={{0,2},{1,3},{2,0},{3,1},{4,6},{5,7},{6,4},{7,5},{8,10},{9,11},{10,... | collective-permute-start | bytes 6152 | tf_op jit(solution)/shard_map/ppermute | solution.py:388
  84.9 2.8 %collective-permute-start.12 = (f32[4,128]{1,0:T(4,128)S(1)}, f32[4,128]{1,0:T(4,128)S(1)}, u32[]{:S(2)}, u32[]{:S(2)}) collective-permute-start(f32[4,128]{1,0:T(4,128)S(1)} %get-tuple-element.73.refs_2_), channel_id=1, source_target_pairs={{0,1},{1,0},{2,3},{3,2},{4,5},{5,4},{6,7},{7,6},{8,9},{9,8},{10,11... | collective-permute-start | bytes 6152 | tf_op jit(solution)/shard_map/ppermute | solution.py:388
  102.7 3.1 %collective-permute-start.17 = (f32[4,128]{1,0:T(4,128)S(1)}, f32[4,128]{1,0:T(4,128)S(1)}, u32[]{:S(2)}, u32[]{:S(2)}) collective-permute-start(f32[4,128]{1,0:T(4,128)S(1)} %get-tuple-element.82.refs_2_), channel_id=1, source_target_pairs={{0,3},{1,2},{2,1},{3,0},{4,7},{5,6},{6,5},{7,4},{8,11},{9,10},{10,... | collective-permute-start | bytes 6152 | tf_op jit(solution)/shard_map/ppermute | solution.py:388
  102.7 3.7 %collective-permute-start.16 = (f32[4,128]{1,0:T(4,128)S(1)}, f32[4,128]{1,0:T(4,128)S(1)}, u32[]{:S(2)}, u32[]{:S(2)}) collective-permute-start(f32[4,128]{1,0:T(4,128)S(1)} %get-tuple-element.82.refs_2_), channel_id=1, source_target_pairs={{0,2},{1,3},{2,0},{3,1},{4,6},{5,7},{6,4},{7,5},{8,10},{9,11},{10,... | collective-permute-start | bytes 6152 | tf_op jit(solution)/shard_map/ppermute | solution.py:388
  103.6 2.8 %collective-permute-start.15 = (f32[4,128]{1,0:T(4,128)S(1)}, f32[4,128]{1,0:T(4,128)S(1)}, u32[]{:S(2)}, u32[]{:S(2)}) collective-permute-start(f32[4,128]{1,0:T(4,128)S(1)} %get-tuple-element.82.refs_2_), channel_id=1, source_target_pairs={{0,1},{1,0},{2,3},{3,2},{4,5},{5,4},{6,7},{7,6},{8,9},{9,8},{10,11... | collective-permute-start | bytes 6152 | tf_op jit(solution)/shard_map/ppermute | solution.py:388
  124.8 3.2 %collective-permute-start.20 = (f32[32,128]{1,0:T(8,128)S(1)}, f32[32,128]{1,0:T(8,128)S(1)}, u32[]{:S(2)}, u32[]{:S(2)}) collective-permute-start(f32[32,128]{1,0:T(8,128)S(1)} %slice.4.refs_2_), channel_id=1, source_target_pairs={{0,3},{1,2},{2,1},{3,0},{4,7},{5,6},{6,5},{7,4},{8,11},{9,10},{10,... | collective-permute-start | bytes 49160 | tf_op jit(solution)/shard_map/ppermute | solution.py:388
  124.8 3.8 %collective-permute-start.19 = (f32[32,128]{1,0:T(8,128)S(1)}, f32[32,128]{1,0:T(8,128)S(1)}, u32[]{:S(2)}, u32[]{:S(2)}) collective-permute-start(f32[32,128]{1,0:T(8,128)S(1)} %slice.4.refs_2_), channel_id=1, source_target_pairs={{0,2},{1,3},{2,0},{3,1},{4,6},{5,7},{6,4},{7,5},{8,10},{9,11},{10,... | collective-permute-start | bytes 49160 | tf_op jit(solution)/shard_map/ppermute | solution.py:388
  126.1 2.5 %collective-permute-start.18 = (f32[32,128]{1,0:T(8,128)S(1)}, f32[32,128]{1,0:T(8,128)S(1)}, u32[]{:S(2)}, u32[]{:S(2)}) collective-permute-start(f32[32,128]{1,0:T(8,128)S(1)} %slice.4.refs_2_), channel_id=1, source_target_pairs={{0,1},{1,0},{2,3},{3,2},{4,5},{5,4},{6,7},{7,6},{8,9},{9,8},{10,11... | collective-permute-start | bytes 49160 | tf_op jit(solution)/shard_map/ppermute | solution.py:388
